TPU v7x, 32 devices: a whole 2x2x4 slice. The times are simulated.
32 devices in a mesh: dp: 8 (over z, core), context: 4 (over y, x).
Axes of the slice: x: 2, y: 2, z: 4, core: 2. Of those that a mesh axis runs over, the one named last changes fastest.
Arguments:
- layer_input: bfloat16 [8, 512, 8192], P('dp', 'context'), may hold values from -150 to 150
- value_weight: bfloat16 [8192, 512], replicated, may hold values from -0.0625 to 0.0625
- queries: bfloat16 [8, 512, 4096], P('dp', 'context'), may hold values from -150 to 150
- key_states: bfloat16 [8, 512, 512], P('dp', 'context'), may hold values from -6 to 6
- out_grads: bfloat16 [8, 512, 4096], P('dp', 'context'), may hold values from -16 to 16
- lengths: int32 [8], P('dp'), may hold values from 0 to 512, as said below
Outputs:
- clipped_sum: float32 [8192, 512], P('context', 'dp')
- doc_norms: float32 [8], P('dp')
- key_grads: bfloat16 [8, 512, 512], P('dp', 'context')
Inputs may be any that keep to these rules, and one draw needn't show every extreme that they name: `lengths`: a slot's document fills the slot's first positions; in every draw some slot is empty and some slot is full.
All inputs are finite; a program needn't handle non-finite values.
Results may differ from a plain program's by a relative error of at most 0.02.
Values may be sent and summed in bfloat16 or wider, within the bound.
No kernel may reach another device: no remote copies, remote signals or barrier semaphores. Data moves between devices by JAX's collectives and lax.ppermute only.
A program may use at most 128 MiB of HBM per device.

v0:
```python
import math

import jax
import jax.numpy as jnp
from jax import lax
from jax.experimental import pallas as pl
from jax.experimental.pallas import tpu as pltpu
from jax.sharding import PartitionSpec as P

HD = 128
LANES = 128
FIRST_SHARE = 10
HEAVY = 10
F32 = jnp.float32
BF16 = jnp.bfloat16
LOG2E = 1.4426950408889634


NT = (((1,), (1,)), ((), ()))
VMEM = pl.BlockSpec(memory_space=pltpu.VMEM)
SMEM = pl.BlockSpec(memory_space=pltpu.SMEM)


def estimate(flops, nbytes, exps=0):
    return pl.CostEstimate(flops=flops, bytes_accessed=nbytes, transcendentals=exps)


def grant(mib):
    return pltpu.CompilerParams(vmem_limit_bytes=mib << 20)


def split(own):
    units = own // LANES
    first = max(1, units * FIRST_SHARE // 16)
    return [first * LANES, (units - first) * LANES]


def cut(place, layer_rows, parts, sizes):
    rows, width = layer_rows.shape
    own = width // parts
    chunks = len(sizes)

    def kernel(place_ref, x_ref, *outs):
        for k in range(parts):
            start = (place_ref[0] ^ k) * own
            for j in range(chunks):
                span = pl.ds(pl.multiple_of(start + sum(sizes[:j]), LANES), sizes[j])
                outs[k * chunks + j][...] = x_ref[:, span]

    out = pl.pallas_call(
        kernel,
        out_shape=[jax.ShapeDtypeStruct((rows, size), BF16) for _ in range(parts) for size in sizes],
        in_specs=[SMEM, VMEM],
        out_specs=[VMEM] * (parts * chunks),
        compiler_params=grant(8),
        cost_estimate=estimate(0, HEAVY * 4 * rows * width),
        name="cut",
    )(place, layer_rows)
    return [[out[k * chunks + j] for j in range(chunks)] for k in range(parts)]


def project(layer_rows, value_weight):
    rows, width = layer_rows.shape
    cols = value_weight.shape[1]
    depth = 2048

    def kernel(x_ref, w_ref, v_ref):
        total = jnp.zeros((rows, cols), F32)
        for start in range(0, width, depth):
            span = slice(start, start + depth)
            total = total + jnp.dot(x_ref[:, span], w_ref[span, :], preferred_element_type=F32)
        v_ref[...] = total.astype(BF16)

    return pl.pallas_call(
        kernel,
        out_shape=jax.ShapeDtypeStruct((rows, cols), BF16),
        in_specs=[VMEM, VMEM],
        out_specs=VMEM,
        compiler_params=grant(14),
        cost_estimate=estimate(2 * rows * width * cols, 2 * width * (cols + rows)),
        name="project",
    )(layer_rows, value_weight)


def masked(block, valid):
    return jnp.where(valid, block, jnp.zeros_like(block))


def lanes(start, size):
    return pl.ds(pl.multiple_of(start, size), size)


def stack_heads(group, heads, source, target, keep):
    rows = source.shape[0]
    for h in range(heads):
        block = source[:, lanes((group * heads + h) * HD, HD)]
        target[h * rows : (h + 1) * rows, :] = keep(block)


def weigh(place, queries, out_grads, keys):
    rows, width = queries.shape
    parts = len(keys)
    kv_width = keys[0].shape[1]
    groups = kv_width // HD
    heads = width // HD // groups
    total = rows * parts
    factor = HD ** (-0.5) * LOG2E
    pair = 2

    def kernel(place_ref, q_ref, o_ref, *rest):
        k_refs, p_ref = rest[:parts], rest[parts]
        v_refs, (q_buf, o_buf) = rest[parts + 1 : 2 * parts + 1], rest[2 * parts + 1 :]
        me, length = place_ref[0], place_ref[1]
        valid = me * rows + lax.broadcasted_iota(jnp.int32, (rows, HD), 0) < length
        row = lax.broadcasted_iota(jnp.int32, (rows, pair * rows), 0)
        lane = lax.broadcasted_iota(jnp.int32, (rows, pair * rows), 1)
        causal = row <= lax.rem(lane, rows)

        @pl.loop(0, groups)
        def _(group):
            cols = lanes(group * HD, HD)
            stack_heads(group, heads, q_ref, q_buf, lambda block: block)
            stack_heads(group, heads, o_ref, o_buf, lambda block: masked(block, valid))
            for h in range(0, heads, pair):
                span = slice(h * rows, (h + pair) * rows)
                q = q_buf[span, :]
                scores = [lax.dot_general(r[:, cols], q, NT, preferred_element_type=F32) for r in k_refs]
                scores[0] = jnp.where(causal, scores[0], -jnp.inf)
                peak = jnp.max(scores[0], axis=0, keepdims=True)
                for k in range(1, parts):
                    higher = jnp.maximum(peak, jnp.max(scores[k], axis=0, keepdims=True))
                    peak = jnp.where((me ^ k) < me, higher, peak)
                peak = peak * factor
                sums = 0.0
                for k in range(parts):
                    shift = peak if k == 0 else jnp.where((me ^ k) < me, peak, jnp.inf)
                    scores[k] = jnp.exp2(scores[k] * factor - shift)
                    sums = sums + jnp.sum(scores[k], axis=0, keepdims=True)
                inverse = 1.0 / sums
                for k in range(parts):
                    p_ref[group, k * rows : (k + 1) * rows, span] = (scores[k] * inverse).astype(BF16)
            for k in range(parts):
                block = p_ref[group, k * rows : (k + 1) * rows, :]
                part = jnp.dot(block, o_buf[...], preferred_element_type=F32)
                v_refs[k][:, cols] = part.astype(v_refs[k].dtype)

    kinds = [F32] + [BF16] * (parts - 1)
    out = pl.pallas_call(
        kernel,
        out_shape=[jax.ShapeDtypeStruct((groups, total, heads * rows), BF16)]
        + [jax.ShapeDtypeStruct((rows, kv_width), kind) for kind in kinds],
        in_specs=[SMEM] + [VMEM] * (2 + parts),
        out_specs=[VMEM] * (1 + parts),
        scratch_shapes=[pltpu.VMEM((heads * rows, HD), BF16)] * 2,
        compiler_params=grant(8 + 2 * parts),
        cost_estimate=estimate(
            HEAVY * 4 * rows * total * width,
            2 * (2 * rows * width + 2 * total * kv_width),
            rows * total * width // HD,
        ),
        name="weigh",
    )(place, queries, out_grads, *keys)
    return out[0], out[1:]


def key_side(place, weights, queries, out_grads, values):
    rows, width = queries.shape
    parts = len(values)
    kv_width = values[0].shape[1]
    groups = kv_width // HD
    heads = width // HD // groups
    total = rows * parts
    scale = HD ** (-0.5)
    pair = 2

    def kernel(place_ref, p_ref, q_ref, o_ref, *rest):
        v_refs, k_refs = rest[:parts], rest[parts : 2 * parts]
        q_buf, o_buf, s_buf = rest[2 * parts :]
        me, length = place_ref[0], place_ref[1]
        valid = me * rows + lax.broadcasted_iota(jnp.int32, (rows, HD), 0) < length

        @pl.loop(0, groups)
        def _(group):
            cols = lanes(group * HD, HD)
            stack_heads(group, heads, q_ref, q_buf, lambda block: block)
            stack_heads(group, heads, o_ref, o_buf, lambda block: masked(block, valid))
            for h in range(0, heads, pair):
                span = slice(h * rows, (h + pair) * rows)
                o = o_buf[span, :]
                grads, offset = [], 0.0
                for k in range(parts):
                    grad = lax.dot_general(v_refs[k][:, cols], o, NT, preferred_element_type=F32)
                    weight = p_ref[group, k * rows : (k + 1) * rows, span].astype(F32)
                    offset = offset + jnp.sum(weight * grad, axis=0, keepdims=True)
                    grads.append(grad)
                for k in range(parts):
                    weight = p_ref[group, k * rows : (k + 1) * rows, span].astype(F32)
                    s_buf[k * rows : (k + 1) * rows, span] = (weight * (grads[k] - offset)).astype(BF16)
            for k in range(parts):
                part = jnp.dot(s_buf[k * rows : (k + 1) * rows, :], q_buf[...], preferred_element_type=F32)
                k_refs[k][:, cols] = (part * scale).astype(k_refs[k].dtype)

    kinds = [F32] + [BF16] * (parts - 1)
    return pl.pallas_call(
        kernel,
        out_shape=[jax.ShapeDtypeStruct((rows, kv_width), kind) for kind in kinds],
        in_specs=[SMEM] + [VMEM] * (3 + parts),
        out_specs=[VMEM] * parts,
        scratch_shapes=[pltpu.VMEM((heads * rows, HD), BF16)] * 2
        + [pltpu.VMEM((total, heads * rows), BF16)],
        compiler_params=grant(8 + 3 * parts),
        cost_estimate=estimate(4 * rows * total * width, 2 * (2 * rows * width + 2 * total * kv_width)),
        name="key_side",
    )(place, weights, queries, out_grads, *values)


def settle(parts_list):
    rows, cols = parts_list[0].shape

    def kernel(*refs):
        total = refs[0][...].astype(F32)
        for r in refs[1:-1]:
            total = total + r[...].astype(F32)
        refs[-1][...] = total.T.astype(BF16)

    return pl.pallas_call(
        kernel,
        out_shape=jax.ShapeDtypeStruct((cols, rows), BF16),
        in_specs=[VMEM] * len(parts_list),
        out_specs=VMEM,
        compiler_params=grant(8),
        cost_estimate=estimate(rows * cols * 4, 10 * rows * cols),
        name="settle",
    )(*parts_list)


def doc_grad(place, value_grads, features, before, blocks):
    parts = len(features)
    rows, chunk = features[0].shape
    cols = value_grads[0].shape[0]
    width = cols // blocks
    half = blocks // 2

    def kernel(place_ref, *refs):
        x_refs, d_refs = refs[:parts], refs[parts : 2 * parts]
        keep_ref, send_ref, square_ref = refs[-3:]
        odd = place_ref[2]
        x = jnp.concatenate([r[...] for r in x_refs], axis=0)

        def side(which):
            picked = []
            for z in range(half):
                block = pl.ds(pl.multiple_of((2 * z + which) * width, width), width)
                picked.append(jnp.concatenate([r[block, :] for r in d_refs], axis=1))
            return jnp.dot(jnp.concatenate(picked, axis=0), x, preferred_element_type=F32)

        kept = side(odd)
        sent = side(1 - odd)
        keep_ref[...] = kept
        send_ref[...] = sent.astype(BF16)
        both = kept * kept + sent * sent
        folded = jnp.sum(both.reshape(half * width // 8, 8, chunk), axis=0)
        squares = sum(folded[:, i * HD : (i + 1) * HD] for i in range(chunk // HD))
        square_ref[...] = squares + (refs[2 * parts][...] if before else 0.0)

    return pl.pallas_call(
        kernel,
        out_shape=[
            jax.ShapeDtypeStruct((half * width, chunk), F32),
            jax.ShapeDtypeStruct((half * width, chunk), BF16),
            jax.ShapeDtypeStruct((8, HD), F32),
        ],
        in_specs=[SMEM] + [VMEM] * (2 * parts + len(before)),
        out_specs=[VMEM] * 3,
        compiler_params=grant(8),
        cost_estimate=estimate(2 * rows * parts * chunk * cols, 2 * rows * parts * (chunk + cols) + 3 * cols * chunk),
        name="doc_grad",
    )(place, *features, *value_grads, *before)


def combine(place, squares, kept, received, order, blocks, clip):
    half = blocks // 2
    tall = kept[0].shape[0]
    sizes = [k.shape[1] for k in kept]
    whole = sum(sizes)
    width = tall // half
    chunks = len(kept)
    count = len(squares)

    def kernel(place_ref, *refs):
        square_refs = refs[:count]
        keep_refs = refs[count : count + chunks]
        got_refs = refs[count + chunks : count + 2 * chunks]
        norm_ref, outs = refs[count + 2 * chunks], refs[count + 2 * chunks + 1 :]
        sums = square_refs[0][...]
        for r in square_refs[1:]:
            sums = sums + r[...]

        def norm(block):
            lanes = jnp.sum(block, axis=1, keepdims=True)
            return jnp.sqrt(jnp.sum(lanes, axis=0, keepdims=True))

        mine, other = norm(sums[:8]), norm(sums[8:])
        norm_ref[...] = jnp.broadcast_to(mine, (8, HD))
        mine, other = clip / (mine + 0.01), clip / (other + 0.01)
        for i in range(half):
            rows = pl.ds(pl.multiple_of(place_ref[order + i] * width, width), width)
            for j in range(chunks):
                total = keep_refs[j][rows, :] * mine + got_refs[j][rows, :].astype(F32) * other
                start = sum(sizes[:j])
                outs[i][:, start : start + sizes[j]] = total.astype(BF16)

    out = pl.pallas_call(
        kernel,
        out_shape=[jax.ShapeDtypeStruct((8, HD), F32)]
        + [jax.ShapeDtypeStruct((width, whole), BF16)] * half,
        in_specs=[SMEM] + [VMEM] * (count + 2 * chunks),
        out_specs=[VMEM] * (half + 1),
        compiler_params=grant(12),
        cost_estimate=estimate(4 * tall * whole, 8 * tall * whole),
        name="combine",
    )(place, *squares, *kept, *received)
    return out[0], out[1:]


def relay(place, flag, mine, got):
    def kernel(place_ref, mine_ref, got_ref, out_ref):
        got = got_ref[...].astype(F32)
        got = jnp.where(place_ref[flag] == 1, got, jnp.zeros_like(got))
        out_ref[...] = (mine_ref[...].astype(F32) + got).astype(BF16)

    return pl.pallas_call(
        kernel,
        out_shape=jax.ShapeDtypeStruct(mine.shape, BF16),
        in_specs=[SMEM, VMEM, VMEM],
        out_specs=VMEM,
        compiler_params=grant(8),
        cost_estimate=estimate(2 * mine.size, 6 * mine.size),
        name="relay",
    )(place, mine, got)


def add_up(place, flag, gated, terms, kind):
    def kernel(place_ref, *refs):
        total = refs[len(gated)][...].astype(F32)
        for r in refs[len(gated) + 1 : -1]:
            total = total + r[...].astype(F32)
        for r in refs[: len(gated)]:
            got = r[...].astype(F32)
            total = total + jnp.where(place_ref[flag] == 1, jnp.zeros_like(got), got)
        refs[-1][...] = total.astype(kind)

    size = terms[0].size
    return pl.pallas_call(
        kernel,
        out_shape=jax.ShapeDtypeStruct(terms[0].shape, kind),
        in_specs=[SMEM] + [VMEM] * (len(gated) + len(terms)),
        out_specs=VMEM,
        compiler_params=grant(8),
        cost_estimate=estimate(8 * size, 14 * size),
        name="add_up",
    )(place, *gated, *terms)


def step(layer_input, value_weight, queries, key_states, out_grads, lengths):
    parts = lax.axis_size("context")
    docs = lax.axis_size("dp")
    planes = docs // 2
    context = lax.axis_index("context")
    doc = lax.axis_index("dp")
    z = doc // 2
    if planes == 4:
        order = [z, 3 * (1 - z % 2), 2 - z // 2]
        order.append(6 - sum(order))
    else:
        order = [z ^ k for k in range(planes)]
    inner = (z > 0) & (z < planes - 1)
    place = jnp.stack([context, lengths[0], doc % 2, z, inner] + order).astype(jnp.int32)
    width = layer_input.shape[2]
    sizes = split(width // parts)
    cols = value_weight.shape[1]

    def over_context(x, k):
        return lax.ppermute(x, "context", [(i, i ^ k) for i in range(parts)])

    def over_planes(x, hops):
        return lax.ppermute(x, "dp", [(2 * a + c, 2 * b + c) for a, b in hops for c in range(2)])

    def over_cores(x):
        return lax.ppermute(x, "dp", [(i, i ^ 1) for i in range(docs)])

    keys = [key_states[0]] + [over_context(key_states[0], k) for k in range(1, parts)]
    pieces = cut(place, layer_input[0], parts, sizes)
    features = []
    for j in range(len(sizes)):
        features.append([pieces[0][j]] + [over_context(pieces[k][j], k) for k in range(1, parts)])
    weights, value_parts = weigh(place, queries[0], out_grads[0], keys)
    blocks = [value_parts[0]] + [over_context(value_parts[k], k) for k in range(1, parts)]
    value_low = settle(blocks)
    value_grads = [value_low] + [over_context(value_low, k) for k in range(1, parts)]

    kept, received, square = [], [], []
    for j in range(len(sizes)):
        keep, send, *square = doc_grad(place, value_grads, features[j], square, docs)
        kept.append(keep)
        received.append(over_cores(send))
    squares = jnp.concatenate([square[0], over_cores(square[0])], axis=0)
    squares = [squares] + [over_context(squares, k) for k in range(1, parts)]
    norm, shares = combine(place, squares, kept, received, 5, docs, math.sqrt(width * cols))

    own_values = project(layer_input[0], value_weight)
    values = [own_values] + [over_context(own_values, k) for k in range(1, parts)]
    key_parts = key_side(place, weights, queries[0], out_grads[0], values)
    key_blocks = [key_parts[0]] + [over_context(key_parts[k], k) for k in range(1, parts)]
    key_grads = add_up(place, 4, [], key_blocks, BF16)[None]

    if planes == 4:
        first = over_planes(shares[1], [(0, 1), (1, 0), (2, 3), (3, 2)])
        far = over_planes(shares[2], [(0, 2), (3, 1)])
        near = over_planes(shares[2], [(1, 2), (2, 1)])
        onward = relay(place, 4, shares[3], first)
        last = over_planes(onward, [(0, 1), (3, 2), (1, 3), (2, 0)])
        total = add_up(place, 4, [first], [shares[0], far, near, last], F32)
    else:
        got = [over_planes(shares[k], [(i, i ^ k) for i in range(planes)]) for k in range(1, planes)]
        total = add_up(place, 4, [], [shares[0]] + got, F32)
    return total.T, norm[0, :1], key_grads


def solution(mesh):
    placed = (
        P("dp", "context", None),
        P(),
        P("dp", "context", None),
        P("dp", "context", None),
        P("dp", "context", None),
        P("dp"),
    )
    return jax.shard_map(
        step,
        mesh=mesh,
        in_specs=placed,
        out_specs=(P("context", "dp"), P("dp"), P("dp", "context", None)),
        check_vma=False,
    )
```

profile of v0, /device:TPU:0, one launch (start us, length us, event | category | flops | bytes accessed | tf_op | source)
XLA Modules:
  0.0 114.0 jit_solution(14773695963018740159)
XLA Ops:
  0.6 3.0 %collective-permute-start.3 = (bf16[128,512]{1,0:T(8,128)(2,1)}, bf16[128,512]{1,0:T(8,128)(2,1)S(1)}, u32[]{:S(2)}, u32[]{:S(2)}) collective-permute-start(bf16[128,512]{1,0:T(8,128)(2,1)} %bitcast.22), channel_id=1, source_target_pairs={{0,1},{1,0},{2,3},{3,2},{4,5},{5,4},{6,7},{7,6},{8,9},{9,8},{10,11... | collective-permute-start | bytes 393224 | tf_op jit(solution)/shard_map/ppermute | solution.py:384
  3.7 1.5 %collective-permute-start.4 = (bf16[128,512]{1,0:T(8,128)(2,1)}, bf16[128,512]{1,0:T(8,128)(2,1)S(1)}, u32[]{:S(2)}, u32[]{:S(2)}) collective-permute-start(bf16[128,512]{1,0:T(8,128)(2,1)} %bitcast.23), channel_id=1, source_target_pairs={{0,2},{1,3},{2,0},{3,1},{4,6},{5,7},{6,4},{7,5},{8,10},{9,11},{10,... | collective-permute-start | bytes 393224 | tf_op jit(solution)/shard_map/ppermute | solution.py:384
  5.9 0.1 stack.36.place_ref
  5.9 1.6 %copy-done = bf16[1,128,8192]{2,1,0:T(8,128)(2,1)S(1)} copy-done((bf16[1,128,8192]{2,1,0:T(8,128)(2,1)S(1)}, bf16[1,128,8192]{2,1,0:T(8,128)(2,1)}, u32[]{:S(2)}) %copy-start) | copy-done | bytes 2097176
  7.5 0.7 cut.1
  8.2 2.0 %collective-permute-start.12 = (bf16[128,1280]{1,0:T(8,128)(2,1)S(1)}, bf16[128,1280]{1,0:T(8,128)(2,1)S(1)}, u32[]{:S(2)}, u32[]{:S(2)}) collective-permute-start(bf16[128,1280]{1,0:T(8,128)(2,1)S(1)} %get-tuple-element.40), channel_id=1, source_target_pairs={{0,1},{1,0},{2,3},{3,2},{4,5},{5,4},{6,7},{7,6},{8,9},{9,8},{10,11... | collective-permute-start | bytes 983048 | tf_op jit(solution)/shard_map/ppermute | solution.py:384
  10.2 1.4 %collective-permute-done.4.rest_2_ = bf16[128,512]{1,0:T(8,128)(2,1)S(1)} collective-permute-done((bf16[128,512]{1,0:T(8,128)(2,1)}, bf16[128,512]{1,0:T(8,128)(2,1)S(1)}, u32[]{:S(2)}, u32[]{:S(2)}) %collective-permute-start.4) | collective-permute-done | bytes 131104 | tf_op jit(solution)/shard_map/ppermute | solution.py:384
  11.7 1.4 %copy-done.2 = bf16[1,128,4096]{2,1,0:T(8,128)(2,1)S(1)} copy-done((bf16[1,128,4096]{2,1,0:T(8,128)(2,1)S(1)}, bf16[1,128,4096]{2,1,0:T(8,128)(2,1)}, u32[]{:S(2)}) %copy-start.2) | copy-done | bytes 1048600
  13.0 1.4 %copy-done.4 = bf16[1,128,4096]{2,1,0:T(8,128)(2,1)S(1)} copy-done((bf16[1,128,4096]{2,1,0:T(8,128)(2,1)S(1)}, bf16[1,128,4096]{2,1,0:T(8,128)(2,1)}, u32[]{:S(2)}) %copy-start.4) | copy-done | bytes 1048600
  14.5 0.9 copy-done.6
  15.4 5.8 %weigh.1 = (bf16[4,512,1024]{2,1,0:T(8,128)(2,1)S(1)}, f32[128,512]{1,0:T(8,128)S(1)}, bf16[128,512]{1,0:T(8,128)(2,1)S(1)}, bf16[128,512]{1,0:T(8,128)(2,1)S(1)}, bf16[128,512]{1,0:T(8,128)(2,1)S(1)}) custom-call(s32[9]{0:T(128)S(1)} %stack.36.place_ref, bf16[128,4096]{1,0:T(8,128)(2,1)S(1)} %bitcast.18, bf16[128,4096]{1,0:T(8,128)(2,1)S(1)} %bitcast.20, ...), custom_call_target="tpu_custom_call" | custom-call | flops 10737418240 | bytes 3145728 | tf_op jit(solution)/shard_map/weigh/pallas_call | solution.py:148
  21.2 1.4 %collective-permute-start.6 = (bf16[128,512]{1,0:T(8,128)(2,1)S(1)}, bf16[128,512]{1,0:T(8,128)(2,1)S(1)}, u32[]{:S(2)}, u32[]{:S(2)}) collective-permute-start(bf16[128,512]{1,0:T(8,128)(2,1)S(1)} %get-tuple-element.36), channel_id=1, source_target_pairs={{0,1},{1,0},{2,3},{3,2},{4,5},{5,4},{6,7},{7,6},{8,9},{9,8},{10,11... | collective-permute-start | bytes 393224 | tf_op jit(solution)/shard_map/ppermute | solution.py:384
  22.6 0.7 collective-permute-start.13
  23.3 1.4 %collective-permute-start.14 = (bf16[128,1280]{1,0:T(8,128)(2,1)S(1)}, bf16[128,1280]{1,0:T(8,128)(2,1)S(1)}, u32[]{:S(2)}, u32[]{:S(2)}) collective-permute-start(bf16[128,1280]{1,0:T(8,128)(2,1)S(1)} %get-tuple-element.42), channel_id=1, source_target_pairs={{0,3},{1,2},{2,1},{3,0},{4,7},{5,6},{6,5},{7,4},{8,11},{9,10},{10,... | collective-permute-start | bytes 983048 | tf_op jit(solution)/shard_map/ppermute | solution.py:384
  24.8 1.5 %collective-permute-start.7 = (bf16[128,512]{1,0:T(8,128)(2,1)S(1)}, bf16[128,512]{1,0:T(8,128)(2,1)S(1)}, u32[]{:S(2)}, u32[]{:S(2)}) collective-permute-start(bf16[128,512]{1,0:T(8,128)(2,1)S(1)} %get-tuple-element.37), channel_id=1, source_target_pairs={{0,2},{1,3},{2,0},{3,1},{4,6},{5,7},{6,4},{7,5},{8,10},{9,11},{10,... | collective-permute-start | bytes 393224 | tf_op jit(solution)/shard_map/ppermute | solution.py:384
  26.3 1.2 %collective-permute-done.6.refs_1_ = bf16[128,512]{1,0:T(8,128)(2,1)S(1)} collective-permute-done((bf16[128,512]{1,0:T(8,128)(2,1)S(1)}, bf16[128,512]{1,0:T(8,128)(2,1)S(1)}, u32[]{:S(2)}, u32[]{:S(2)}) %collective-permute-start.6) | collective-permute-done | bytes 131104 | tf_op jit(solution)/shard_map/ppermute | solution.py:384
  27.5 1.4 %collective-permute-start.8 = (bf16[128,512]{1,0:T(8,128)(2,1)S(1)}, bf16[128,512]{1,0:T(8,128)(2,1)S(1)}, u32[]{:S(2)}, u32[]{:S(2)}) collective-permute-start(bf16[128,512]{1,0:T(8,128)(2,1)S(1)} %get-tuple-element.38), channel_id=1, source_target_pairs={{0,3},{1,2},{2,1},{3,0},{4,7},{5,6},{6,5},{7,4},{8,11},{9,10},{10,... | collective-permute-start | bytes 393224 | tf_op jit(solution)/shard_map/ppermute | solution.py:384
  28.9 14.6 %collective-permute-done.7.refs_2_ = bf16[128,512]{1,0:T(8,128)(2,1)S(1)} collective-permute-done((bf16[128,512]{1,0:T(8,128)(2,1)S(1)}, bf16[128,512]{1,0:T(8,128)(2,1)S(1)}, u32[]{:S(2)}, u32[]{:S(2)}) %collective-permute-start.7) | collective-permute-done | bytes 131104 | tf_op jit(solution)/shard_map/ppermute | solution.py:384
  43.5 0.1 settle.1.refs_4_
  43.6 0.6 collective-permute-start.10
  44.2 1.4 %collective-permute-start.11 = (bf16[512,128]{1,0:T(8,128)(2,1)S(1)}, bf16[512,128]{1,0:T(8,128)(2,1)S(1)}, u32[]{:S(2)}, u32[]{:S(2)}) collective-permute-start(bf16[512,128]{1,0:T(8,128)(2,1)S(1)} %settle.1.refs_4_), channel_id=1, source_target_pairs={{0,3},{1,2},{2,1},{3,0},{4,7},{5,6},{6,5},{7,4},{8,11},{9,10},{10,... | collective-permute-start | bytes 393224 | tf_op jit(solution)/shard_map/ppermute | solution.py:384
  45.6 1.6 %collective-permute-start.9 = (bf16[512,128]{1,0:T(8,128)(2,1)S(1)}, bf16[512,128]{1,0:T(8,128)(2,1)S(1)}, u32[]{:S(2)}, u32[]{:S(2)}) collective-permute-start(bf16[512,128]{1,0:T(8,128)(2,1)S(1)} %settle.1.refs_4_), channel_id=1, source_target_pairs={{0,1},{1,0},{2,3},{3,2},{4,5},{5,4},{6,7},{7,6},{8,9},{9,8},{10,11... | collective-permute-start | bytes 393224 | tf_op jit(solution)/shard_map/ppermute | solution.py:384
  47.2 3.4 %collective-permute-done.10.refs_6_ = bf16[512,128]{1,0:T(8,128)(2,1)S(1)} collective-permute-done((bf16[512,128]{1,0:T(8,128)(2,1)S(1)}, bf16[512,128]{1,0:T(8,128)(2,1)S(1)}, u32[]{:S(2)}, u32[]{:S(2)}) %collective-permute-start.10) | collective-permute-done | bytes 131104 | tf_op jit(solution)/shard_map/ppermute | solution.py:384
  50.6 1.2 %collective-permute-done.9.refs_5_ = bf16[512,128]{1,0:T(8,128)(2,1)S(1)} collective-permute-done((bf16[512,128]{1,0:T(8,128)(2,1)S(1)}, bf16[512,128]{1,0:T(8,128)(2,1)S(1)}, u32[]{:S(2)}, u32[]{:S(2)}) %collective-permute-start.9) | collective-permute-done | bytes 131104 | tf_op jit(solution)/shard_map/ppermute | solution.py:384
  51.8 1.4 %doc_grad.2 = (f32[256,1280]{1,0:T(8,128)S(1)}, bf16[256,1280]{1,0:T(8,128)(2,1)S(1)}, f32[8,128]{1,0:T(8,128)S(1)}) custom-call(s32[9]{0:T(128)S(1)} %stack.36.place_ref, bf16[128,1280]{1,0:T(8,128)(2,1)S(1)} %get-tuple-element.39.refs_0_, bf16[128,1280]{1,0:T(8,128)(2,1)S(1)} %collective-permute-done.12.refs_1_, ...), custom_call_target="tpu_custom_call" | custom-call | flops 671088640 | bytes 3801088 | tf_op jit(solution)/shard_map/doc_grad/pallas_call | solution.py:266
  53.2 0.1 collective-permute-start.19
  53.3 0.7 collective-permute-start
  53.9 1.6 %collective-permute-start.1 = (bf16[128,768]{1,0:T(8,128)(2,1)S(1)}, bf16[128,768]{1,0:T(8,128)(2,1)S(1)}, u32[]{:S(2)}, u32[]{:S(2)}) collective-permute-start(bf16[128,768]{1,0:T(8,128)(2,1)S(1)} %get-tuple-element.33), channel_id=1, source_target_pairs={{0,2},{1,3},{2,0},{3,1},{4,6},{5,7},{6,4},{7,5},{8,10},{9,11},{10,... | collective-permute-start | bytes 589832 | tf_op jit(solution)/shard_map/ppermute | solution.py:384
  55.6 1.2 %collective-permute-start.2 = (bf16[128,768]{1,0:T(8,128)(2,1)S(1)}, bf16[128,768]{1,0:T(8,128)(2,1)S(1)}, u32[]{:S(2)}, u32[]{:S(2)}) collective-permute-start(bf16[128,768]{1,0:T(8,128)(2,1)S(1)} %get-tuple-element.34), channel_id=1, source_target_pairs={{0,3},{1,2},{2,1},{3,0},{4,7},{5,6},{6,5},{7,4},{8,11},{9,10},{10,... | collective-permute-start | bytes 589832 | tf_op jit(solution)/shard_map/ppermute | solution.py:384
  56.8 4.3 %collective-permute-done.refs_1_ = bf16[128,768]{1,0:T(8,128)(2,1)S(1)} collective-permute-done((bf16[128,768]{1,0:T(8,128)(2,1)S(1)}, bf16[128,768]{1,0:T(8,128)(2,1)S(1)}, u32[]{:S(2)}, u32[]{:S(2)}) %collective-permute-start) | collective-permute-done | bytes 196640 | tf_op jit(solution)/shard_map/ppermute | solution.py:384
  61.1 4.0 %collective-permute-done.1.refs_2_ = bf16[128,768]{1,0:T(8,128)(2,1)S(1)} collective-permute-done((bf16[128,768]{1,0:T(8,128)(2,1)S(1)}, bf16[128,768]{1,0:T(8,128)(2,1)S(1)}, u32[]{:S(2)}, u32[]{:S(2)}) %collective-permute-start.1) | collective-permute-done | bytes 196640 | tf_op jit(solution)/shard_map/ppermute | solution.py:384
  65.1 1.1 doc_grad.3
  66.3 0.1 collective-permute-start.20
  66.3 0.5 collective-permute-start.15
  66.8 1.2 %collective-permute-done.15 = f32[8,128]{1,0:T(8,128)S(1)} collective-permute-done((f32[8,128]{1,0:T(8,128)S(1)}, f32[8,128]{1,0:T(8,128)S(1)}, u32[]{:S(2)}, u32[]{:S(2)}) %collective-permute-start.15) | collective-permute-done | bytes 4128 | tf_op jit(solution)/shard_map/ppermute | solution.py:390
  68.0 1.4 %collective-permute-start.16 = (f32[16,128]{1,0:T(8,128)S(1)}, f32[16,128]{1,0:T(8,128)S(1)}, u32[]{:S(2)}, u32[]{:S(2)}) collective-permute-start(f32[16,128]{1,0:T(8,128)S(1)} %constant_dynamic-update-slice_fusion.refs_0_), channel_id=1, source_target_pairs={{0,1},{1,0},{2,3},{3,2},{4,5},{5,4},{6,7},{7,6},{8,9},{9,8},{10,11... | collective-permute-start | bytes 24584 | tf_op jit(solution)/shard_map/ppermute | solution.py:384
  69.5 0.6 collective-permute-start.17
  70.0 1.5 %collective-permute-start.18 = (f32[16,128]{1,0:T(8,128)S(1)}, f32[16,128]{1,0:T(8,128)S(1)}, u32[]{:S(2)}, u32[]{:S(2)}) collective-permute-start(f32[16,128]{1,0:T(8,128)S(1)} %constant_dynamic-update-slice_fusion.refs_0_), channel_id=1, source_target_pairs={{0,3},{1,2},{2,1},{3,0},{4,7},{5,6},{6,5},{7,4},{8,11},{9,10},{10,... | collective-permute-start | bytes 24584 | tf_op jit(solution)/shard_map/ppermute | solution.py:384
  71.5 0.2 collective-permute-done.16.refs_1_
  71.7 1.4 %collective-permute-done.17.refs_2_ = f32[16,128]{1,0:T(8,128)S(1)} collective-permute-done((f32[16,128]{1,0:T(8,128)S(1)}, f32[16,128]{1,0:T(8,128)S(1)}, u32[]{:S(2)}, u32[]{:S(2)}) %collective-permute-start.17) | collective-permute-done | bytes 8224 | tf_op jit(solution)/shard_map/ppermute | solution.py:384
  73.1 1.5 %collective-permute-done.18.refs_3_ = f32[16,128]{1,0:T(8,128)S(1)} collective-permute-done((f32[16,128]{1,0:T(8,128)S(1)}, f32[16,128]{1,0:T(8,128)S(1)}, u32[]{:S(2)}, u32[]{:S(2)}) %collective-permute-start.18) | collective-permute-done | bytes 8224 | tf_op jit(solution)/shard_map/ppermute | solution.py:384
  74.6 1.2 %combine.1 = (f32[8,128]{1,0:T(8,128)S(1)}, bf16[64,2048]{1,0:T(8,128)(2,1)S(1)}, bf16[64,2048]{1,0:T(8,128)(2,1)S(1)}, bf16[64,2048]{1,0:T(8,128)(2,1)S(1)}, bf16[64,2048]{1,0:T(8,128)(2,1)S(1)}) custom-call(s32[9]{0:T(128)S(1)} %stack.36.place_ref, f32[16,128]{1,0:T(8,128)S(1)} %constant_dynamic-update-slice_fusion.refs_0_, ...), custom_call_target="tpu_custom_call" | custom-call | flops 2097152 | bytes 4194304 | tf_op jit(solution)/shard_map/combine/pallas_call | solution.py:313
  75.8 1.7 %collective-permute-start.21 = (bf16[64,2048]{1,0:T(8,128)(2,1)S(1)}, bf16[64,2048]{1,0:T(8,128)(2,1)S(1)}, u32[]{:S(2)}, u32[]{:S(2)}) collective-permute-start(bf16[64,2048]{1,0:T(8,128)(2,1)S(1)} %get-tuple-element.49), channel_id=1, source_target_pairs={{0,8},{4,12},{8,0},{12,4},{16,24},{20,28},{24,16},{28,20},{1,9},{5... | collective-permute-start | bytes 786440 | tf_op jit(solution)/shard_map/ppermute | solution.py:387
  77.5 1.3 %project.1.rest_0_ = bf16[128,512]{1,0:T(8,128)(2,1)S(1)} custom-call(bf16[128,8192]{1,0:T(8,128)(2,1)S(1)} %bitcast.17, bf16[8192,512]{1,0:T(8,128)(2,1)S(1)} %bitcast.15), custom_call_target="tpu_custom_call" | custom-call | flops 1073741824 | bytes 10485760 | tf_op jit(solution)/shard_map/project/pallas_call | solution.py:74
  78.7 1.4 %collective-permute-start.25 = (bf16[128,512]{1,0:T(8,128)(2,1)S(1)}, bf16[128,512]{1,0:T(8,128)(2,1)S(1)}, u32[]{:S(2)}, u32[]{:S(2)}) collective-permute-start(bf16[128,512]{1,0:T(8,128)(2,1)S(1)} %project.1.rest_0_), channel_id=1, source_target_pairs={{0,1},{1,0},{2,3},{3,2},{4,5},{5,4},{6,7},{7,6},{8,9},{9,8},{10,11... | collective-permute-start | bytes 393224 | tf_op jit(solution)/shard_map/ppermute | solution.py:384
  80.1 0.6 collective-permute-start.26
  80.7 1.6 %collective-permute-start.27 = (bf16[128,512]{1,0:T(8,128)(2,1)S(1)}, bf16[128,512]{1,0:T(8,128)(2,1)S(1)}, u32[]{:S(2)}, u32[]{:S(2)}) collective-permute-start(bf16[128,512]{1,0:T(8,128)(2,1)S(1)} %project.1.rest_0_), channel_id=1, source_target_pairs={{0,3},{1,2},{2,1},{3,0},{4,7},{5,6},{6,5},{7,4},{8,11},{9,10},{10,... | collective-permute-start | bytes 393224 | tf_op jit(solution)/shard_map/ppermute | solution.py:384
  82.3 2.2 %collective-permute-done.25.rest_1_ = bf16[128,512]{1,0:T(8,128)(2,1)S(1)} collective-permute-done((bf16[128,512]{1,0:T(8,128)(2,1)S(1)}, bf16[128,512]{1,0:T(8,128)(2,1)S(1)}, u32[]{:S(2)}, u32[]{:S(2)}) %collective-permute-start.25) | collective-permute-done | bytes 131104 | tf_op jit(solution)/shard_map/ppermute | solution.py:384
  84.5 0.5 collective-permute-done.26.rest_2_
  85.0 1.5 %collective-permute-done.27.rest_3_ = bf16[128,512]{1,0:T(8,128)(2,1)S(1)} collective-permute-done((bf16[128,512]{1,0:T(8,128)(2,1)S(1)}, bf16[128,512]{1,0:T(8,128)(2,1)S(1)}, u32[]{:S(2)}, u32[]{:S(2)}) %collective-permute-start.27) | collective-permute-done | bytes 131104 | tf_op jit(solution)/shard_map/ppermute | solution.py:384
  86.6 5.1 %key_side.1 = (f32[128,512]{1,0:T(8,128)S(1)}, bf16[128,512]{1,0:T(8,128)(2,1)S(1)}, bf16[128,512]{1,0:T(8,128)(2,1)S(1)}, bf16[128,512]{1,0:T(8,128)(2,1)S(1)}) custom-call(s32[9]{0:T(128)S(1)} %stack.36.place_ref, bf16[4,512,1024]{2,1,0:T(8,128)(2,1)S(1)} %get-tuple-element.54.p_ref, bf16[128,4096]{1,0:T(8,128)(2,1)S(1)} %bitcast.19, ...), custom_call_target="tpu_custom_call" | custom-call | flops 1073741824 | bytes 3145728 | tf_op jit(solution)/shard_map/key_side/pallas_call | solution.py:204
  91.7 1.7 %collective-permute-start.28 = (bf16[128,512]{1,0:T(8,128)(2,1)S(1)}, bf16[128,512]{1,0:T(8,128)(2,1)S(1)}, u32[]{:S(2)}, u32[]{:S(2)}) collective-permute-start(bf16[128,512]{1,0:T(8,128)(2,1)S(1)} %get-tuple-element.56), channel_id=1, source_target_pairs={{0,1},{1,0},{2,3},{3,2},{4,5},{5,4},{6,7},{7,6},{8,9},{9,8},{10,11... | collective-permute-start | bytes 393224 | tf_op jit(solution)/shard_map/ppermute | solution.py:384
  93.5 4.5 %collective-permute-start.22 = (bf16[64,2048]{1,0:T(8,128)(2,1)S(1)}, bf16[64,2048]{1,0:T(8,128)(2,1)S(1)}, u32[]{:S(2)}, u32[]{:S(2)}) collective-permute-start(bf16[64,2048]{1,0:T(8,128)(2,1)S(1)} %get-tuple-element.51), channel_id=1, source_target_pairs={{0,16},{4,20},{24,8},{28,12},{1,17},{5,21},{25,9},{29,13},{2,18},{... | collective-permute-start | bytes 786440 | tf_op jit(solution)/shard_map/ppermute | solution.py:387
  98.0 0.7 collective-permute-start.23
  98.6 0.6 relay.1
  99.3 1.2 %collective-permute-start.24 = (bf16[64,2048]{1,0:T(8,128)(2,1)S(1)}, bf16[64,2048]{1,0:T(8,128)(2,1)S(1)}, u32[]{:S(2)}, u32[]{:S(2)}) collective-permute-start(bf16[64,2048]{1,0:T(8,128)(2,1)S(1)} %relay.1), channel_id=1, source_target_pairs={{0,8},{4,12},{24,16},{28,20},{8,24},{12,28},{16,0},{20,4},{1,9},{5... | collective-permute-start | bytes 786440 | tf_op jit(solution)/shard_map/ppermute | solution.py:387
  100.5 0.5 collective-permute-start.29
  101.0 1.3 %collective-permute-start.30 = (bf16[128,512]{1,0:T(8,128)(2,1)S(1)}, bf16[128,512]{1,0:T(8,128)(2,1)S(1)}, u32[]{:S(2)}, u32[]{:S(2)}) collective-permute-start(bf16[128,512]{1,0:T(8,128)(2,1)S(1)} %get-tuple-element.58), channel_id=1, source_target_pairs={{0,3},{1,2},{2,1},{3,0},{4,7},{5,6},{6,5},{7,4},{8,11},{9,10},{10,... | collective-permute-start | bytes 393224 | tf_op jit(solution)/shard_map/ppermute | solution.py:384
  102.3 3.1 %collective-permute-done.29.refs_2_ = bf16[128,512]{1,0:T(8,128)(2,1)S(1)} collective-permute-done((bf16[128,512]{1,0:T(8,128)(2,1)S(1)}, bf16[128,512]{1,0:T(8,128)(2,1)S(1)}, u32[]{:S(2)}, u32[]{:S(2)}) %collective-permute-start.29) | collective-permute-done | bytes 131104 | tf_op jit(solution)/shard_map/ppermute | solution.py:384
  105.5 1.4 %collective-permute-done.30.refs_3_ = bf16[128,512]{1,0:T(8,128)(2,1)S(1)} collective-permute-done((bf16[128,512]{1,0:T(8,128)(2,1)S(1)}, bf16[128,512]{1,0:T(8,128)(2,1)S(1)}, u32[]{:S(2)}, u32[]{:S(2)}) %collective-permute-start.30) | collective-permute-done | bytes 131104 | tf_op jit(solution)/shard_map/ppermute | solution.py:384
  106.9 1.3 %add_up.3 = bf16[128,512]{1,0:T(8,128)(2,1)} custom-call(s32[9]{0:T(128)S(1)} %stack.36.place_ref, f32[128,512]{1,0:T(8,128)S(1)} %get-tuple-element.55.refs_0_, bf16[128,512]{1,0:T(8,128)(2,1)S(1)} %collective-permute-done.28.refs_1_, bf16[128,512]{1,0:T(8,128)(2,1)S(1)} %collective-permute-done.29.refs_2_, bf16[128,512]{1,0:T(8,128)(2,1)S(1)} %collective-permute-done.30.refs_3_), custom_call_target="tpu_custom_call" | custom-call | flops 524288 | bytes 917504 | tf_op jit(solution)/shard_map/add_up/pallas_call | solution.py:354
  108.1 0.5 slice.3
  108.6 3.9 %collective-permute-done.24.refs_4_ = bf16[64,2048]{1,0:T(8,128)(2,1)S(1)} collective-permute-done((bf16[64,2048]{1,0:T(8,128)(2,1)S(1)}, bf16[64,2048]{1,0:T(8,128)(2,1)S(1)}, u32[]{:S(2)}, u32[]{:S(2)}) %collective-permute-start.24) | collective-permute-done | bytes 262176 | tf_op jit(solution)/shard_map/ppermute | solution.py:387
  112.5 1.5 %add_up.2 = f32[64,2048]{1,0:T(8,128)} custom-call(s32[9]{0:T(128)S(1)} %stack.36.place_ref, bf16[64,2048]{1,0:T(8,128)(2,1)S(1)} %collective-permute-done.21.got_ref.refs_0_, bf16[64,2048]{1,0:T(8,128)(2,1)S(1)} %get-tuple-element.50.refs_1_, bf16[64,2048]{1,0:T(8,128)(2,1)S(1)} %collective-permute-done.22.refs_2_, ...), custom_call_target="tpu_custom_call" | custom-call | flops 1048576 | bytes 1835008 | tf_op jit(solution)/shard_map/add_up/pallas_call | solution.py:354
  (32 shorter events, 0.1 us)
Async XLA Ops:
  0.6 9.6 %collective-permute-start.3 = (bf16[128,512]{1,0:T(8,128)(2,1)}, bf16[128,512]{1,0:T(8,128)(2,1)S(1)}, u32[]{:S(2)}, u32[]{:S(2)}) collective-permute-start(bf16[128,512]{1,0:T(8,128)(2,1)} %bitcast.22), channel_id=1, source_target_pairs={{0,1},{1,0},{2,3},{3,2},{4,5},{5,4},{6,7},{7,6},{8,9},{9,8},{10,11... | collective-permute-start | bytes 393224 | tf_op jit(solution)/shard_map/ppermute | solution.py:384
  3.7 8.0 %collective-permute-start.4 = (bf16[128,512]{1,0:T(8,128)(2,1)}, bf16[128,512]{1,0:T(8,128)(2,1)S(1)}, u32[]{:S(2)}, u32[]{:S(2)}) collective-permute-start(bf16[128,512]{1,0:T(8,128)(2,1)} %bitcast.23), channel_id=1, source_target_pairs={{0,2},{1,3},{2,0},{3,1},{4,6},{5,7},{6,4},{7,5},{8,10},{9,11},{10,... | collective-permute-start | bytes 393224 | tf_op jit(solution)/shard_map/ppermute | solution.py:384
  5.2 6.5 %collective-permute-start.5 = (bf16[128,512]{1,0:T(8,128)(2,1)}, bf16[128,512]{1,0:T(8,128)(2,1)S(1)}, u32[]{:S(2)}, u32[]{:S(2)}) collective-permute-start(bf16[128,512]{1,0:T(8,128)(2,1)} %bitcast.24), channel_id=1, source_target_pairs={{0,3},{1,2},{2,1},{3,0},{4,7},{5,6},{6,5},{7,4},{8,11},{9,10},{10,... | collective-permute-start | bytes 393224 | tf_op jit(solution)/shard_map/ppermute | solution.py:384
  5.9 1.6 %copy-start = (bf16[1,128,8192]{2,1,0:T(8,128)(2,1)S(1)}, bf16[1,128,8192]{2,1,0:T(8,128)(2,1)}, u32[]{:S(2)}) copy-start(bf16[1,128,8192]{2,1,0:T(8,128)(2,1)} %param.6) | copy-start | bytes 6291460
  8.2 37.3 %collective-permute-start.12 = (bf16[128,1280]{1,0:T(8,128)(2,1)S(1)}, bf16[128,1280]{1,0:T(8,128)(2,1)S(1)}, u32[]{:S(2)}, u32[]{:S(2)}) collective-permute-start(bf16[128,1280]{1,0:T(8,128)(2,1)S(1)} %get-tuple-element.40), channel_id=1, source_target_pairs={{0,1},{1,0},{2,3},{3,2},{4,5},{5,4},{6,7},{7,6},{8,9},{9,8},{10,11... | collective-permute-start | bytes 983048 | tf_op jit(solution)/shard_map/ppermute | solution.py:384
  11.7 65.8 %slice-start = ((s8[8388608]{0:T(1024)(128)(4,1)}), s8[4194304]{0:T(1024)(128)(4,1)S(1)}, s32[]{:S(2)}) async-start(s8[8388608]{0:T(1024)(128)(4,1)} %bitcast.14), calls=%async_computation | async-start | bytes 8388608
  11.7 1.4 %copy-start.2 = (bf16[1,128,4096]{2,1,0:T(8,128)(2,1)S(1)}, bf16[1,128,4096]{2,1,0:T(8,128)(2,1)}, u32[]{:S(2)}) copy-start(bf16[1,128,4096]{2,1,0:T(8,128)(2,1)} %param.8) | copy-start | bytes 3145732
  13.0 1.4 %copy-start.4 = (bf16[1,128,4096]{2,1,0:T(8,128)(2,1)S(1)}, bf16[1,128,4096]{2,1,0:T(8,128)(2,1)}, u32[]{:S(2)}) copy-start(bf16[1,128,4096]{2,1,0:T(8,128)(2,1)} %param.10) | copy-start | bytes 3145732
  14.5 0.9 copy-start.6
  15.4 62.1 %slice-start.1 = ((s8[8388608]{0:T(1024)(128)(4,1)}), s8[4194304]{0:T(1024)(128)(4,1)S(1)}, s32[]{:S(2)}) async-start(s8[8388608]{0:T(1024)(128)(4,1)} %bitcast.14), calls=%async_computation.1 | async-start | bytes 8388608
  21.2 56.2 %copy-start.1 = (bf16[1,128,8192]{2,1,0:T(8,128)(2,1)S(1)}, bf16[1,128,8192]{2,1,0:T(8,128)(2,1)}, u32[]{:S(2)}) copy-start(bf16[1,128,8192]{2,1,0:T(8,128)(2,1)} %param.6) | copy-start | bytes 6291460
  21.2 6.3 %collective-permute-start.6 = (bf16[128,512]{1,0:T(8,128)(2,1)S(1)}, bf16[128,512]{1,0:T(8,128)(2,1)S(1)}, u32[]{:S(2)}, u32[]{:S(2)}) collective-permute-start(bf16[128,512]{1,0:T(8,128)(2,1)S(1)} %get-tuple-element.36), channel_id=1, source_target_pairs={{0,1},{1,0},{2,3},{3,2},{4,5},{5,4},{6,7},{7,6},{8,9},{9,8},{10,11... | collective-permute-start | bytes 393224 | tf_op jit(solution)/shard_map/ppermute | solution.py:384
  22.6 24.6 %collective-permute-start.13 = (bf16[128,1280]{1,0:T(8,128)(2,1)S(1)}, bf16[128,1280]{1,0:T(8,128)(2,1)S(1)}, u32[]{:S(2)}, u32[]{:S(2)}) collective-permute-start(bf16[128,1280]{1,0:T(8,128)(2,1)S(1)} %get-tuple-element.41), channel_id=1, source_target_pairs={{0,2},{1,3},{2,0},{3,1},{4,6},{5,7},{6,4},{7,5},{8,10},{9,11},{10,... | collective-permute-start | bytes 983048 | tf_op jit(solution)/shard_map/ppermute | solution.py:384
  23.3 23.8 %collective-permute-start.14 = (bf16[128,1280]{1,0:T(8,128)(2,1)S(1)}, bf16[128,1280]{1,0:T(8,128)(2,1)S(1)}, u32[]{:S(2)}, u32[]{:S(2)}) collective-permute-start(bf16[128,1280]{1,0:T(8,128)(2,1)S(1)} %get-tuple-element.42), channel_id=1, source_target_pairs={{0,3},{1,2},{2,1},{3,0},{4,7},{5,6},{6,5},{7,4},{8,11},{9,10},{10,... | collective-permute-start | bytes 983048 | tf_op jit(solution)/shard_map/ppermute | solution.py:384
  24.8 18.7 %collective-permute-start.7 = (bf16[128,512]{1,0:T(8,128)(2,1)S(1)}, bf16[128,512]{1,0:T(8,128)(2,1)S(1)}, u32[]{:S(2)}, u32[]{:S(2)}) collective-permute-start(bf16[128,512]{1,0:T(8,128)(2,1)S(1)} %get-tuple-element.37), channel_id=1, source_target_pairs={{0,2},{1,3},{2,0},{3,1},{4,6},{5,7},{6,4},{7,5},{8,10},{9,11},{10,... | collective-permute-start | bytes 393224 | tf_op jit(solution)/shard_map/ppermute | solution.py:384
  27.5 16.0 %collective-permute-start.8 = (bf16[128,512]{1,0:T(8,128)(2,1)S(1)}, bf16[128,512]{1,0:T(8,128)(2,1)S(1)}, u32[]{:S(2)}, u32[]{:S(2)}) collective-permute-start(bf16[128,512]{1,0:T(8,128)(2,1)S(1)} %get-tuple-element.38), channel_id=1, source_target_pairs={{0,3},{1,2},{2,1},{3,0},{4,7},{5,6},{6,5},{7,4},{8,11},{9,10},{10,... | collective-permute-start | bytes 393224 | tf_op jit(solution)/shard_map/ppermute | solution.py:384
  43.6 7.0 %collective-permute-start.10 = (bf16[512,128]{1,0:T(8,128)(2,1)S(1)}, bf16[512,128]{1,0:T(8,128)(2,1)S(1)}, u32[]{:S(2)}, u32[]{:S(2)}) collective-permute-start(bf16[512,128]{1,0:T(8,128)(2,1)S(1)} %settle.1.refs_4_), channel_id=1, source_target_pairs={{0,2},{1,3},{2,0},{3,1},{4,6},{5,7},{6,4},{7,5},{8,10},{9,11},{10,... | collective-permute-start | bytes 393224 | tf_op jit(solution)/shard_map/ppermute | solution.py:384
  44.2 6.4 %collective-permute-start.11 = (bf16[512,128]{1,0:T(8,128)(2,1)S(1)}, bf16[512,128]{1,0:T(8,128)(2,1)S(1)}, u32[]{:S(2)}, u32[]{:S(2)}) collective-permute-start(bf16[512,128]{1,0:T(8,128)(2,1)S(1)} %settle.1.refs_4_), channel_id=1, source_target_pairs={{0,3},{1,2},{2,1},{3,0},{4,7},{5,6},{6,5},{7,4},{8,11},{9,10},{10,... | collective-permute-start | bytes 393224 | tf_op jit(solution)/shard_map/ppermute | solution.py:384
  45.6 6.2 %collective-permute-start.9 = (bf16[512,128]{1,0:T(8,128)(2,1)S(1)}, bf16[512,128]{1,0:T(8,128)(2,1)S(1)}, u32[]{:S(2)}, u32[]{:S(2)}) collective-permute-start(bf16[512,128]{1,0:T(8,128)(2,1)S(1)} %settle.1.refs_4_), channel_id=1, source_target_pairs={{0,1},{1,0},{2,3},{3,2},{4,5},{5,4},{6,7},{7,6},{8,9},{9,8},{10,11... | collective-permute-start | bytes 393224 | tf_op jit(solution)/shard_map/ppermute | solution.py:384
  53.2 21.4 %collective-permute-start.19 = (bf16[256,1280]{1,0:T(8,128)(2,1)S(1)}, bf16[256,1280]{1,0:T(8,128)(2,1)S(1)}, u32[]{:S(2)}, u32[]{:S(2)}) collective-permute-start(bf16[256,1280]{1,0:T(8,128)(2,1)S(1)} %get-tuple-element.47), channel_id=1, source_target_pairs={{0,4},{4,0},{8,12},{12,8},{16,20},{20,16},{24,28},{28,24},{1,5},{5... | collective-permute-start | bytes 1966088 | tf_op jit(solution)/shard_map/ppermute | solution.py:390
  53.3 7.8 %collective-permute-start = (bf16[128,768]{1,0:T(8,128)(2,1)S(1)}, bf16[128,768]{1,0:T(8,128)(2,1)S(1)}, u32[]{:S(2)}, u32[]{:S(2)}) collective-permute-start(bf16[128,768]{1,0:T(8,128)(2,1)S(1)} %get-tuple-element.32), channel_id=1, source_target_pairs={{0,1},{1,0},{2,3},{3,2},{4,5},{5,4},{6,7},{7,6},{8,9},{9,8},{10,11... | collective-permute-start | bytes 589832 | tf_op jit(solution)/shard_map/ppermute | solution.py:384
  53.9 11.2 %collective-permute-start.1 = (bf16[128,768]{1,0:T(8,128)(2,1)S(1)}, bf16[128,768]{1,0:T(8,128)(2,1)S(1)}, u32[]{:S(2)}, u32[]{:S(2)}) collective-permute-start(bf16[128,768]{1,0:T(8,128)(2,1)S(1)} %get-tuple-element.33), channel_id=1, source_target_pairs={{0,2},{1,3},{2,0},{3,1},{4,6},{5,7},{6,4},{7,5},{8,10},{9,11},{10,... | collective-permute-start | bytes 589832 | tf_op jit(solution)/shard_map/ppermute | solution.py:384
  55.6 9.6 %collective-permute-start.2 = (bf16[128,768]{1,0:T(8,128)(2,1)S(1)}, bf16[128,768]{1,0:T(8,128)(2,1)S(1)}, u32[]{:S(2)}, u32[]{:S(2)}) collective-permute-start(bf16[128,768]{1,0:T(8,128)(2,1)S(1)} %get-tuple-element.34), channel_id=1, source_target_pairs={{0,3},{1,2},{2,1},{3,0},{4,7},{5,6},{6,5},{7,4},{8,11},{9,10},{10,... | collective-permute-start | bytes 589832 | tf_op jit(solution)/shard_map/ppermute | solution.py:384
  66.3 8.3 %collective-permute-start.20 = (bf16[256,768]{1,0:T(8,128)(2,1)S(1)}, bf16[256,768]{1,0:T(8,128)(2,1)S(1)}, u32[]{:S(2)}, u32[]{:S(2)}) collective-permute-start(bf16[256,768]{1,0:T(8,128)(2,1)S(1)} %get-tuple-element.48), channel_id=1, source_target_pairs={{0,4},{4,0},{8,12},{12,8},{16,20},{20,16},{24,28},{28,24},{1,5},{5... | collective-permute-start | bytes 1179656 | tf_op jit(solution)/shard_map/ppermute | solution.py:390
  66.3 1.7 %collective-permute-start.15 = (f32[8,128]{1,0:T(8,128)S(1)}, f32[8,128]{1,0:T(8,128)S(1)}, u32[]{:S(2)}, u32[]{:S(2)}) collective-permute-start(f32[8,128]{1,0:T(8,128)S(1)} %get-tuple-element.44), channel_id=1, source_target_pairs={{0,4},{4,0},{8,12},{12,8},{16,20},{20,16},{24,28},{28,24},{1,5},{5... | collective-permute-start | bytes 12296 | tf_op jit(solution)/shard_map/ppermute | solution.py:390
  68.0 3.7 %collective-permute-start.16 = (f32[16,128]{1,0:T(8,128)S(1)}, f32[16,128]{1,0:T(8,128)S(1)}, u32[]{:S(2)}, u32[]{:S(2)}) collective-permute-start(f32[16,128]{1,0:T(8,128)S(1)} %constant_dynamic-update-slice_fusion.refs_0_), channel_id=1, source_target_pairs={{0,1},{1,0},{2,3},{3,2},{4,5},{5,4},{6,7},{7,6},{8,9},{9,8},{10,11... | collective-permute-start | bytes 24584 | tf_op jit(solution)/shard_map/ppermute | solution.py:384
  69.5 3.7 %collective-permute-start.17 = (f32[16,128]{1,0:T(8,128)S(1)}, f32[16,128]{1,0:T(8,128)S(1)}, u32[]{:S(2)}, u32[]{:S(2)}) collective-permute-start(f32[16,128]{1,0:T(8,128)S(1)} %constant_dynamic-update-slice_fusion.refs_0_), channel_id=1, source_target_pairs={{0,2},{1,3},{2,0},{3,1},{4,6},{5,7},{6,4},{7,5},{8,10},{9,11},{10,... | collective-permute-start | bytes 24584 | tf_op jit(solution)/shard_map/ppermute | solution.py:384
  70.0 4.5 %collective-permute-start.18 = (f32[16,128]{1,0:T(8,128)S(1)}, f32[16,128]{1,0:T(8,128)S(1)}, u32[]{:S(2)}, u32[]{:S(2)}) collective-permute-start(f32[16,128]{1,0:T(8,128)S(1)} %constant_dynamic-update-slice_fusion.refs_0_), channel_id=1, source_target_pairs={{0,3},{1,2},{2,1},{3,0},{4,7},{5,6},{6,5},{7,4},{8,11},{9,10},{10,... | collective-permute-start | bytes 24584 | tf_op jit(solution)/shard_map/ppermute | solution.py:384
  75.8 10.8 %copy-start.3 = (bf16[1,128,4096]{2,1,0:T(8,128)(2,1)S(1)}, bf16[1,128,4096]{2,1,0:T(8,128)(2,1)}, u32[]{:S(2)}) copy-start(bf16[1,128,4096]{2,1,0:T(8,128)(2,1)} %param.8) | copy-start | bytes 3145732
  75.8 10.8 %copy-start.5 = (bf16[1,128,4096]{2,1,0:T(8,128)(2,1)S(1)}, bf16[1,128,4096]{2,1,0:T(8,128)(2,1)}, u32[]{:S(2)}) copy-start(bf16[1,128,4096]{2,1,0:T(8,128)(2,1)} %param.10) | copy-start | bytes 3145732
  75.8 22.9 %collective-permute-start.21 = (bf16[64,2048]{1,0:T(8,128)(2,1)S(1)}, bf16[64,2048]{1,0:T(8,128)(2,1)S(1)}, u32[]{:S(2)}, u32[]{:S(2)}) collective-permute-start(bf16[64,2048]{1,0:T(8,128)(2,1)S(1)} %get-tuple-element.49), channel_id=1, source_target_pairs={{0,8},{4,12},{8,0},{12,4},{16,24},{20,28},{24,16},{28,20},{1,9},{5... | collective-permute-start | bytes 786440 | tf_op jit(solution)/shard_map/ppermute | solution.py:387
  78.7 5.8 %collective-permute-start.25 = (bf16[128,512]{1,0:T(8,128)(2,1)S(1)}, bf16[128,512]{1,0:T(8,128)(2,1)S(1)}, u32[]{:S(2)}, u32[]{:S(2)}) collective-permute-start(bf16[128,512]{1,0:T(8,128)(2,1)S(1)} %project.1.rest_0_), channel_id=1, source_target_pairs={{0,1},{1,0},{2,3},{3,2},{4,5},{5,4},{6,7},{7,6},{8,9},{9,8},{10,11... | collective-permute-start | bytes 393224 | tf_op jit(solution)/shard_map/ppermute | solution.py:384
  80.1 5.0 %collective-permute-start.26 = (bf16[128,512]{1,0:T(8,128)(2,1)S(1)}, bf16[128,512]{1,0:T(8,128)(2,1)S(1)}, u32[]{:S(2)}, u32[]{:S(2)}) collective-permute-start(bf16[128,512]{1,0:T(8,128)(2,1)S(1)} %project.1.rest_0_), channel_id=1, source_target_pairs={{0,2},{1,3},{2,0},{3,1},{4,6},{5,7},{6,4},{7,5},{8,10},{9,11},{10,... | collective-permute-start | bytes 393224 | tf_op jit(solution)/shard_map/ppermute | solution.py:384
  80.7 5.9 %collective-permute-start.27 = (bf16[128,512]{1,0:T(8,128)(2,1)S(1)}, bf16[128,512]{1,0:T(8,128)(2,1)S(1)}, u32[]{:S(2)}, u32[]{:S(2)}) collective-permute-start(bf16[128,512]{1,0:T(8,128)(2,1)S(1)} %project.1.rest_0_), channel_id=1, source_target_pairs={{0,3},{1,2},{2,1},{3,0},{4,7},{5,6},{6,5},{7,4},{8,11},{9,10},{10,... | collective-permute-start | bytes 393224 | tf_op jit(solution)/shard_map/ppermute | solution.py:384
  91.7 9.3 %collective-permute-start.28 = (bf16[128,512]{1,0:T(8,128)(2,1)S(1)}, bf16[128,512]{1,0:T(8,128)(2,1)S(1)}, u32[]{:S(2)}, u32[]{:S(2)}) collective-permute-start(bf16[128,512]{1,0:T(8,128)(2,1)S(1)} %get-tuple-element.56), channel_id=1, source_target_pairs={{0,1},{1,0},{2,3},{3,2},{4,5},{5,4},{6,7},{7,6},{8,9},{9,8},{10,11... | collective-permute-start | bytes 393224 | tf_op jit(solution)/shard_map/ppermute | solution.py:384
  93.5 15.2 %collective-permute-start.22 = (bf16[64,2048]{1,0:T(8,128)(2,1)S(1)}, bf16[64,2048]{1,0:T(8,128)(2,1)S(1)}, u32[]{:S(2)}, u32[]{:S(2)}) collective-permute-start(bf16[64,2048]{1,0:T(8,128)(2,1)S(1)} %get-tuple-element.51), channel_id=1, source_target_pairs={{0,16},{4,20},{24,8},{28,12},{1,17},{5,21},{25,9},{29,13},{2,18},{... | collective-permute-start | bytes 786440 | tf_op jit(solution)/shard_map/ppermute | solution.py:387
  98.0 10.7 %collective-permute-start.23 = (bf16[64,2048]{1,0:T(8,128)(2,1)S(1)}, bf16[64,2048]{1,0:T(8,128)(2,1)S(1)}, u32[]{:S(2)}, u32[]{:S(2)}) collective-permute-start(bf16[64,2048]{1,0:T(8,128)(2,1)S(1)} %get-tuple-element.51), channel_id=1, source_target_pairs={{8,16},{12,20},{16,8},{20,12},{9,17},{13,21},{17,9},{21,13},{10,18... | collective-permute-start | bytes 786440 | tf_op jit(solution)/shard_map/ppermute | solution.py:387
  99.3 13.2 %collective-permute-start.24 = (bf16[64,2048]{1,0:T(8,128)(2,1)S(1)}, bf16[64,2048]{1,0:T(8,128)(2,1)S(1)}, u32[]{:S(2)}, u32[]{:S(2)}) collective-permute-start(bf16[64,2048]{1,0:T(8,128)(2,1)S(1)} %relay.1), channel_id=1, source_target_pairs={{0,8},{4,12},{24,16},{28,20},{8,24},{12,28},{16,0},{20,4},{1,9},{5... | collective-permute-start | bytes 786440 | tf_op jit(solution)/shard_map/ppermute | solution.py:387
  100.5 5.0 %collective-permute-start.29 = (bf16[128,512]{1,0:T(8,128)(2,1)S(1)}, bf16[128,512]{1,0:T(8,128)(2,1)S(1)}, u32[]{:S(2)}, u32[]{:S(2)}) collective-permute-start(bf16[128,512]{1,0:T(8,128)(2,1)S(1)} %get-tuple-element.57), channel_id=1, source_target_pairs={{0,2},{1,3},{2,0},{3,1},{4,6},{5,7},{6,4},{7,5},{8,10},{9,11},{10,... | collective-permute-start | bytes 393224 | tf_op jit(solution)/shard_map/ppermute | solution.py:384
  101.0 5.9 %collective-permute-start.30 = (bf16[128,512]{1,0:T(8,128)(2,1)S(1)}, bf16[128,512]{1,0:T(8,128)(2,1)S(1)}, u32[]{:S(2)}, u32[]{:S(2)}) collective-permute-start(bf16[128,512]{1,0:T(8,128)(2,1)S(1)} %get-tuple-element.58), channel_id=1, source_target_pairs={{0,3},{1,2},{2,1},{3,0},{4,7},{5,6},{6,5},{7,4},{8,11},{9,10},{10,... | collective-permute-start | bytes 393224 | tf_op jit(solution)/shard_map/ppermute | solution.py:384
where the time goes:
time: 114 us
  waiting for transfers between devices  47.1 us (41%)
  starting transfers between devices  39.4 us (35%)
  Pallas kernels  20.2 us (18%)
  local copies, waits for them, and re-layouts  5.92 us (5%)
  between operations  1.44 us (1%)
    ppermute x24, waiting for transfers between devices, over_context(): return lax.ppermute(x, 'context', [(i, i ^ k) for i in range(parts)])  42 us
    ppermute x24, starting transfers between devices, over_context(): return lax.ppermute(x, 'context', [(i, i ^ k) for i in range(parts)])  30.7 us
    ppermute x4, starting transfers between devices, over_planes(): lax.ppermute(x, 'dp', [(2 * a + c, 2 * b + c) for a, b in hops for c in r...  8.03 us
    pallas_call x1, Pallas kernels, weigh(): pl.pallas_call(kernel, out_shape=[jax.ShapeDtypeStruct((groups, total, he...  5.85 us
    unnamed x19, local copies, waits for them, and re-layouts  5.32 us
    pallas_call x1, Pallas kernels, key_side(): pl.pallas_call(kernel, out_shape=[jax.ShapeDtypeStruct((rows, kv_width),...  5.14 us
    ppermute x4, waiting for transfers between devices, over_planes(): lax.ppermute(x, 'dp', [(2 * a + c, 2 * b + c) for a, b in hops for c in r...  3.86 us
    pallas_call x2, Pallas kernels, add_up(): pl.pallas_call(kernel, out_shape=jax.ShapeDtypeStruct(terms[0].shape, kin...  2.76 us
  transfers between devices with their start and end apart: 31, of which 17 were waited for; matrix products, arithmetic and copies ran while one was open for 1% of the time, Pallas kernels for 14%

commit v1 on v0

--- a/solution.py
+++ b/solution.py
@@ -9,7 +9,9 @@
 
 HD = 128
 LANES = 128
-FIRST_SHARE = 10
+TERMS = 8
+EARLY_SHARE = 6
+FIRST_SHARE = 8
 HEAVY = 10
 F32 = jnp.float32
 BF16 = jnp.bfloat16
@@ -57,6 +59,20 @@
         name="cut",
     )(place, layer_rows)
     return [[out[k * chunks + j] for j in range(chunks)] for k in range(parts)]
+
+
+def anchor():
+    def kernel(out_ref):
+        out_ref[...] = jnp.zeros((8, HD), F32)
+
+    return pl.pallas_call(
+        kernel,
+        out_shape=jax.ShapeDtypeStruct((8, HD), F32),
+        out_specs=VMEM,
+        compiler_params=grant(1),
+        cost_estimate=estimate(10**10, 0),
+        name="anchor",
+    )()
 
 
 def project(layer_rows, value_weight):
@@ -234,48 +250,140 @@
     )(*parts_list)
 
 
-def doc_grad(place, value_grads, features, before, blocks):
-    parts = len(features)
-    rows, chunk = features[0].shape
+def doc_grad(place, value_grads, features, spans, before, blocks, kind):
+    parts = len(value_grads)
+    rows = features[0][0].shape[0]
+    chunk = sum(size for _, size in spans)
     cols = value_grads[0].shape[0]
     width = cols // blocks
     half = blocks // 2
+    count = parts * len(spans)
 
     def kernel(place_ref, *refs):
-        x_refs, d_refs = refs[:parts], refs[parts : 2 * parts]
+        x_refs, d_refs = refs[:count], refs[count : count + parts]
         keep_ref, send_ref, square_ref = refs[-3:]
         odd = place_ref[2]
-        x = jnp.concatenate([r[...] for r in x_refs], axis=0)
-
-        def side(which):
-            picked = []
+
+        def picked(which):
+            blocks_of = []
             for z in range(half):
                 block = pl.ds(pl.multiple_of((2 * z + which) * width, width), width)
-                picked.append(jnp.concatenate([r[block, :] for r in d_refs], axis=1))
-            return jnp.dot(jnp.concatenate(picked, axis=0), x, preferred_element_type=F32)
-
-        kept = side(odd)
-        sent = side(1 - odd)
-        keep_ref[...] = kept
-        send_ref[...] = sent.astype(BF16)
-        both = kept * kept + sent * sent
-        folded = jnp.sum(both.reshape(half * width // 8, 8, chunk), axis=0)
-        squares = sum(folded[:, i * HD : (i + 1) * HD] for i in range(chunk // HD))
-        square_ref[...] = squares + (refs[2 * parts][...] if before else 0.0)
-
+                blocks_of.append(jnp.concatenate([r[block, :] for r in d_refs], axis=1))
+            return jnp.concatenate(blocks_of, axis=0)
+
+        ours, theirs = picked(odd), picked(1 - odd)
+        squares = refs[count + parts][...]
+        at = 0
+        for i, (start, size) in enumerate(spans):
+            span = slice(start, start + size)
+            x = jnp.concatenate([r[:, span] for r in x_refs[i * parts : (i + 1) * parts]], axis=0)
+            kept = jnp.dot(ours, x, preferred_element_type=F32)
+            sent = jnp.dot(theirs, x, preferred_element_type=F32)
+            keep_ref[:, at : at + size] = kept.astype(kind)
+            send_ref[:, at : at + size] = sent.astype(BF16)
+            both = kept * kept + sent * sent
+            folded = jnp.sum(both.reshape(half * width // 8, 8, size), axis=0)
+            for j in range(size // HD):
+                squares = squares + folded[:, j * HD : (j + 1) * HD]
+            at += size
+        square_ref[...] = squares
+
+    inputs = [x for chunk_of in features for x in chunk_of]
     return pl.pallas_call(
         kernel,
         out_shape=[
-            jax.ShapeDtypeStruct((half * width, chunk), F32),
+            jax.ShapeDtypeStruct((half * width, chunk), kind),
             jax.ShapeDtypeStruct((half * width, chunk), BF16),
             jax.ShapeDtypeStruct((8, HD), F32),
         ],
-        in_specs=[SMEM] + [VMEM] * (2 * parts + len(before)),
+        in_specs=[SMEM] + [VMEM] * (count + parts + 1),
         out_specs=[VMEM] * 3,
-        compiler_params=grant(8),
+        compiler_params=grant(10),
         cost_estimate=estimate(2 * rows * parts * chunk * cols, 2 * rows * parts * (chunk + cols) + 3 * cols * chunk),
         name="doc_grad",
-    )(place, *features, *value_grads, *before)
+    )(place, *inputs, *value_grads, before)
+
+
+def pack(place, kept, received, blocks):
+    half = blocks // 2
+    tall, chunk = kept.shape
+    width = tall // half
+
+    def kernel(place_ref, keep_ref, got_ref, *outs):
+        for k in range(half):
+            rows = pl.ds(pl.multiple_of((place_ref[3] ^ k) * width, width), width)
+            outs[k][:width, :] = keep_ref[rows, :]
+            outs[k][width:, :] = got_ref[rows, :]
+
+    return pl.pallas_call(
+        kernel,
+        out_shape=[jax.ShapeDtypeStruct((2 * width, chunk), BF16)] * half,
+        in_specs=[SMEM, VMEM, VMEM],
+        out_specs=[VMEM] * half,
+        compiler_params=grant(8),
+        cost_estimate=estimate(0, 8 * tall * chunk),
+        name="pack",
+    )(place, kept, received)
+
+
+def finish(place, flag, own, plain, mine, first, others):
+    planes = len(plain)
+    width = plain[0].shape[0] // 2
+    chunk = plain[0].shape[1]
+    rest = mine.shape[1] - LANES
+
+    def kernel(place_ref, own_ref, *refs):
+        plain_refs, (mine_ref, *got_refs, out_ref) = refs[:planes], refs[planes:]
+        factors = [[own_ref[:1, :1], own_ref[8:9, :1]]]
+        sums = mine_ref[:, :rest].astype(F32)
+        if flag is None:
+            for r in got_refs:
+                factors.append(gather_terms(r[:TERMS, rest:]))
+                sums = sums + r[:, :rest].astype(F32)
+        else:
+            first_ref, far_ref, near_ref, last_ref = got_refs
+            inner = place_ref[flag] == 1
+            factors.append(gather_terms(first_ref[:TERMS, rest:]))
+            last = last_ref[: 2 * TERMS, rest:]
+            for ref, start in ((far_ref, 0), (near_ref, TERMS)):
+                direct = gather_terms(ref[:TERMS, rest:])
+                passed = gather_terms(last[start : start + TERMS])
+                factors.append([jnp.where(inner, d, p) for d, p in zip(direct, passed)])
+            for r in got_refs[1:]:
+                sums = sums + r[:, :rest].astype(F32)
+            got = first_ref[:, :rest].astype(F32)
+            sums = sums + jnp.where(inner, jnp.zeros_like(got), got)
+        out_ref[:, chunk:] = sums
+        total = 0.0
+        for (even, odd), r in zip(factors, plain_refs):
+            total = total + r[:width, :].astype(F32) * even + r[width:, :].astype(F32) * odd
+        out_ref[:, :chunk] = total
+
+    args = [own, *plain, mine, first, *others]
+    return pl.pallas_call(
+        kernel,
+        out_shape=jax.ShapeDtypeStruct((width, chunk + rest), F32),
+        in_specs=[SMEM] + [VMEM] * len(args),
+        out_specs=VMEM,
+        compiler_params=grant(8),
+        cost_estimate=estimate(12 * width * (chunk + rest), 20 * width * (chunk + rest)),
+        name="finish",
+    )(place, *args)
+
+
+def spread(value):
+    rest = jnp.broadcast_to(value, (1, LANES))
+    terms = []
+    for _ in range(3):
+        term = rest.astype(BF16)
+        rest = rest - term.astype(F32)
+        terms.append(term)
+    return terms + [jnp.zeros((1, LANES), BF16)]
+
+
+def gather_terms(block):
+    block = block.astype(F32)
+    return [block[i : i + 1, :1] + block[i + 1 : i + 2, :1] + block[i + 2 : i + 3, :1] for i in (0, 4)]
 
 
 def combine(place, squares, kept, received, order, blocks, clip):
@@ -291,7 +399,8 @@
         square_refs = refs[:count]
         keep_refs = refs[count : count + chunks]
         got_refs = refs[count + chunks : count + 2 * chunks]
-        norm_ref, outs = refs[count + 2 * chunks], refs[count + 2 * chunks + 1 :]
+        norm_ref, factor_ref = refs[count + 2 * chunks : count + 2 * chunks + 2]
+        outs = refs[count + 2 * chunks + 2 :]
         sums = square_refs[0][...]
         for r in square_refs[1:]:
             sums = sums + r[...]
@@ -303,7 +412,12 @@
         mine, other = norm(sums[:8]), norm(sums[8:])
         norm_ref[...] = jnp.broadcast_to(mine, (8, HD))
         mine, other = clip / (mine + 0.01), clip / (other + 0.01)
+        factor_ref[:8, :] = jnp.broadcast_to(mine, (8, HD))
+        factor_ref[8:, :] = jnp.broadcast_to(other, (8, HD))
+        terms = jnp.concatenate(spread(mine) + spread(other), axis=0)
         for i in range(half):
+            outs[i][:TERMS, whole:] = terms
+            outs[i][TERMS:, whole:] = jnp.zeros((width - TERMS, LANES), BF16)
             rows = pl.ds(pl.multiple_of(place_ref[order + i] * width, width), width)
             for j in range(chunks):
                 total = keep_refs[j][rows, :] * mine + got_refs[j][rows, :].astype(F32) * other
@@ -312,22 +426,26 @@
 
     out = pl.pallas_call(
         kernel,
-        out_shape=[jax.ShapeDtypeStruct((8, HD), F32)]
-        + [jax.ShapeDtypeStruct((width, whole), BF16)] * half,
+        out_shape=[jax.ShapeDtypeStruct((8, HD), F32), jax.ShapeDtypeStruct((16, HD), F32)]
+        + [jax.ShapeDtypeStruct((width, whole + LANES), BF16)] * half,
         in_specs=[SMEM] + [VMEM] * (count + 2 * chunks),
-        out_specs=[VMEM] * (half + 1),
+        out_specs=[VMEM] * (half + 2),
         compiler_params=grant(12),
         cost_estimate=estimate(4 * tall * whole, 8 * tall * whole),
         name="combine",
     )(place, *squares, *kept, *received)
-    return out[0], out[1:]
+    return out[0], out[1], out[2:]
 
 
 def relay(place, flag, mine, got):
+    whole = mine.shape[1] - LANES
+
     def kernel(place_ref, mine_ref, got_ref, out_ref):
-        got = got_ref[...].astype(F32)
+        got = got_ref[:, :whole].astype(F32)
         got = jnp.where(place_ref[flag] == 1, got, jnp.zeros_like(got))
-        out_ref[...] = (mine_ref[...].astype(F32) + got).astype(BF16)
+        out_ref[:, :whole] = (mine_ref[:, :whole].astype(F32) + got).astype(BF16)
+        out_ref[:, whole:] = mine_ref[:, whole:]
+        out_ref[TERMS : 2 * TERMS, whole:] = got_ref[:TERMS, whole:]
 
     return pl.pallas_call(
         kernel,
@@ -378,40 +496,56 @@
     place = jnp.stack([context, lengths[0], doc % 2, z, inner] + order).astype(jnp.int32)
     width = layer_input.shape[2]
     sizes = split(width // parts)
+    early = max(1, width // parts // LANES * EARLY_SHARE // 16) * LANES
+    spans = [(early, sizes[0] - early), (0, sizes[1])]
+    start = 0 if early < sizes[0] else 1
+    spans = spans[start:]
     cols = value_weight.shape[1]
 
     def over_context(x, k):
         return lax.ppermute(x, "context", [(i, i ^ k) for i in range(parts)])
 
+    def to_later(x, k):
+        return lax.ppermute(x, "context", [(i, i ^ k) for i in range(parts) ])
+
+    def to_earlier(x, k):
+        return lax.ppermute(x, "context", [(i, i ^ k) for i in range(parts) ])
+
     def over_planes(x, hops):
         return lax.ppermute(x, "dp", [(2 * a + c, 2 * b + c) for a, b in hops for c in range(2)])
 
+    def swap(k):
+        return [(i, i ^ k) for i in range(planes)]
+
     def over_cores(x):
         return lax.ppermute(x, "dp", [(i, i ^ 1) for i in range(docs)])
 
-    keys = [key_states[0]] + [over_context(key_states[0], k) for k in range(1, parts)]
+    zeros = anchor()
+    keys = [key_states[0]] + [to_later(key_states[0], k) for k in range(1, parts)]
     pieces = cut(place, layer_input[0], parts, sizes)
     features = []
     for j in range(len(sizes)):
         features.append([pieces[0][j]] + [over_context(pieces[k][j], k) for k in range(1, parts)])
     weights, value_parts = weigh(place, queries[0], out_grads[0], keys)
-    blocks = [value_parts[0]] + [over_context(value_parts[k], k) for k in range(1, parts)]
+    blocks = [value_parts[0]] + [to_earlier(value_parts[k], k) for k in range(1, parts)]
     value_low = settle(blocks)
     value_grads = [value_low] + [over_context(value_low, k) for k in range(1, parts)]
 
-    kept, received, square = [], [], []
-    for j in range(len(sizes)):
-        keep, send, *square = doc_grad(place, value_grads, features[j], square, docs)
-        kept.append(keep)
-        received.append(over_cores(send))
-    squares = jnp.concatenate([square[0], over_cores(square[0])], axis=0)
+    keep, send, square = doc_grad(place, value_grads, features[:1], [(0, early)], zeros, docs, BF16)
+    got = over_cores(send)
+    plain = pack(place, keep, got, docs)
+    plain = [plain[0]] + [over_planes(plain[k], swap(k)) for k in range(1, planes)]
+    keep, send, square = doc_grad(place, value_grads, features[start:], spans, square, docs, F32)
+    got = over_cores(send)
+    squares = jnp.concatenate([square, over_cores(square)], axis=0)
     squares = [squares] + [over_context(squares, k) for k in range(1, parts)]
-    norm, shares = combine(place, squares, kept, received, 5, docs, math.sqrt(width * cols))
+    norm, factors, shares = combine(place, squares, [keep], [got], 5, docs, math.sqrt(width * cols))
+
 
     own_values = project(layer_input[0], value_weight)
-    values = [own_values] + [over_context(own_values, k) for k in range(1, parts)]
+    values = [own_values] + [to_later(own_values, k) for k in range(1, parts)]
     key_parts = key_side(place, weights, queries[0], out_grads[0], values)
-    key_blocks = [key_parts[0]] + [over_context(key_parts[k], k) for k in range(1, parts)]
+    key_blocks = [key_parts[0]] + [to_earlier(key_parts[k], k) for k in range(1, parts)]
     key_grads = add_up(place, 4, [], key_blocks, BF16)[None]
 
     if planes == 4:
@@ -420,10 +554,10 @@
         near = over_planes(shares[2], [(1, 2), (2, 1)])
         onward = relay(place, 4, shares[3], first)
         last = over_planes(onward, [(0, 1), (3, 2), (1, 3), (2, 0)])
-        total = add_up(place, 4, [first], [shares[0], far, near, last], F32)
+        total = finish(place, 4, factors, plain, shares[0], first, [far, near, last])
     else:
-        got = [over_planes(shares[k], [(i, i ^ k) for i in range(planes)]) for k in range(1, planes)]
-        total = add_up(place, 4, [], [shares[0]] + got, F32)
+        got = [over_planes(shares[k], swap(k)) for k in range(1, planes)]
+        total = finish(place, None, factors, plain, shares[0], got[0], got[1:])
     return total.T, norm[0, :1], key_grads
 
 

time: 114 us -> 119 us (1.044)
  waiting for transfers between devices: 47.1 us -> 51.6 us
  local copies, waits for them, and re-layouts: 5.92 us -> 3.97 us
  starting transfers between devices: 39.4 us -> 41.1 us
    ppermute x24 -> x12, waiting for transfers between devices: 42 us -> 16.4 us  [over_context(): return lax.ppermute(x, 'context', [(i, i ^ k) for i in range(parts)])]
    ppermute x24 -> x12, starting transfers between devices: 30.7 us -> 13.4 us  [over_context(): return lax.ppermute(x, 'context', [(i, i ^ k) for i in range(parts)])]
    ppermute x0 -> x12, waiting for transfers between devices: none -> 16.6 us  [the longest x6 10.9 us: to_earlier(): return lax.ppermute(x, 'context', [(i, i ^ k) for i in range(parts)])]
    ppermute x0 -> x12, starting transfers between devices: none -> 15.5 us  [the longest x6 8.13 us: to_later(): return lax.ppermute(x, 'context', [(i, i ^ k) for i in range(parts)])]
    ppermute x4 -> x7, waiting for transfers between devices: 3.86 us -> 17.1 us  [over_planes(): lax.ppermute(x, 'dp', [(2 * a + c, 2 * b + c) for a, b in hops for c in r...]
    ppermute x4 -> x7, starting transfers between devices: 8.03 us -> 11.5 us  [over_planes(): lax.ppermute(x, 'dp', [(2 * a + c, 2 * b + c) for a, b in hops for c in r...]
    pallas_call x1 -> x4, Pallas kernels: 1.18 us -> 3.29 us  [the longest x1 1.74 us: finish(): pl.pallas_call(kernel, out_shape=jax.ShapeDtypeStruct((width, chunk + res...]
    unnamed x19 -> x17, local copies, waits for them, and re-layouts: 5.32 us -> 3.37 us
  transfers between devices with their start and end apart: 31 -> 34, of which waited for: 17 -> 14; matrix products, arithmetic and copies ran while one was open for 1% -> 1% of each run, Pallas kernels for 14% -> 10%
where the time goes in v1:
time: 119 us
  waiting for transfers between devices  51.6 us (43%)
  starting transfers between devices  41.1 us (35%)
  Pallas kernels  21 us (18%)
  local copies, waits for them, and re-layouts  3.97 us (3%)
  between operations  1.48 us (1%)
    ppermute x7, waiting for transfers between devices, over_planes(): lax.ppermute(x, 'dp', [(2 * a + c, 2 * b + c) for a, b in hops for c in r...  17.1 us
    ppermute x12, waiting for transfers between devices, over_context(): return lax.ppermute(x, 'context', [(i, i ^ k) for i in range(parts)])  16.4 us
    ppermute x12, starting transfers between devices, over_context(): return lax.ppermute(x, 'context', [(i, i ^ k) for i in range(parts)])  13.4 us
    ppermute x7, starting transfers between devices, over_planes(): lax.ppermute(x, 'dp', [(2 * a + c, 2 * b + c) for a, b in hops for c in r...  11.5 us
    ppermute x6, waiting for transfers between devices, to_earlier(): return lax.ppermute(x, 'context', [(i, i ^ k) for i in range(parts)])  10.9 us
    ppermute x6, starting transfers between devices, to_later(): return lax.ppermute(x, 'context', [(i, i ^ k) for i in range(parts)])  8.13 us
    ppermute x6, starting transfers between devices, to_earlier(): return lax.ppermute(x, 'context', [(i, i ^ k) for i in range(parts)])  7.42 us
    pallas_call x1, Pallas kernels, weigh(): pl.pallas_call(kernel, out_shape=[jax.ShapeDtypeStruct((groups, total, he...  5.85 us
  transfers between devices with their start and end apart: 34, of which 14 were waited for; matrix products, arithmetic and copies ran while one was open for 1% of the time, Pallas kernels for 10%

profile of v1, /device:TPU:0, one launch (start us, length us, event | category | flops | bytes accessed | tf_op | source)
XLA Modules:
  0.0 119.1 jit_solution(6487567595363857001)
XLA Ops:
  0.6 3.0 %collective-permute-start.6 = (bf16[128,512]{1,0:T(8,128)(2,1)}, bf16[128,512]{1,0:T(8,128)(2,1)S(1)}, u32[]{:S(2)}, u32[]{:S(2)}) collective-permute-start(bf16[128,512]{1,0:T(8,128)(2,1)} %bitcast.22), channel_id=1, source_target_pairs={{0,1},{1,0},{2,3},{3,2},{4,5},{5,4},{6,7},{7,6},{8,9},{9,8},{10,11... | collective-permute-start | bytes 393224 | tf_op jit(solution)/shard_map/ppermute | solution.py:509
  3.7 1.5 %collective-permute-start.7 = (bf16[128,512]{1,0:T(8,128)(2,1)}, bf16[128,512]{1,0:T(8,128)(2,1)S(1)}, u32[]{:S(2)}, u32[]{:S(2)}) collective-permute-start(bf16[128,512]{1,0:T(8,128)(2,1)} %bitcast.23), channel_id=1, source_target_pairs={{0,2},{1,3},{2,0},{3,1},{4,6},{5,7},{6,4},{7,5},{8,10},{9,11},{10,... | collective-permute-start | bytes 393224 | tf_op jit(solution)/shard_map/ppermute | solution.py:509
  5.9 0.1 stack.36.place_ref
  5.9 1.9 %collective-permute-done.6.rest_1_ = bf16[128,512]{1,0:T(8,128)(2,1)S(1)} collective-permute-done((bf16[128,512]{1,0:T(8,128)(2,1)}, bf16[128,512]{1,0:T(8,128)(2,1)S(1)}, u32[]{:S(2)}, u32[]{:S(2)}) %collective-permute-start.6) | collective-permute-done | bytes 131104 | tf_op jit(solution)/shard_map/ppermute | solution.py:509
  7.9 3.8 %collective-permute-done.7.rest_2_ = bf16[128,512]{1,0:T(8,128)(2,1)S(1)} collective-permute-done((bf16[128,512]{1,0:T(8,128)(2,1)}, bf16[128,512]{1,0:T(8,128)(2,1)S(1)}, u32[]{:S(2)}, u32[]{:S(2)}) %collective-permute-start.7) | collective-permute-done | bytes 131104 | tf_op jit(solution)/shard_map/ppermute | solution.py:509
  11.7 1.2 %copy-done.1 = bf16[1,128,4096]{2,1,0:T(8,128)(2,1)S(1)} copy-done((bf16[1,128,4096]{2,1,0:T(8,128)(2,1)S(1)}, bf16[1,128,4096]{2,1,0:T(8,128)(2,1)}, u32[]{:S(2)}) %copy-start.1) | copy-done | bytes 1048600
  12.9 1.2 %copy-done.3 = bf16[1,128,4096]{2,1,0:T(8,128)(2,1)S(1)} copy-done((bf16[1,128,4096]{2,1,0:T(8,128)(2,1)S(1)}, bf16[1,128,4096]{2,1,0:T(8,128)(2,1)}, u32[]{:S(2)}) %copy-start.3) | copy-done | bytes 1048600
  14.1 0.9 copy-done.5
  15.0 5.9 %weigh.1 = (bf16[4,512,1024]{2,1,0:T(8,128)(2,1)S(1)}, f32[128,512]{1,0:T(8,128)S(1)}, bf16[128,512]{1,0:T(8,128)(2,1)S(1)}, bf16[128,512]{1,0:T(8,128)(2,1)S(1)}, bf16[128,512]{1,0:T(8,128)(2,1)S(1)}) custom-call(s32[9]{0:T(128)S(1)} %stack.36.place_ref, bf16[128,4096]{1,0:T(8,128)(2,1)S(1)} %bitcast.18, bf16[128,4096]{1,0:T(8,128)(2,1)S(1)} %bitcast.20, ...), custom_call_target="tpu_custom_call" | custom-call | flops 10737418240 | bytes 3145728 | tf_op jit(solution)/shard_map/weigh/pallas_call | solution.py:164
  20.9 1.6 %collective-permute-start.10 = (bf16[128,512]{1,0:T(8,128)(2,1)S(1)}, bf16[128,512]{1,0:T(8,128)(2,1)S(1)}, u32[]{:S(2)}, u32[]{:S(2)}) collective-permute-start(bf16[128,512]{1,0:T(8,128)(2,1)S(1)} %get-tuple-element.46), channel_id=1, source_target_pairs={{0,2},{1,3},{2,0},{3,1},{4,6},{5,7},{6,4},{7,5},{8,10},{9,11},{10,... | collective-permute-start | bytes 393224 | tf_op jit(solution)/shard_map/ppermute | solution.py:512
  22.4 0.7 cut.1
  23.1 0.6 collective-permute-start
  23.7 1.2 %collective-permute-start.1 = (bf16[128,1024]{1,0:T(8,128)(2,1)S(1)}, bf16[128,1024]{1,0:T(8,128)(2,1)S(1)}, u32[]{:S(2)}, u32[]{:S(2)}) collective-permute-start(bf16[128,1024]{1,0:T(8,128)(2,1)S(1)} %get-tuple-element.38), channel_id=1, source_target_pairs={{0,2},{1,3},{2,0},{3,1},{4,6},{5,7},{6,4},{7,5},{8,10},{9,11},{10,... | collective-permute-start | bytes 786440 | tf_op jit(solution)/shard_map/ppermute | solution.py:506
  24.9 1.8 %collective-permute-start.11 = (bf16[128,512]{1,0:T(8,128)(2,1)S(1)}, bf16[128,512]{1,0:T(8,128)(2,1)S(1)}, u32[]{:S(2)}, u32[]{:S(2)}) collective-permute-start(bf16[128,512]{1,0:T(8,128)(2,1)S(1)} %get-tuple-element.47), channel_id=1, source_target_pairs={{0,3},{1,2},{2,1},{3,0},{4,7},{5,6},{6,5},{7,4},{8,11},{9,10},{10,... | collective-permute-start | bytes 393224 | tf_op jit(solution)/shard_map/ppermute | solution.py:512
  26.7 0.5 collective-permute-start.9
  27.2 0.3 collective-permute-done.10.refs_2_
  27.5 1.4 %collective-permute-start.2 = (bf16[128,1024]{1,0:T(8,128)(2,1)S(1)}, bf16[128,1024]{1,0:T(8,128)(2,1)S(1)}, u32[]{:S(2)}, u32[]{:S(2)}) collective-permute-start(bf16[128,1024]{1,0:T(8,128)(2,1)S(1)} %get-tuple-element.39), channel_id=1, source_target_pairs={{0,3},{1,2},{2,1},{3,0},{4,7},{5,6},{6,5},{7,4},{8,11},{9,10},{10,... | collective-permute-start | bytes 786440 | tf_op jit(solution)/shard_map/ppermute | solution.py:506
  28.9 6.3 %collective-permute-done.11.refs_3_ = bf16[128,512]{1,0:T(8,128)(2,1)S(1)} collective-permute-done((bf16[128,512]{1,0:T(8,128)(2,1)S(1)}, bf16[128,512]{1,0:T(8,128)(2,1)S(1)}, u32[]{:S(2)}, u32[]{:S(2)}) %collective-permute-start.11) | collective-permute-done | bytes 131104 | tf_op jit(solution)/shard_map/ppermute | solution.py:512
  35.2 2.8 %collective-permute-done.9.refs_1_ = bf16[128,512]{1,0:T(8,128)(2,1)S(1)} collective-permute-done((bf16[128,512]{1,0:T(8,128)(2,1)S(1)}, bf16[128,512]{1,0:T(8,128)(2,1)S(1)}, u32[]{:S(2)}, u32[]{:S(2)}) %collective-permute-start.9) | collective-permute-done | bytes 131104 | tf_op jit(solution)/shard_map/ppermute | solution.py:512
  38.0 0.1 settle.1.refs_4_.refs_8_
  38.2 0.6 collective-permute-start.12
  38.8 1.5 %collective-permute-start.3 = (bf16[128,1024]{1,0:T(8,128)(2,1)S(1)}, bf16[128,1024]{1,0:T(8,128)(2,1)S(1)}, u32[]{:S(2)}, u32[]{:S(2)}) collective-permute-start(bf16[128,1024]{1,0:T(8,128)(2,1)S(1)} %get-tuple-element.41), channel_id=1, source_target_pairs={{0,1},{1,0},{2,3},{3,2},{4,5},{5,4},{6,7},{7,6},{8,9},{9,8},{10,11... | collective-permute-start | bytes 786440 | tf_op jit(solution)/shard_map/ppermute | solution.py:506
  40.3 0.5 collective-permute-start.4
  40.8 1.5 %collective-permute-start.5 = (bf16[128,1024]{1,0:T(8,128)(2,1)S(1)}, bf16[128,1024]{1,0:T(8,128)(2,1)S(1)}, u32[]{:S(2)}, u32[]{:S(2)}) collective-permute-start(bf16[128,1024]{1,0:T(8,128)(2,1)S(1)} %get-tuple-element.43), channel_id=1, source_target_pairs={{0,3},{1,2},{2,1},{3,0},{4,7},{5,6},{6,5},{7,4},{8,11},{9,10},{10,... | collective-permute-start | bytes 786440 | tf_op jit(solution)/shard_map/ppermute | solution.py:506
  42.3 1.3 %collective-permute-done.2.refs_3_ = bf16[128,1024]{1,0:T(8,128)(2,1)S(1)} collective-permute-done((bf16[128,1024]{1,0:T(8,128)(2,1)S(1)}, bf16[128,1024]{1,0:T(8,128)(2,1)S(1)}, u32[]{:S(2)}, u32[]{:S(2)}) %collective-permute-start.2) | collective-permute-done | bytes 262176 | tf_op jit(solution)/shard_map/ppermute | solution.py:506
  43.6 1.5 %collective-permute-start.13 = (bf16[512,128]{1,0:T(8,128)(2,1)S(1)}, bf16[512,128]{1,0:T(8,128)(2,1)S(1)}, u32[]{:S(2)}, u32[]{:S(2)}) collective-permute-start(bf16[512,128]{1,0:T(8,128)(2,1)S(1)} %settle.1.refs_4_.refs_8_), channel_id=1, source_target_pairs={{0,2},{1,3},{2,0},{3,1},{4,6},{5,7},{6,4},{7,5},{8,10},{9,11},{10,... | collective-permute-start | bytes 393224 | tf_op jit(solution)/shard_map/ppermute | solution.py:506
  45.1 1.3 %collective-permute-done.12.refs_5_.refs_9_ = bf16[512,128]{1,0:T(8,128)(2,1)S(1)} collective-permute-done((bf16[512,128]{1,0:T(8,128)(2,1)S(1)}, bf16[512,128]{1,0:T(8,128)(2,1)S(1)}, u32[]{:S(2)}, u32[]{:S(2)}) %collective-permute-start.12) | collective-permute-done | bytes 131104 | tf_op jit(solution)/shard_map/ppermute | solution.py:506
  46.5 1.1 collective-permute-start.14
  47.6 4.0 %collective-permute-done.13.refs_6_.refs_10_ = bf16[512,128]{1,0:T(8,128)(2,1)S(1)} collective-permute-done((bf16[512,128]{1,0:T(8,128)(2,1)S(1)}, bf16[512,128]{1,0:T(8,128)(2,1)S(1)}, u32[]{:S(2)}, u32[]{:S(2)}) %collective-permute-start.13) | collective-permute-done | bytes 131104 | tf_op jit(solution)/shard_map/ppermute | solution.py:506
  51.6 6.2 %collective-permute-done.14.refs_7_.refs_11_ = bf16[512,128]{1,0:T(8,128)(2,1)S(1)} collective-permute-done((bf16[512,128]{1,0:T(8,128)(2,1)S(1)}, bf16[512,128]{1,0:T(8,128)(2,1)S(1)}, u32[]{:S(2)}, u32[]{:S(2)}) %collective-permute-start.14) | collective-permute-done | bytes 131104 | tf_op jit(solution)/shard_map/ppermute | solution.py:506
  57.9 1.1 doc_grad.2
  59.0 1.4 %doc_grad.3 = (f32[256,1280]{1,0:T(8,128)S(1)}, bf16[256,1280]{1,0:T(8,128)(2,1)S(1)}, f32[8,128]{1,0:T(8,128)S(1)}) custom-call(s32[9]{0:T(128)S(1)} %stack.36.place_ref, bf16[128,1024]{1,0:T(8,128)(2,1)S(1)} %get-tuple-element.36.refs_0_, bf16[128,1024]{1,0:T(8,128)(2,1)S(1)} %collective-permute-done.refs_1_, ...), custom_call_target="tpu_custom_call" | custom-call | flops 671088640 | bytes 3801088 | tf_op jit(solution)/shard_map/doc_grad/pallas_call | solution.py:292
  60.4 0.1 collective-permute-start.19
  60.5 0.5 collective-permute-start.15
  61.0 0.1 collective-permute-start.20
  61.1 1.5 %collective-permute-done.15 = f32[8,128]{1,0:T(8,128)S(1)} collective-permute-done((f32[8,128]{1,0:T(8,128)S(1)}, f32[8,128]{1,0:T(8,128)S(1)}, u32[]{:S(2)}, u32[]{:S(2)}) %collective-permute-start.15) | collective-permute-done | bytes 4128 | tf_op jit(solution)/shard_map/ppermute | solution.py:521
  62.6 1.5 %collective-permute-start.16 = (f32[16,128]{1,0:T(8,128)S(1)}, f32[16,128]{1,0:T(8,128)S(1)}, u32[]{:S(2)}, u32[]{:S(2)}) collective-permute-start(f32[16,128]{1,0:T(8,128)S(1)} %constant_dynamic-update-slice_fusion.refs_0_), channel_id=1, source_target_pairs={{0,1},{1,0},{2,3},{3,2},{4,5},{5,4},{6,7},{7,6},{8,9},{9,8},{10,11... | collective-permute-start | bytes 24584 | tf_op jit(solution)/shard_map/ppermute | solution.py:506
  64.1 0.5 collective-permute-start.17
  64.7 1.2 %project.1.rest_0_ = bf16[128,512]{1,0:T(8,128)(2,1)S(1)} custom-call(bf16[128,8192]{1,0:T(8,128)(2,1)S(1)} %bitcast.17, bf16[8192,512]{1,0:T(8,128)(2,1)S(1)} %bitcast.15), custom_call_target="tpu_custom_call" | custom-call | flops 1073741824 | bytes 10485760 | tf_op jit(solution)/shard_map/project/pallas_call | solution.py:90
  66.0 1.7 %collective-permute-start.28 = (bf16[128,512]{1,0:T(8,128)(2,1)S(1)}, bf16[128,512]{1,0:T(8,128)(2,1)S(1)}, u32[]{:S(2)}, u32[]{:S(2)}) collective-permute-start(bf16[128,512]{1,0:T(8,128)(2,1)S(1)} %project.1.rest_0_), channel_id=1, source_target_pairs={{0,1},{1,0},{2,3},{3,2},{4,5},{5,4},{6,7},{7,6},{8,9},{9,8},{10,11... | collective-permute-start | bytes 393224 | tf_op jit(solution)/shard_map/ppermute | solution.py:509
  67.7 0.3 collective-permute-start.29
  68.0 1.5 %collective-permute-start.30 = (bf16[128,512]{1,0:T(8,128)(2,1)S(1)}, bf16[128,512]{1,0:T(8,128)(2,1)S(1)}, u32[]{:S(2)}, u32[]{:S(2)}) collective-permute-start(bf16[128,512]{1,0:T(8,128)(2,1)S(1)} %project.1.rest_0_), channel_id=1, source_target_pairs={{0,3},{1,2},{2,1},{3,0},{4,7},{5,6},{6,5},{7,4},{8,11},{9,10},{10,... | collective-permute-start | bytes 393224 | tf_op jit(solution)/shard_map/ppermute | solution.py:509
  69.5 1.4 %collective-permute-start.18 = (f32[16,128]{1,0:T(8,128)S(1)}, f32[16,128]{1,0:T(8,128)S(1)}, u32[]{:S(2)}, u32[]{:S(2)}) collective-permute-start(f32[16,128]{1,0:T(8,128)S(1)} %constant_dynamic-update-slice_fusion.refs_0_), channel_id=1, source_target_pairs={{0,3},{1,2},{2,1},{3,0},{4,7},{5,6},{6,5},{7,4},{8,11},{9,10},{10,... | collective-permute-start | bytes 24584 | tf_op jit(solution)/shard_map/ppermute | solution.py:506
  70.9 0.6 pack.1
  71.5 3.5 %collective-permute-done.18.refs_3_ = f32[16,128]{1,0:T(8,128)S(1)} collective-permute-done((f32[16,128]{1,0:T(8,128)S(1)}, f32[16,128]{1,0:T(8,128)S(1)}, u32[]{:S(2)}, u32[]{:S(2)}) %collective-permute-start.18) | collective-permute-done | bytes 8224 | tf_op jit(solution)/shard_map/ppermute | solution.py:506
  75.0 1.5 %collective-permute-start.21 = (bf16[128,768]{1,0:T(8,128)(2,1)S(1)}, bf16[128,768]{1,0:T(8,128)(2,1)S(1)}, u32[]{:S(2)}, u32[]{:S(2)}) collective-permute-start(bf16[128,768]{1,0:T(8,128)(2,1)S(1)} %get-tuple-element.56), channel_id=1, source_target_pairs={{0,8},{4,12},{8,0},{12,4},{16,24},{20,28},{24,16},{28,20},{1,9},{5... | collective-permute-start | bytes 589832 | tf_op jit(solution)/shard_map/ppermute | solution.py:515
  76.5 1.0 combine.1
  77.5 0.6 collective-permute-start.24
  78.1 5.4 %key_side.1 = (f32[128,512]{1,0:T(8,128)S(1)}, bf16[128,512]{1,0:T(8,128)(2,1)S(1)}, bf16[128,512]{1,0:T(8,128)(2,1)S(1)}, bf16[128,512]{1,0:T(8,128)(2,1)S(1)}) custom-call(s32[9]{0:T(128)S(1)} %stack.36.place_ref, bf16[4,512,1024]{2,1,0:T(8,128)(2,1)S(1)} %get-tuple-element.64.p_ref, bf16[128,4096]{1,0:T(8,128)(2,1)S(1)} %bitcast.19, ...), custom_call_target="tpu_custom_call" | custom-call | flops 1073741824 | bytes 3145728 | tf_op jit(solution)/shard_map/key_side/pallas_call | solution.py:220
  83.5 0.8 collective-permute-start.31
  84.3 1.5 %collective-permute-start.32 = (bf16[128,512]{1,0:T(8,128)(2,1)S(1)}, bf16[128,512]{1,0:T(8,128)(2,1)S(1)}, u32[]{:S(2)}, u32[]{:S(2)}) collective-permute-start(bf16[128,512]{1,0:T(8,128)(2,1)S(1)} %get-tuple-element.67), channel_id=1, source_target_pairs={{0,2},{1,3},{2,0},{3,1},{4,6},{5,7},{6,4},{7,5},{8,10},{9,11},{10,... | collective-permute-start | bytes 393224 | tf_op jit(solution)/shard_map/ppermute | solution.py:512
  85.8 1.3 %collective-permute-start.33 = (bf16[128,512]{1,0:T(8,128)(2,1)S(1)}, bf16[128,512]{1,0:T(8,128)(2,1)S(1)}, u32[]{:S(2)}, u32[]{:S(2)}) collective-permute-start(bf16[128,512]{1,0:T(8,128)(2,1)S(1)} %get-tuple-element.68), channel_id=1, source_target_pairs={{0,3},{1,2},{2,1},{3,0},{4,7},{5,6},{6,5},{7,4},{8,11},{9,10},{10,... | collective-permute-start | bytes 393224 | tf_op jit(solution)/shard_map/ppermute | solution.py:512
  87.0 1.5 %collective-permute-done.31.refs_1_ = bf16[128,512]{1,0:T(8,128)(2,1)S(1)} collective-permute-done((bf16[128,512]{1,0:T(8,128)(2,1)S(1)}, bf16[128,512]{1,0:T(8,128)(2,1)S(1)}, u32[]{:S(2)}, u32[]{:S(2)}) %collective-permute-start.31) | collective-permute-done | bytes 131104 | tf_op jit(solution)/shard_map/ppermute | solution.py:512
  88.5 2.5 %collective-permute-start.22 = (bf16[128,768]{1,0:T(8,128)(2,1)S(1)}, bf16[128,768]{1,0:T(8,128)(2,1)S(1)}, u32[]{:S(2)}, u32[]{:S(2)}) collective-permute-start(bf16[128,768]{1,0:T(8,128)(2,1)S(1)} %get-tuple-element.57), channel_id=1, source_target_pairs={{0,16},{4,20},{8,24},{12,28},{16,0},{20,4},{24,8},{28,12},{1,17},{... | collective-permute-start | bytes 589832 | tf_op jit(solution)/shard_map/ppermute | solution.py:515
  91.0 1.4 %collective-permute-start.23 = (bf16[128,768]{1,0:T(8,128)(2,1)S(1)}, bf16[128,768]{1,0:T(8,128)(2,1)S(1)}, u32[]{:S(2)}, u32[]{:S(2)}) collective-permute-start(bf16[128,768]{1,0:T(8,128)(2,1)S(1)} %get-tuple-element.58), channel_id=1, source_target_pairs={{0,24},{4,28},{8,16},{12,20},{16,8},{20,12},{24,0},{28,4},{1,25},{... | collective-permute-start | bytes 589832 | tf_op jit(solution)/shard_map/ppermute | solution.py:515
  92.4 0.6 relay.1
  93.0 3.6 %collective-permute-start.25 = (bf16[64,1408]{1,0:T(8,128)(2,1)S(1)}, bf16[64,1408]{1,0:T(8,128)(2,1)S(1)}, u32[]{:S(2)}, u32[]{:S(2)}) collective-permute-start(bf16[64,1408]{1,0:T(8,128)(2,1)S(1)} %get-tuple-element.61), channel_id=1, source_target_pairs={{0,16},{4,20},{24,8},{28,12},{1,17},{5,21},{25,9},{29,13},{2,18},{... | collective-permute-start | bytes 540680 | tf_op jit(solution)/shard_map/ppermute | solution.py:515
  96.6 0.7 collective-permute-start.26
  97.3 1.2 %collective-permute-start.27 = (bf16[64,1408]{1,0:T(8,128)(2,1)S(1)}, bf16[64,1408]{1,0:T(8,128)(2,1)S(1)}, u32[]{:S(2)}, u32[]{:S(2)}) collective-permute-start(bf16[64,1408]{1,0:T(8,128)(2,1)S(1)} %relay.1), channel_id=1, source_target_pairs={{0,8},{4,12},{24,16},{28,20},{8,24},{12,28},{16,0},{20,4},{1,9},{5... | collective-permute-start | bytes 540680 | tf_op jit(solution)/shard_map/ppermute | solution.py:515
  98.5 1.3 %add_up.1 = bf16[128,512]{1,0:T(8,128)(2,1)} custom-call(s32[9]{0:T(128)S(1)} %stack.36.place_ref, f32[128,512]{1,0:T(8,128)S(1)} %get-tuple-element.65.refs_0_, bf16[128,512]{1,0:T(8,128)(2,1)S(1)} %collective-permute-done.31.refs_1_, bf16[128,512]{1,0:T(8,128)(2,1)S(1)} %collective-permute-done.32.refs_2_, bf16[128,512]{1,0:T(8,128)(2,1)S(1)} %collective-permute-done.33.refs_3_), custom_call_target="tpu_custom_call" | custom-call | flops 524288 | bytes 917504 | tf_op jit(solution)/shard_map/add_up/pallas_call | solution.py:472
  99.8 0.5 slice.3
  100.3 6.3 %collective-permute-done.22.refs_2_ = bf16[128,768]{1,0:T(8,128)(2,1)S(1)} collective-permute-done((bf16[128,768]{1,0:T(8,128)(2,1)S(1)}, bf16[128,768]{1,0:T(8,128)(2,1)S(1)}, u32[]{:S(2)}, u32[]{:S(2)}) %collective-permute-start.22) | collective-permute-done | bytes 196640 | tf_op jit(solution)/shard_map/ppermute | solution.py:515
  106.6 10.8 %collective-permute-done.27.refs_8_ = bf16[64,1408]{1,0:T(8,128)(2,1)S(1)} collective-permute-done((bf16[64,1408]{1,0:T(8,128)(2,1)S(1)}, bf16[64,1408]{1,0:T(8,128)(2,1)S(1)}, u32[]{:S(2)}, u32[]{:S(2)}) %collective-permute-start.27) | collective-permute-done | bytes 180256 | tf_op jit(solution)/shard_map/ppermute | solution.py:515
  117.4 1.7 %finish.1 = f32[64,2048]{1,0:T(8,128)} custom-call(s32[9]{0:T(128)S(1)} %stack.36.place_ref, f32[16,128]{1,0:T(8,128)S(1)} %get-tuple-element.52.own_ref, bf16[128,768]{1,0:T(8,128)(2,1)S(1)} %get-tuple-element.55.refs_0_, bf16[128,768]{1,0:T(8,128)(2,1)S(1)} %collective-permute-done.21.refs_1_, bf16[128,768]{1,0:T(8,128)(2,1)S(1)} %collective-permute-done.22.refs_2_, ...), custom_call_target="tpu_custom_call" | custom-call | flops 1572864 | bytes 2621440 | tf_op jit(solution)/shard_map/finish/pallas_call | solution.py:363
  (38 shorter events, 0.1 us)
Async XLA Ops:
  0.6 7.2 %collective-permute-start.6 = (bf16[128,512]{1,0:T(8,128)(2,1)}, bf16[128,512]{1,0:T(8,128)(2,1)S(1)}, u32[]{:S(2)}, u32[]{:S(2)}) collective-permute-start(bf16[128,512]{1,0:T(8,128)(2,1)} %bitcast.22), channel_id=1, source_target_pairs={{0,1},{1,0},{2,3},{3,2},{4,5},{5,4},{6,7},{7,6},{8,9},{9,8},{10,11... | collective-permute-start | bytes 393224 | tf_op jit(solution)/shard_map/ppermute | solution.py:509
  3.7 8.0 %collective-permute-start.7 = (bf16[128,512]{1,0:T(8,128)(2,1)}, bf16[128,512]{1,0:T(8,128)(2,1)S(1)}, u32[]{:S(2)}, u32[]{:S(2)}) collective-permute-start(bf16[128,512]{1,0:T(8,128)(2,1)} %bitcast.23), channel_id=1, source_target_pairs={{0,2},{1,3},{2,0},{3,1},{4,6},{5,7},{6,4},{7,5},{8,10},{9,11},{10,... | collective-permute-start | bytes 393224 | tf_op jit(solution)/shard_map/ppermute | solution.py:509
  5.2 6.5 %collective-permute-start.8 = (bf16[128,512]{1,0:T(8,128)(2,1)}, bf16[128,512]{1,0:T(8,128)(2,1)S(1)}, u32[]{:S(2)}, u32[]{:S(2)}) collective-permute-start(bf16[128,512]{1,0:T(8,128)(2,1)} %bitcast.24), channel_id=1, source_target_pairs={{0,3},{1,2},{2,1},{3,0},{4,7},{5,6},{6,5},{7,4},{8,11},{9,10},{10,... | collective-permute-start | bytes 393224 | tf_op jit(solution)/shard_map/ppermute | solution.py:509
  11.7 1.2 %copy-start.1 = (bf16[1,128,4096]{2,1,0:T(8,128)(2,1)S(1)}, bf16[1,128,4096]{2,1,0:T(8,128)(2,1)}, u32[]{:S(2)}) copy-start(bf16[1,128,4096]{2,1,0:T(8,128)(2,1)} %param.8) | copy-start | bytes 3145732
  12.9 1.2 %copy-start.3 = (bf16[1,128,4096]{2,1,0:T(8,128)(2,1)S(1)}, bf16[1,128,4096]{2,1,0:T(8,128)(2,1)}, u32[]{:S(2)}) copy-start(bf16[1,128,4096]{2,1,0:T(8,128)(2,1)} %param.10) | copy-start | bytes 3145732
  14.1 0.9 copy-start.5
  15.0 7.4 %copy-start = (bf16[1,128,8192]{2,1,0:T(8,128)(2,1)S(1)}, bf16[1,128,8192]{2,1,0:T(8,128)(2,1)}, u32[]{:S(2)}) copy-start(bf16[1,128,8192]{2,1,0:T(8,128)(2,1)} %param.6) | copy-start | bytes 6291460
  20.9 6.6 %collective-permute-start.10 = (bf16[128,512]{1,0:T(8,128)(2,1)S(1)}, bf16[128,512]{1,0:T(8,128)(2,1)S(1)}, u32[]{:S(2)}, u32[]{:S(2)}) collective-permute-start(bf16[128,512]{1,0:T(8,128)(2,1)S(1)} %get-tuple-element.46), channel_id=1, source_target_pairs={{0,2},{1,3},{2,0},{3,1},{4,6},{5,7},{6,4},{7,5},{8,10},{9,11},{10,... | collective-permute-start | bytes 393224 | tf_op jit(solution)/shard_map/ppermute | solution.py:512
  23.1 17.1 %collective-permute-start = (bf16[128,1024]{1,0:T(8,128)(2,1)S(1)}, bf16[128,1024]{1,0:T(8,128)(2,1)S(1)}, u32[]{:S(2)}, u32[]{:S(2)}) collective-permute-start(bf16[128,1024]{1,0:T(8,128)(2,1)S(1)} %get-tuple-element.37), channel_id=1, source_target_pairs={{0,1},{1,0},{2,3},{3,2},{4,5},{5,4},{6,7},{7,6},{8,9},{9,8},{10,11... | collective-permute-start | bytes 786440 | tf_op jit(solution)/shard_map/ppermute | solution.py:506
  23.7 17.1 %collective-permute-start.1 = (bf16[128,1024]{1,0:T(8,128)(2,1)S(1)}, bf16[128,1024]{1,0:T(8,128)(2,1)S(1)}, u32[]{:S(2)}, u32[]{:S(2)}) collective-permute-start(bf16[128,1024]{1,0:T(8,128)(2,1)S(1)} %get-tuple-element.38), channel_id=1, source_target_pairs={{0,2},{1,3},{2,0},{3,1},{4,6},{5,7},{6,4},{7,5},{8,10},{9,11},{10,... | collective-permute-start | bytes 786440 | tf_op jit(solution)/shard_map/ppermute | solution.py:506
  24.9 10.3 %collective-permute-start.11 = (bf16[128,512]{1,0:T(8,128)(2,1)S(1)}, bf16[128,512]{1,0:T(8,128)(2,1)S(1)}, u32[]{:S(2)}, u32[]{:S(2)}) collective-permute-start(bf16[128,512]{1,0:T(8,128)(2,1)S(1)} %get-tuple-element.47), channel_id=1, source_target_pairs={{0,3},{1,2},{2,1},{3,0},{4,7},{5,6},{6,5},{7,4},{8,11},{9,10},{10,... | collective-permute-start | bytes 393224 | tf_op jit(solution)/shard_map/ppermute | solution.py:512
  26.7 11.4 %collective-permute-start.9 = (bf16[128,512]{1,0:T(8,128)(2,1)S(1)}, bf16[128,512]{1,0:T(8,128)(2,1)S(1)}, u32[]{:S(2)}, u32[]{:S(2)}) collective-permute-start(bf16[128,512]{1,0:T(8,128)(2,1)S(1)} %get-tuple-element.45), channel_id=1, source_target_pairs={{0,1},{1,0},{2,3},{3,2},{4,5},{5,4},{6,7},{7,6},{8,9},{9,8},{10,11... | collective-permute-start | bytes 393224 | tf_op jit(solution)/shard_map/ppermute | solution.py:512
  27.5 16.1 %collective-permute-start.2 = (bf16[128,1024]{1,0:T(8,128)(2,1)S(1)}, bf16[128,1024]{1,0:T(8,128)(2,1)S(1)}, u32[]{:S(2)}, u32[]{:S(2)}) collective-permute-start(bf16[128,1024]{1,0:T(8,128)(2,1)S(1)} %get-tuple-element.39), channel_id=1, source_target_pairs={{0,3},{1,2},{2,1},{3,0},{4,7},{5,6},{6,5},{7,4},{8,11},{9,10},{10,... | collective-permute-start | bytes 786440 | tf_op jit(solution)/shard_map/ppermute | solution.py:506
  38.2 8.3 %collective-permute-start.12 = (bf16[512,128]{1,0:T(8,128)(2,1)S(1)}, bf16[512,128]{1,0:T(8,128)(2,1)S(1)}, u32[]{:S(2)}, u32[]{:S(2)}) collective-permute-start(bf16[512,128]{1,0:T(8,128)(2,1)S(1)} %settle.1.refs_4_.refs_8_), channel_id=1, source_target_pairs={{0,1},{1,0},{2,3},{3,2},{4,5},{5,4},{6,7},{7,6},{8,9},{9,8},{10,11... | collective-permute-start | bytes 393224 | tf_op jit(solution)/shard_map/ppermute | solution.py:506
  38.8 20.2 %collective-permute-start.3 = (bf16[128,1024]{1,0:T(8,128)(2,1)S(1)}, bf16[128,1024]{1,0:T(8,128)(2,1)S(1)}, u32[]{:S(2)}, u32[]{:S(2)}) collective-permute-start(bf16[128,1024]{1,0:T(8,128)(2,1)S(1)} %get-tuple-element.41), channel_id=1, source_target_pairs={{0,1},{1,0},{2,3},{3,2},{4,5},{5,4},{6,7},{7,6},{8,9},{9,8},{10,11... | collective-permute-start | bytes 786440 | tf_op jit(solution)/shard_map/ppermute | solution.py:506
  40.3 18.7 %collective-permute-start.4 = (bf16[128,1024]{1,0:T(8,128)(2,1)S(1)}, bf16[128,1024]{1,0:T(8,128)(2,1)S(1)}, u32[]{:S(2)}, u32[]{:S(2)}) collective-permute-start(bf16[128,1024]{1,0:T(8,128)(2,1)S(1)} %get-tuple-element.42), channel_id=1, source_target_pairs={{0,2},{1,3},{2,0},{3,1},{4,6},{5,7},{6,4},{7,5},{8,10},{9,11},{10,... | collective-permute-start | bytes 786440 | tf_op jit(solution)/shard_map/ppermute | solution.py:506
  40.8 23.9 %slice-start = ((s8[8388608]{0:T(1024)(128)(4,1)}), s8[4194304]{0:T(1024)(128)(4,1)S(1)}, s32[]{:S(2)}) async-start(s8[8388608]{0:T(1024)(128)(4,1)} %bitcast.14), calls=%async_computation | async-start | bytes 8388608
  40.8 23.9 %slice-start.1 = ((s8[8388608]{0:T(1024)(128)(4,1)}), s8[4194304]{0:T(1024)(128)(4,1)S(1)}, s32[]{:S(2)}) async-start(s8[8388608]{0:T(1024)(128)(4,1)} %bitcast.14), calls=%async_computation.1 | async-start | bytes 8388608
  40.8 18.2 %collective-permute-start.5 = (bf16[128,1024]{1,0:T(8,128)(2,1)S(1)}, bf16[128,1024]{1,0:T(8,128)(2,1)S(1)}, u32[]{:S(2)}, u32[]{:S(2)}) collective-permute-start(bf16[128,1024]{1,0:T(8,128)(2,1)S(1)} %get-tuple-element.43), channel_id=1, source_target_pairs={{0,3},{1,2},{2,1},{3,0},{4,7},{5,6},{6,5},{7,4},{8,11},{9,10},{10,... | collective-permute-start | bytes 786440 | tf_op jit(solution)/shard_map/ppermute | solution.py:506
  43.6 8.0 %collective-permute-start.13 = (bf16[512,128]{1,0:T(8,128)(2,1)S(1)}, bf16[512,128]{1,0:T(8,128)(2,1)S(1)}, u32[]{:S(2)}, u32[]{:S(2)}) collective-permute-start(bf16[512,128]{1,0:T(8,128)(2,1)S(1)} %settle.1.refs_4_.refs_8_), channel_id=1, source_target_pairs={{0,2},{1,3},{2,0},{3,1},{4,6},{5,7},{6,4},{7,5},{8,10},{9,11},{10,... | collective-permute-start | bytes 393224 | tf_op jit(solution)/shard_map/ppermute | solution.py:506
  46.5 11.4 %collective-permute-start.14 = (bf16[512,128]{1,0:T(8,128)(2,1)S(1)}, bf16[512,128]{1,0:T(8,128)(2,1)S(1)}, u32[]{:S(2)}, u32[]{:S(2)}) collective-permute-start(bf16[512,128]{1,0:T(8,128)(2,1)S(1)} %settle.1.refs_4_.refs_8_), channel_id=1, source_target_pairs={{0,3},{1,2},{2,1},{3,0},{4,7},{5,6},{6,5},{7,4},{8,11},{9,10},{10,... | collective-permute-start | bytes 393224 | tf_op jit(solution)/shard_map/ppermute | solution.py:506
  60.4 16.1 %collective-permute-start.19 = (bf16[256,1280]{1,0:T(8,128)(2,1)S(1)}, bf16[256,1280]{1,0:T(8,128)(2,1)S(1)}, u32[]{:S(2)}, u32[]{:S(2)}) collective-permute-start(bf16[256,1280]{1,0:T(8,128)(2,1)S(1)} %get-tuple-element.51), channel_id=1, source_target_pairs={{0,4},{4,0},{8,12},{12,8},{16,20},{20,16},{24,28},{28,24},{1,5},{5... | collective-permute-start | bytes 1966088 | tf_op jit(solution)/shard_map/ppermute | solution.py:521
  60.5 2.1 %collective-permute-start.15 = (f32[8,128]{1,0:T(8,128)S(1)}, f32[8,128]{1,0:T(8,128)S(1)}, u32[]{:S(2)}, u32[]{:S(2)}) collective-permute-start(f32[8,128]{1,0:T(8,128)S(1)} %get-tuple-element.49), channel_id=1, source_target_pairs={{0,4},{4,0},{8,12},{12,8},{16,20},{20,16},{24,28},{28,24},{1,5},{5... | collective-permute-start | bytes 12296 | tf_op jit(solution)/shard_map/ppermute | solution.py:521
  61.0 8.5 %collective-permute-start.20 = (bf16[256,768]{1,0:T(8,128)(2,1)S(1)}, bf16[256,768]{1,0:T(8,128)(2,1)S(1)}, u32[]{:S(2)}, u32[]{:S(2)}) collective-permute-start(bf16[256,768]{1,0:T(8,128)(2,1)S(1)} %get-tuple-element.54), channel_id=1, source_target_pairs={{0,4},{4,0},{8,12},{12,8},{16,20},{20,16},{24,28},{28,24},{1,5},{5... | collective-permute-start | bytes 1179656 | tf_op jit(solution)/shard_map/ppermute | solution.py:521
  62.6 15.5 %copy-start.2 = (bf16[1,128,4096]{2,1,0:T(8,128)(2,1)S(1)}, bf16[1,128,4096]{2,1,0:T(8,128)(2,1)}, u32[]{:S(2)}) copy-start(bf16[1,128,4096]{2,1,0:T(8,128)(2,1)} %param.8) | copy-start | bytes 3145732
  62.6 15.5 %copy-start.4 = (bf16[1,128,4096]{2,1,0:T(8,128)(2,1)S(1)}, bf16[1,128,4096]{2,1,0:T(8,128)(2,1)}, u32[]{:S(2)}) copy-start(bf16[1,128,4096]{2,1,0:T(8,128)(2,1)} %param.10) | copy-start | bytes 3145732
  62.6 5.1 %collective-permute-start.16 = (f32[16,128]{1,0:T(8,128)S(1)}, f32[16,128]{1,0:T(8,128)S(1)}, u32[]{:S(2)}, u32[]{:S(2)}) collective-permute-start(f32[16,128]{1,0:T(8,128)S(1)} %constant_dynamic-update-slice_fusion.refs_0_), channel_id=1, source_target_pairs={{0,1},{1,0},{2,3},{3,2},{4,5},{5,4},{6,7},{7,6},{8,9},{9,8},{10,11... | collective-permute-start | bytes 24584 | tf_op jit(solution)/shard_map/ppermute | solution.py:506
  64.1 3.9 %collective-permute-start.17 = (f32[16,128]{1,0:T(8,128)S(1)}, f32[16,128]{1,0:T(8,128)S(1)}, u32[]{:S(2)}, u32[]{:S(2)}) collective-permute-start(f32[16,128]{1,0:T(8,128)S(1)} %constant_dynamic-update-slice_fusion.refs_0_), channel_id=1, source_target_pairs={{0,2},{1,3},{2,0},{3,1},{4,6},{5,7},{6,4},{7,5},{8,10},{9,11},{10,... | collective-permute-start | bytes 24584 | tf_op jit(solution)/shard_map/ppermute | solution.py:506
  66.0 12.1 %collective-permute-start.28 = (bf16[128,512]{1,0:T(8,128)(2,1)S(1)}, bf16[128,512]{1,0:T(8,128)(2,1)S(1)}, u32[]{:S(2)}, u32[]{:S(2)}) collective-permute-start(bf16[128,512]{1,0:T(8,128)(2,1)S(1)} %project.1.rest_0_), channel_id=1, source_target_pairs={{0,1},{1,0},{2,3},{3,2},{4,5},{5,4},{6,7},{7,6},{8,9},{9,8},{10,11... | collective-permute-start | bytes 393224 | tf_op jit(solution)/shard_map/ppermute | solution.py:509
  67.7 10.4 %collective-permute-start.29 = (bf16[128,512]{1,0:T(8,128)(2,1)S(1)}, bf16[128,512]{1,0:T(8,128)(2,1)S(1)}, u32[]{:S(2)}, u32[]{:S(2)}) collective-permute-start(bf16[128,512]{1,0:T(8,128)(2,1)S(1)} %project.1.rest_0_), channel_id=1, source_target_pairs={{0,2},{1,3},{2,0},{3,1},{4,6},{5,7},{6,4},{7,5},{8,10},{9,11},{10,... | collective-permute-start | bytes 393224 | tf_op jit(solution)/shard_map/ppermute | solution.py:509
  68.0 10.1 %collective-permute-start.30 = (bf16[128,512]{1,0:T(8,128)(2,1)S(1)}, bf16[128,512]{1,0:T(8,128)(2,1)S(1)}, u32[]{:S(2)}, u32[]{:S(2)}) collective-permute-start(bf16[128,512]{1,0:T(8,128)(2,1)S(1)} %project.1.rest_0_), channel_id=1, source_target_pairs={{0,3},{1,2},{2,1},{3,0},{4,7},{5,6},{6,5},{7,4},{8,11},{9,10},{10,... | collective-permute-start | bytes 393224 | tf_op jit(solution)/shard_map/ppermute | solution.py:509
  69.5 5.5 %collective-permute-start.18 = (f32[16,128]{1,0:T(8,128)S(1)}, f32[16,128]{1,0:T(8,128)S(1)}, u32[]{:S(2)}, u32[]{:S(2)}) collective-permute-start(f32[16,128]{1,0:T(8,128)S(1)} %constant_dynamic-update-slice_fusion.refs_0_), channel_id=1, source_target_pairs={{0,3},{1,2},{2,1},{3,0},{4,7},{5,6},{6,5},{7,4},{8,11},{9,10},{10,... | collective-permute-start | bytes 24584 | tf_op jit(solution)/shard_map/ppermute | solution.py:506
  75.0 22.3 %collective-permute-start.21 = (bf16[128,768]{1,0:T(8,128)(2,1)S(1)}, bf16[128,768]{1,0:T(8,128)(2,1)S(1)}, u32[]{:S(2)}, u32[]{:S(2)}) collective-permute-start(bf16[128,768]{1,0:T(8,128)(2,1)S(1)} %get-tuple-element.56), channel_id=1, source_target_pairs={{0,8},{4,12},{8,0},{12,4},{16,24},{20,28},{24,16},{28,20},{1,9},{5... | collective-permute-start | bytes 589832 | tf_op jit(solution)/shard_map/ppermute | solution.py:515
  77.5 13.5 %collective-permute-start.24 = (bf16[64,1408]{1,0:T(8,128)(2,1)S(1)}, bf16[64,1408]{1,0:T(8,128)(2,1)S(1)}, u32[]{:S(2)}, u32[]{:S(2)}) collective-permute-start(bf16[64,1408]{1,0:T(8,128)(2,1)S(1)} %get-tuple-element.60), channel_id=1, source_target_pairs={{0,8},{4,12},{8,0},{12,4},{16,24},{20,28},{24,16},{28,20},{1,9},{5... | collective-permute-start | bytes 540680 | tf_op jit(solution)/shard_map/ppermute | solution.py:515
  83.5 5.0 %collective-permute-start.31 = (bf16[128,512]{1,0:T(8,128)(2,1)S(1)}, bf16[128,512]{1,0:T(8,128)(2,1)S(1)}, u32[]{:S(2)}, u32[]{:S(2)}) collective-permute-start(bf16[128,512]{1,0:T(8,128)(2,1)S(1)} %get-tuple-element.66), channel_id=1, source_target_pairs={{0,1},{1,0},{2,3},{3,2},{4,5},{5,4},{6,7},{7,6},{8,9},{9,8},{10,11... | collective-permute-start | bytes 393224 | tf_op jit(solution)/shard_map/ppermute | solution.py:512
  84.3 8.7 %collective-permute-start.32 = (bf16[128,512]{1,0:T(8,128)(2,1)S(1)}, bf16[128,512]{1,0:T(8,128)(2,1)S(1)}, u32[]{:S(2)}, u32[]{:S(2)}) collective-permute-start(bf16[128,512]{1,0:T(8,128)(2,1)S(1)} %get-tuple-element.67), channel_id=1, source_target_pairs={{0,2},{1,3},{2,0},{3,1},{4,6},{5,7},{6,4},{7,5},{8,10},{9,11},{10,... | collective-permute-start | bytes 393224 | tf_op jit(solution)/shard_map/ppermute | solution.py:512
  85.8 10.8 %collective-permute-start.33 = (bf16[128,512]{1,0:T(8,128)(2,1)S(1)}, bf16[128,512]{1,0:T(8,128)(2,1)S(1)}, u32[]{:S(2)}, u32[]{:S(2)}) collective-permute-start(bf16[128,512]{1,0:T(8,128)(2,1)S(1)} %get-tuple-element.68), channel_id=1, source_target_pairs={{0,3},{1,2},{2,1},{3,0},{4,7},{5,6},{6,5},{7,4},{8,11},{9,10},{10,... | collective-permute-start | bytes 393224 | tf_op jit(solution)/shard_map/ppermute | solution.py:512
  88.5 18.0 %collective-permute-start.22 = (bf16[128,768]{1,0:T(8,128)(2,1)S(1)}, bf16[128,768]{1,0:T(8,128)(2,1)S(1)}, u32[]{:S(2)}, u32[]{:S(2)}) collective-permute-start(bf16[128,768]{1,0:T(8,128)(2,1)S(1)} %get-tuple-element.57), channel_id=1, source_target_pairs={{0,16},{4,20},{8,24},{12,28},{16,0},{20,4},{24,8},{28,12},{1,17},{... | collective-permute-start | bytes 589832 | tf_op jit(solution)/shard_map/ppermute | solution.py:515
  91.0 15.5 %collective-permute-start.23 = (bf16[128,768]{1,0:T(8,128)(2,1)S(1)}, bf16[128,768]{1,0:T(8,128)(2,1)S(1)}, u32[]{:S(2)}, u32[]{:S(2)}) collective-permute-start(bf16[128,768]{1,0:T(8,128)(2,1)S(1)} %get-tuple-element.58), channel_id=1, source_target_pairs={{0,24},{4,28},{8,16},{12,20},{16,8},{20,12},{24,0},{28,4},{1,25},{... | collective-permute-start | bytes 589832 | tf_op jit(solution)/shard_map/ppermute | solution.py:515
  93.0 13.6 %collective-permute-start.25 = (bf16[64,1408]{1,0:T(8,128)(2,1)S(1)}, bf16[64,1408]{1,0:T(8,128)(2,1)S(1)}, u32[]{:S(2)}, u32[]{:S(2)}) collective-permute-start(bf16[64,1408]{1,0:T(8,128)(2,1)S(1)} %get-tuple-element.61), channel_id=1, source_target_pairs={{0,16},{4,20},{24,8},{28,12},{1,17},{5,21},{25,9},{29,13},{2,18},{... | collective-permute-start | bytes 540680 | tf_op jit(solution)/shard_map/ppermute | solution.py:515
  96.6 10.0 %collective-permute-start.26 = (bf16[64,1408]{1,0:T(8,128)(2,1)S(1)}, bf16[64,1408]{1,0:T(8,128)(2,1)S(1)}, u32[]{:S(2)}, u32[]{:S(2)}) collective-permute-start(bf16[64,1408]{1,0:T(8,128)(2,1)S(1)} %get-tuple-element.61), channel_id=1, source_target_pairs={{8,16},{12,20},{16,8},{20,12},{9,17},{13,21},{17,9},{21,13},{10,18... | collective-permute-start | bytes 540680 | tf_op jit(solution)/shard_map/ppermute | solution.py:515
  97.3 20.1 %collective-permute-start.27 = (bf16[64,1408]{1,0:T(8,128)(2,1)S(1)}, bf16[64,1408]{1,0:T(8,128)(2,1)S(1)}, u32[]{:S(2)}, u32[]{:S(2)}) collective-permute-start(bf16[64,1408]{1,0:T(8,128)(2,1)S(1)} %relay.1), channel_id=1, source_target_pairs={{0,8},{4,12},{24,16},{28,20},{8,24},{12,28},{16,0},{20,4},{1,9},{5... | collective-permute-start | bytes 540680 | tf_op jit(solution)/shard_map/ppermute | solution.py:515

commit v2 on v1

--- a/solution.py
+++ b/solution.py
@@ -37,28 +37,37 @@
     return [first * LANES, (units - first) * LANES]
 
 
-def cut(place, layer_rows, parts, sizes):
+def cut(place, layer_rows, out_grads, queries, parts, sizes):
     rows, width = layer_rows.shape
     own = width // parts
     chunks = len(sizes)
-
-    def kernel(place_ref, x_ref, *outs):
+    heads = out_grads.shape[1]
+
+    def kernel(place_ref, x_ref, o_ref, q_ref, *refs):
+        outs, (grad_ref, query_ref) = refs[: parts * chunks], refs[parts * chunks :]
         for k in range(parts):
             start = (place_ref[0] ^ k) * own
             for j in range(chunks):
                 span = pl.ds(pl.multiple_of(start + sum(sizes[:j]), LANES), sizes[j])
                 outs[k * chunks + j][...] = x_ref[:, span]
+        me, length = place_ref[0], place_ref[1]
+        valid = me * rows + lax.broadcasted_iota(jnp.int32, (rows, LANES), 0) < length
+        for start in range(0, heads, LANES):
+            block = o_ref[:, start : start + LANES]
+            grad_ref[:, start : start + LANES] = jnp.where(valid, block, jnp.zeros_like(block))
+        query_ref[...] = q_ref[...]
 
     out = pl.pallas_call(
         kernel,
-        out_shape=[jax.ShapeDtypeStruct((rows, size), BF16) for _ in range(parts) for size in sizes],
-        in_specs=[SMEM, VMEM],
-        out_specs=[VMEM] * (parts * chunks),
-        compiler_params=grant(8),
+        out_shape=[jax.ShapeDtypeStruct((rows, size), BF16) for _ in range(parts) for size in sizes]
+        + [jax.ShapeDtypeStruct(out_grads.shape, BF16)] * 2,
+        in_specs=[SMEM] + [VMEM] * 3,
+        out_specs=[VMEM] * (parts * chunks + 2),
+        compiler_params=grant(12),
         cost_estimate=estimate(0, HEAVY * 4 * rows * width),
         name="cut",
-    )(place, layer_rows)
-    return [[out[k * chunks + j] for j in range(chunks)] for k in range(parts)]
+    )(place, layer_rows, out_grads, queries)
+    return [[out[k * chunks + j] for j in range(chunks)] for k in range(parts)], *out[-2:]
 
 
 def anchor():
@@ -98,19 +107,14 @@
     )(layer_rows, value_weight)
 
 
-def masked(block, valid):
-    return jnp.where(valid, block, jnp.zeros_like(block))
-
-
 def lanes(start, size):
     return pl.ds(pl.multiple_of(start, size), size)
 
 
-def stack_heads(group, heads, source, target, keep):
+def stack_heads(group, heads, source, target):
     rows = source.shape[0]
     for h in range(heads):
-        block = source[:, lanes((group * heads + h) * HD, HD)]
-        target[h * rows : (h + 1) * rows, :] = keep(block)
+        target[h * rows : (h + 1) * rows, :] = source[:, lanes((group * heads + h) * HD, HD)]
 
 
 def weigh(place, queries, out_grads, keys):
@@ -126,8 +130,7 @@
     def kernel(place_ref, q_ref, o_ref, *rest):
         k_refs, p_ref = rest[:parts], rest[parts]
         v_refs, (q_buf, o_buf) = rest[parts + 1 : 2 * parts + 1], rest[2 * parts + 1 :]
-        me, length = place_ref[0], place_ref[1]
-        valid = me * rows + lax.broadcasted_iota(jnp.int32, (rows, HD), 0) < length
+        me = place_ref[0]
         row = lax.broadcasted_iota(jnp.int32, (rows, pair * rows), 0)
         lane = lax.broadcasted_iota(jnp.int32, (rows, pair * rows), 1)
         causal = row <= lax.rem(lane, rows)
@@ -135,8 +138,8 @@
         @pl.loop(0, groups)
         def _(group):
             cols = lanes(group * HD, HD)
-            stack_heads(group, heads, q_ref, q_buf, lambda block: block)
-            stack_heads(group, heads, o_ref, o_buf, lambda block: masked(block, valid))
+            stack_heads(group, heads, q_ref, q_buf)
+            stack_heads(group, heads, o_ref, o_buf)
             for h in range(0, heads, pair):
                 span = slice(h * rows, (h + pair) * rows)
                 q = q_buf[span, :]
@@ -179,7 +182,7 @@
     return out[0], out[1:]
 
 
-def key_side(place, weights, queries, out_grads, values):
+def key_side(weights, queries, out_grads, values):
     rows, width = queries.shape
     parts = len(values)
     kv_width = values[0].shape[1]
@@ -189,17 +192,15 @@
     scale = HD ** (-0.5)
     pair = 2
 
-    def kernel(place_ref, p_ref, q_ref, o_ref, *rest):
+    def kernel(p_ref, q_ref, o_ref, *rest):
         v_refs, k_refs = rest[:parts], rest[parts : 2 * parts]
         q_buf, o_buf, s_buf = rest[2 * parts :]
-        me, length = place_ref[0], place_ref[1]
-        valid = me * rows + lax.broadcasted_iota(jnp.int32, (rows, HD), 0) < length
 
         @pl.loop(0, groups)
         def _(group):
             cols = lanes(group * HD, HD)
-            stack_heads(group, heads, q_ref, q_buf, lambda block: block)
-            stack_heads(group, heads, o_ref, o_buf, lambda block: masked(block, valid))
+            stack_heads(group, heads, q_ref, q_buf)
+            stack_heads(group, heads, o_ref, o_buf)
             for h in range(0, heads, pair):
                 span = slice(h * rows, (h + pair) * rows)
                 o = o_buf[span, :]
@@ -220,14 +221,14 @@
     return pl.pallas_call(
         kernel,
         out_shape=[jax.ShapeDtypeStruct((rows, kv_width), kind) for kind in kinds],
-        in_specs=[SMEM] + [VMEM] * (3 + parts),
+        in_specs=[VMEM] * (3 + parts),
         out_specs=[VMEM] * parts,
         scratch_shapes=[pltpu.VMEM((heads * rows, HD), BF16)] * 2
         + [pltpu.VMEM((total, heads * rows), BF16)],
         compiler_params=grant(8 + 3 * parts),
         cost_estimate=estimate(4 * rows * total * width, 2 * (2 * rows * width + 2 * total * kv_width)),
         name="key_side",
-    )(place, weights, queries, out_grads, *values)
+    )(weights, queries, out_grads, *values)
 
 
 def settle(parts_list):
@@ -333,7 +334,7 @@
     rest = mine.shape[1] - LANES
 
     def kernel(place_ref, own_ref, *refs):
-        plain_refs, (mine_ref, *got_refs, out_ref) = refs[:planes], refs[planes:]
+        plain_refs, (mine_ref, *got_refs, out_ref, held, sems) = refs[:planes], refs[planes:]
         factors = [[own_ref[:1, :1], own_ref[8:9, :1]]]
         sums = mine_ref[:, :rest].astype(F32)
         if flag is None:
@@ -353,18 +354,25 @@
                 sums = sums + r[:, :rest].astype(F32)
             got = first_ref[:, :rest].astype(F32)
             sums = sums + jnp.where(inner, jnp.zeros_like(got), got)
-        out_ref[:, chunk:] = sums
+        held[:, chunk:] = sums
+        back = pltpu.make_async_copy(held.at[:, pl.ds(chunk, rest)], out_ref.at[:, pl.ds(chunk, rest)], sems.at[0])
+        back.start()
         total = 0.0
         for (even, odd), r in zip(factors, plain_refs):
             total = total + r[:width, :].astype(F32) * even + r[width:, :].astype(F32) * odd
-        out_ref[:, :chunk] = total
+        held[:, :chunk] = total
+        front = pltpu.make_async_copy(held.at[:, pl.ds(0, chunk)], out_ref.at[:, pl.ds(0, chunk)], sems.at[1])
+        front.start()
+        back.wait()
+        front.wait()
 
     args = [own, *plain, mine, first, *others]
     return pl.pallas_call(
         kernel,
         out_shape=jax.ShapeDtypeStruct((width, chunk + rest), F32),
         in_specs=[SMEM] + [VMEM] * len(args),
-        out_specs=VMEM,
+        out_specs=pl.BlockSpec(memory_space=pl.ANY),
+        scratch_shapes=[pltpu.VMEM((width, chunk + rest), F32), pltpu.SemaphoreType.DMA((2,))],
         compiler_params=grant(8),
         cost_estimate=estimate(12 * width * (chunk + rest), 20 * width * (chunk + rest)),
         name="finish",
@@ -505,12 +513,6 @@
     def over_context(x, k):
         return lax.ppermute(x, "context", [(i, i ^ k) for i in range(parts)])
 
-    def to_later(x, k):
-        return lax.ppermute(x, "context", [(i, i ^ k) for i in range(parts) ])
-
-    def to_earlier(x, k):
-        return lax.ppermute(x, "context", [(i, i ^ k) for i in range(parts) ])
-
     def over_planes(x, hops):
         return lax.ppermute(x, "dp", [(2 * a + c, 2 * b + c) for a, b in hops for c in range(2)])
 
@@ -521,13 +523,14 @@
         return lax.ppermute(x, "dp", [(i, i ^ 1) for i in range(docs)])
 
     zeros = anchor()
-    keys = [key_states[0]] + [to_later(key_states[0], k) for k in range(1, parts)]
-    pieces = cut(place, layer_input[0], parts, sizes)
+    keys = [over_context(key_states[0], k) for k in range(1, parts)]
+    pieces, grads, heads = cut(place, layer_input[0], out_grads[0], queries[0], parts, sizes)
     features = []
     for j in range(len(sizes)):
         features.append([pieces[0][j]] + [over_context(pieces[k][j], k) for k in range(1, parts)])
-    weights, value_parts = weigh(place, queries[0], out_grads[0], keys)
-    blocks = [value_parts[0]] + [to_earlier(value_parts[k], k) for k in range(1, parts)]
+    own_keys = key_states[0] * (lengths[0] >= 0).astype(BF16)
+    weights, value_parts = weigh(place, heads, grads, [own_keys] + keys)
+    blocks = [value_parts[0]] + [over_context(value_parts[k], k) for k in range(1, parts)]
     value_low = settle(blocks)
     value_grads = [value_low] + [over_context(value_low, k) for k in range(1, parts)]
 
@@ -543,9 +546,9 @@
 
 
     own_values = project(layer_input[0], value_weight)
-    values = [own_values] + [to_later(own_values, k) for k in range(1, parts)]
-    key_parts = key_side(place, weights, queries[0], out_grads[0], values)
-    key_blocks = [key_parts[0]] + [to_earlier(key_parts[k], k) for k in range(1, parts)]
+    values = [own_values] + [over_context(own_values, k) for k in range(1, parts)]
+    key_parts = key_side(weights, heads, grads, values)
+    key_blocks = [key_parts[0]] + [over_context(key_parts[k], k) for k in range(1, parts)]
     key_grads = add_up(place, 4, [], key_blocks, BF16)[None]
 
     if planes == 4:

time: 119 us -> 115 us (0.966)
  waiting for transfers between devices: 51.6 us -> 43.7 us
  starting transfers between devices: 41.1 us -> 44 us
    ppermute x12 -> x24, starting transfers between devices: 13.4 us -> 31.8 us  [over_context(): return lax.ppermute(x, 'context', [(i, i ^ k) for i in range(parts)])]
    ppermute x12 -> x0, waiting for transfers between devices: 16.6 us -> none  [the longest x6 10.9 us: to_earlier(): return lax.ppermute(x, 'context', [(i, i ^ k) for i in range(parts)])]
    ppermute x12 -> x0, starting transfers between devices: 15.5 us -> none  [the longest x6 8.13 us: to_later(): return lax.ppermute(x, 'context', [(i, i ^ k) for i in range(parts)])]
    ppermute x12 -> x24, waiting for transfers between devices: 16.4 us -> 25.2 us  [over_context(): return lax.ppermute(x, 'context', [(i, i ^ k) for i in range(parts)])]
    unnamed x17 -> x15, local copies, waits for them, and re-layouts: 3.37 us -> 4.06 us
  transfers between devices with their start and end apart: 34 -> 34, of which waited for: 14 -> 13; matrix products, arithmetic and copies ran while one was open for 1% -> 1% of each run, Pallas kernels for 10% -> 10%
where the time goes in v2:
time: 115 us; the launch traced here: 114 us
  starting transfers between devices  44 us (38%)
  waiting for transfers between devices  43.7 us (38%)
  Pallas kernels  20.4 us (18%)
  local copies, waits for them, and re-layouts  4.66 us (4%)
  between operations  1.51 us (1%)
    ppermute x24, starting transfers between devices, over_context(): return lax.ppermute(x, 'context', [(i, i ^ k) for i in range(parts)])  31.8 us
    ppermute x24, waiting for transfers between devices, over_context(): return lax.ppermute(x, 'context', [(i, i ^ k) for i in range(parts)])  25.2 us
    ppermute x7, waiting for transfers between devices, over_planes(): lax.ppermute(x, 'dp', [(2 * a + c, 2 * b + c) for a, b in hops for c in r...  17 us
    ppermute x7, starting transfers between devices, over_planes(): lax.ppermute(x, 'dp', [(2 * a + c, 2 * b + c) for a, b in hops for c in r...  11.5 us
    pallas_call x1, Pallas kernels, weigh(): pl.pallas_call(kernel, out_shape=[jax.ShapeDtypeStruct((groups, total, he...  5.78 us
    pallas_call x1, Pallas kernels, key_side(): pl.pallas_call(kernel, out_shape=[jax.ShapeDtypeStruct((rows, kv_width),...  4.57 us
    unnamed x15, local copies, waits for them, and re-layouts  4.06 us
    pallas_call x2, Pallas kernels, doc_grad(): pl.pallas_call(kernel, out_shape=[jax.ShapeDtypeStruct((half * width, chu...  2.55 us
  transfers between devices with their start and end apart: 34, of which 13 were waited for; matrix products, arithmetic and copies ran while one was open for 1% of the time, Pallas kernels for 10%

profile of v2, /device:TPU:0, one launch (start us, length us, event | category | flops | bytes accessed | tf_op | source)
XLA Modules:
  0.0 114.3 jit_solution(18310714058576749532)
XLA Ops:
  0.6 3.0 %collective-permute-start.6 = (bf16[128,512]{1,0:T(8,128)(2,1)}, bf16[128,512]{1,0:T(8,128)(2,1)S(1)}, u32[]{:S(2)}, u32[]{:S(2)}) collective-permute-start(bf16[128,512]{1,0:T(8,128)(2,1)} %bitcast.23), channel_id=1, source_target_pairs={{0,1},{1,0},{2,3},{3,2},{4,5},{5,4},{6,7},{7,6},{8,9},{9,8},{10,11... | collective-permute-start | bytes 393224 | tf_op jit(solution)/shard_map/ppermute | solution.py:514
  3.7 1.5 %collective-permute-start.7 = (bf16[128,512]{1,0:T(8,128)(2,1)}, bf16[128,512]{1,0:T(8,128)(2,1)S(1)}, u32[]{:S(2)}, u32[]{:S(2)}) collective-permute-start(bf16[128,512]{1,0:T(8,128)(2,1)} %bitcast.24), channel_id=1, source_target_pairs={{0,2},{1,3},{2,0},{3,1},{4,6},{5,7},{6,4},{7,5},{8,10},{9,11},{10,... | collective-permute-start | bytes 393224 | tf_op jit(solution)/shard_map/ppermute | solution.py:514
  5.2 0.0 collective-permute-start.8
  5.9 0.1 stack.36.place_ref
  6.0 1.6 %copy-done = bf16[1,128,8192]{2,1,0:T(8,128)(2,1)S(1)} copy-done((bf16[1,128,8192]{2,1,0:T(8,128)(2,1)S(1)}, bf16[1,128,8192]{2,1,0:T(8,128)(2,1)}, u32[]{:S(2)}) %copy-start) | copy-done | bytes 2097176
  7.6 1.2 %copy-done.2 = bf16[1,128,4096]{2,1,0:T(8,128)(2,1)S(1)} copy-done((bf16[1,128,4096]{2,1,0:T(8,128)(2,1)S(1)}, bf16[1,128,4096]{2,1,0:T(8,128)(2,1)}, u32[]{:S(2)}) %copy-start.2) | copy-done | bytes 1048600
  8.8 1.2 %copy-done.3 = bf16[1,128,4096]{2,1,0:T(8,128)(2,1)S(1)} copy-done((bf16[1,128,4096]{2,1,0:T(8,128)(2,1)S(1)}, bf16[1,128,4096]{2,1,0:T(8,128)(2,1)}, u32[]{:S(2)}) %copy-start.3) | copy-done | bytes 1048600
  10.0 1.0 cut.1
  11.1 0.6 collective-permute-done.7.rest_2_
  11.7 5.8 %weigh.1 = (bf16[4,512,1024]{2,1,0:T(8,128)(2,1)S(1)}, f32[128,512]{1,0:T(8,128)S(1)}, bf16[128,512]{1,0:T(8,128)(2,1)S(1)}, bf16[128,512]{1,0:T(8,128)(2,1)S(1)}, bf16[128,512]{1,0:T(8,128)(2,1)S(1)}) custom-call(s32[9]{0:T(128)S(1)} %stack.36.place_ref, bf16[128,4096]{1,0:T(8,128)(2,1)S(1)} %get-tuple-element.46.q_ref, ...), custom_call_target="tpu_custom_call" | custom-call | flops 10737418240 | bytes 3145728 | tf_op jit(solution)/shard_map/weigh/pallas_call | solution.py:167
  17.4 1.6 %collective-permute-start.10 = (bf16[128,512]{1,0:T(8,128)(2,1)S(1)}, bf16[128,512]{1,0:T(8,128)(2,1)S(1)}, u32[]{:S(2)}, u32[]{:S(2)}) collective-permute-start(bf16[128,512]{1,0:T(8,128)(2,1)S(1)} %get-tuple-element.50), channel_id=1, source_target_pairs={{0,2},{1,3},{2,0},{3,1},{4,6},{5,7},{6,4},{7,5},{8,10},{9,11},{10,... | collective-permute-start | bytes 393224 | tf_op jit(solution)/shard_map/ppermute | solution.py:514
  19.0 1.4 %collective-permute-start = (bf16[128,1024]{1,0:T(8,128)(2,1)S(1)}, bf16[128,1024]{1,0:T(8,128)(2,1)S(1)}, u32[]{:S(2)}, u32[]{:S(2)}) collective-permute-start(bf16[128,1024]{1,0:T(8,128)(2,1)S(1)} %get-tuple-element.39), channel_id=1, source_target_pairs={{0,1},{1,0},{2,3},{3,2},{4,5},{5,4},{6,7},{7,6},{8,9},{9,8},{10,11... | collective-permute-start | bytes 786440 | tf_op jit(solution)/shard_map/ppermute | solution.py:514
  20.4 0.5 collective-permute-start.1
  20.9 1.6 %collective-permute-start.11 = (bf16[128,512]{1,0:T(8,128)(2,1)S(1)}, bf16[128,512]{1,0:T(8,128)(2,1)S(1)}, u32[]{:S(2)}, u32[]{:S(2)}) collective-permute-start(bf16[128,512]{1,0:T(8,128)(2,1)S(1)} %get-tuple-element.51), channel_id=1, source_target_pairs={{0,3},{1,2},{2,1},{3,0},{4,7},{5,6},{6,5},{7,4},{8,11},{9,10},{10,... | collective-permute-start | bytes 393224 | tf_op jit(solution)/shard_map/ppermute | solution.py:514
  22.5 1.4 %collective-permute-start.9 = (bf16[128,512]{1,0:T(8,128)(2,1)S(1)}, bf16[128,512]{1,0:T(8,128)(2,1)S(1)}, u32[]{:S(2)}, u32[]{:S(2)}) collective-permute-start(bf16[128,512]{1,0:T(8,128)(2,1)S(1)} %get-tuple-element.49), channel_id=1, source_target_pairs={{0,1},{1,0},{2,3},{3,2},{4,5},{5,4},{6,7},{7,6},{8,9},{9,8},{10,11... | collective-permute-start | bytes 393224 | tf_op jit(solution)/shard_map/ppermute | solution.py:514
  23.9 0.1 collective-permute-done.10.refs_2_
  24.0 2.5 %collective-permute-start.2 = (bf16[128,1024]{1,0:T(8,128)(2,1)S(1)}, bf16[128,1024]{1,0:T(8,128)(2,1)S(1)}, u32[]{:S(2)}, u32[]{:S(2)}) collective-permute-start(bf16[128,1024]{1,0:T(8,128)(2,1)S(1)} %get-tuple-element.41), channel_id=1, source_target_pairs={{0,3},{1,2},{2,1},{3,0},{4,7},{5,6},{6,5},{7,4},{8,11},{9,10},{10,... | collective-permute-start | bytes 786440 | tf_op jit(solution)/shard_map/ppermute | solution.py:514
  26.4 4.6 %collective-permute-done.11.refs_3_ = bf16[128,512]{1,0:T(8,128)(2,1)S(1)} collective-permute-done((bf16[128,512]{1,0:T(8,128)(2,1)S(1)}, bf16[128,512]{1,0:T(8,128)(2,1)S(1)}, u32[]{:S(2)}, u32[]{:S(2)}) %collective-permute-start.11) | collective-permute-done | bytes 131104 | tf_op jit(solution)/shard_map/ppermute | solution.py:514
  31.1 2.8 %collective-permute-done.9.refs_1_ = bf16[128,512]{1,0:T(8,128)(2,1)S(1)} collective-permute-done((bf16[128,512]{1,0:T(8,128)(2,1)S(1)}, bf16[128,512]{1,0:T(8,128)(2,1)S(1)}, u32[]{:S(2)}, u32[]{:S(2)}) %collective-permute-start.9) | collective-permute-done | bytes 131104 | tf_op jit(solution)/shard_map/ppermute | solution.py:514
  33.9 0.1 settle.1.refs_4_.refs_8_
  34.0 1.4 %collective-permute-start.12 = (bf16[512,128]{1,0:T(8,128)(2,1)S(1)}, bf16[512,128]{1,0:T(8,128)(2,1)S(1)}, u32[]{:S(2)}, u32[]{:S(2)}) collective-permute-start(bf16[512,128]{1,0:T(8,128)(2,1)S(1)} %settle.1.refs_4_.refs_8_), channel_id=1, source_target_pairs={{0,1},{1,0},{2,3},{3,2},{4,5},{5,4},{6,7},{7,6},{8,9},{9,8},{10,11... | collective-permute-start | bytes 393224 | tf_op jit(solution)/shard_map/ppermute | solution.py:514
  35.4 0.7 collective-permute-start.3
  36.1 0.5 collective-permute-start.4
  36.6 2.3 %collective-permute-start.5 = (bf16[128,1024]{1,0:T(8,128)(2,1)S(1)}, bf16[128,1024]{1,0:T(8,128)(2,1)S(1)}, u32[]{:S(2)}, u32[]{:S(2)}) collective-permute-start(bf16[128,1024]{1,0:T(8,128)(2,1)S(1)} %get-tuple-element.45), channel_id=1, source_target_pairs={{0,3},{1,2},{2,1},{3,0},{4,7},{5,6},{6,5},{7,4},{8,11},{9,10},{10,... | collective-permute-start | bytes 786440 | tf_op jit(solution)/shard_map/ppermute | solution.py:514
  38.9 0.5 collective-permute-done.2.refs_3_
  39.4 1.5 %collective-permute-start.13 = (bf16[512,128]{1,0:T(8,128)(2,1)S(1)}, bf16[512,128]{1,0:T(8,128)(2,1)S(1)}, u32[]{:S(2)}, u32[]{:S(2)}) collective-permute-start(bf16[512,128]{1,0:T(8,128)(2,1)S(1)} %settle.1.refs_4_.refs_8_), channel_id=1, source_target_pairs={{0,2},{1,3},{2,0},{3,1},{4,6},{5,7},{6,4},{7,5},{8,10},{9,11},{10,... | collective-permute-start | bytes 393224 | tf_op jit(solution)/shard_map/ppermute | solution.py:514
  40.9 1.3 %collective-permute-done.12.refs_5_.refs_9_ = bf16[512,128]{1,0:T(8,128)(2,1)S(1)} collective-permute-done((bf16[512,128]{1,0:T(8,128)(2,1)S(1)}, bf16[512,128]{1,0:T(8,128)(2,1)S(1)}, u32[]{:S(2)}, u32[]{:S(2)}) %collective-permute-start.12) | collective-permute-done | bytes 131104 | tf_op jit(solution)/shard_map/ppermute | solution.py:514
  42.3 1.3 %collective-permute-start.14 = (bf16[512,128]{1,0:T(8,128)(2,1)S(1)}, bf16[512,128]{1,0:T(8,128)(2,1)S(1)}, u32[]{:S(2)}, u32[]{:S(2)}) collective-permute-start(bf16[512,128]{1,0:T(8,128)(2,1)S(1)} %settle.1.refs_4_.refs_8_), channel_id=1, source_target_pairs={{0,3},{1,2},{2,1},{3,0},{4,7},{5,6},{6,5},{7,4},{8,11},{9,10},{10,... | collective-permute-start | bytes 393224 | tf_op jit(solution)/shard_map/ppermute | solution.py:514
  43.6 3.9 %collective-permute-done.13.refs_6_.refs_10_ = bf16[512,128]{1,0:T(8,128)(2,1)S(1)} collective-permute-done((bf16[512,128]{1,0:T(8,128)(2,1)S(1)}, bf16[512,128]{1,0:T(8,128)(2,1)S(1)}, u32[]{:S(2)}, u32[]{:S(2)}) %collective-permute-start.13) | collective-permute-done | bytes 131104 | tf_op jit(solution)/shard_map/ppermute | solution.py:514
  47.5 6.3 %collective-permute-done.14.refs_7_.refs_11_ = bf16[512,128]{1,0:T(8,128)(2,1)S(1)} collective-permute-done((bf16[512,128]{1,0:T(8,128)(2,1)S(1)}, bf16[512,128]{1,0:T(8,128)(2,1)S(1)}, u32[]{:S(2)}, u32[]{:S(2)}) %collective-permute-start.14) | collective-permute-done | bytes 131104 | tf_op jit(solution)/shard_map/ppermute | solution.py:514
  53.8 1.1 doc_grad.2
  54.9 1.4 %doc_grad.3 = (f32[256,1280]{1,0:T(8,128)S(1)}, bf16[256,1280]{1,0:T(8,128)(2,1)S(1)}, f32[8,128]{1,0:T(8,128)S(1)}) custom-call(s32[9]{0:T(128)S(1)} %stack.36.place_ref, bf16[128,1024]{1,0:T(8,128)(2,1)S(1)} %get-tuple-element.38.refs_0_, bf16[128,1024]{1,0:T(8,128)(2,1)S(1)} %collective-permute-done.refs_1_, ...), custom_call_target="tpu_custom_call" | custom-call | flops 671088640 | bytes 3801088 | tf_op jit(solution)/shard_map/doc_grad/pallas_call | solution.py:293
  56.4 0.1 collective-permute-start.19
  56.4 0.5 collective-permute-start.15
  56.9 0.1 collective-permute-start.20
  57.0 1.5 %collective-permute-done.15 = f32[8,128]{1,0:T(8,128)S(1)} collective-permute-done((f32[8,128]{1,0:T(8,128)S(1)}, f32[8,128]{1,0:T(8,128)S(1)}, u32[]{:S(2)}, u32[]{:S(2)}) %collective-permute-start.15) | collective-permute-done | bytes 4128 | tf_op jit(solution)/shard_map/ppermute | solution.py:523
  58.5 1.6 %collective-permute-start.16 = (f32[16,128]{1,0:T(8,128)S(1)}, f32[16,128]{1,0:T(8,128)S(1)}, u32[]{:S(2)}, u32[]{:S(2)}) collective-permute-start(f32[16,128]{1,0:T(8,128)S(1)} %constant_dynamic-update-slice_fusion.refs_0_), channel_id=1, source_target_pairs={{0,1},{1,0},{2,3},{3,2},{4,5},{5,4},{6,7},{7,6},{8,9},{9,8},{10,11... | collective-permute-start | bytes 24584 | tf_op jit(solution)/shard_map/ppermute | solution.py:514
  60.1 1.5 %collective-permute-start.17 = (f32[16,128]{1,0:T(8,128)S(1)}, f32[16,128]{1,0:T(8,128)S(1)}, u32[]{:S(2)}, u32[]{:S(2)}) collective-permute-start(f32[16,128]{1,0:T(8,128)S(1)} %constant_dynamic-update-slice_fusion.refs_0_), channel_id=1, source_target_pairs={{0,2},{1,3},{2,0},{3,1},{4,6},{5,7},{6,4},{7,5},{8,10},{9,11},{10,... | collective-permute-start | bytes 24584 | tf_op jit(solution)/shard_map/ppermute | solution.py:514
  61.7 1.3 %project.1.rest_0_ = bf16[128,512]{1,0:T(8,128)(2,1)S(1)} custom-call(bf16[128,8192]{1,0:T(8,128)(2,1)S(1)} %bitcast.19, bf16[8192,512]{1,0:T(8,128)(2,1)S(1)} %bitcast.17), custom_call_target="tpu_custom_call" | custom-call | flops 1073741824 | bytes 10485760 | tf_op jit(solution)/shard_map/project/pallas_call | solution.py:99
  62.9 0.6 collective-permute-start.28
  63.6 0.4 collective-permute-start.29
  63.9 2.6 %collective-permute-start.30 = (bf16[128,512]{1,0:T(8,128)(2,1)S(1)}, bf16[128,512]{1,0:T(8,128)(2,1)S(1)}, u32[]{:S(2)}, u32[]{:S(2)}) collective-permute-start(bf16[128,512]{1,0:T(8,128)(2,1)S(1)} %project.1.rest_0_), channel_id=1, source_target_pairs={{0,3},{1,2},{2,1},{3,0},{4,7},{5,6},{6,5},{7,4},{8,11},{9,10},{10,... | collective-permute-start | bytes 393224 | tf_op jit(solution)/shard_map/ppermute | solution.py:514
  66.5 0.3 collective-permute-start.18
  66.9 0.6 pack.1
  67.5 3.6 %collective-permute-done.18.refs_3_ = f32[16,128]{1,0:T(8,128)S(1)} collective-permute-done((f32[16,128]{1,0:T(8,128)S(1)}, f32[16,128]{1,0:T(8,128)S(1)}, u32[]{:S(2)}, u32[]{:S(2)}) %collective-permute-start.18) | collective-permute-done | bytes 8224 | tf_op jit(solution)/shard_map/ppermute | solution.py:514
  71.1 1.6 %collective-permute-start.21 = (bf16[128,768]{1,0:T(8,128)(2,1)S(1)}, bf16[128,768]{1,0:T(8,128)(2,1)S(1)}, u32[]{:S(2)}, u32[]{:S(2)}) collective-permute-start(bf16[128,768]{1,0:T(8,128)(2,1)S(1)} %get-tuple-element.60), channel_id=1, source_target_pairs={{0,8},{4,12},{8,0},{12,4},{16,24},{20,28},{24,16},{28,20},{1,9},{5... | collective-permute-start | bytes 589832 | tf_op jit(solution)/shard_map/ppermute | solution.py:517
  72.6 1.0 combine.1
  73.6 0.5 collective-permute-start.24
  74.1 4.6 %key_side.1 = (f32[128,512]{1,0:T(8,128)S(1)}, bf16[128,512]{1,0:T(8,128)(2,1)S(1)}, bf16[128,512]{1,0:T(8,128)(2,1)S(1)}, bf16[128,512]{1,0:T(8,128)(2,1)S(1)}) custom-call(bf16[4,512,1024]{2,1,0:T(8,128)(2,1)S(1)} %get-tuple-element.68.p_ref, bf16[128,4096]{1,0:T(8,128)(2,1)S(1)} %get-tuple-element.46.q_ref, ...), custom_call_target="tpu_custom_call" | custom-call | flops 1073741824 | bytes 3145728 | tf_op jit(solution)/shard_map/key_side/pallas_call | solution.py:221
  78.7 0.6 collective-permute-start.31
  79.3 1.5 %collective-permute-start.32 = (bf16[128,512]{1,0:T(8,128)(2,1)S(1)}, bf16[128,512]{1,0:T(8,128)(2,1)S(1)}, u32[]{:S(2)}, u32[]{:S(2)}) collective-permute-start(bf16[128,512]{1,0:T(8,128)(2,1)S(1)} %get-tuple-element.71), channel_id=1, source_target_pairs={{0,2},{1,3},{2,0},{3,1},{4,6},{5,7},{6,4},{7,5},{8,10},{9,11},{10,... | collective-permute-start | bytes 393224 | tf_op jit(solution)/shard_map/ppermute | solution.py:514
  80.8 1.5 %collective-permute-start.33 = (bf16[128,512]{1,0:T(8,128)(2,1)S(1)}, bf16[128,512]{1,0:T(8,128)(2,1)S(1)}, u32[]{:S(2)}, u32[]{:S(2)}) collective-permute-start(bf16[128,512]{1,0:T(8,128)(2,1)S(1)} %get-tuple-element.72), channel_id=1, source_target_pairs={{0,3},{1,2},{2,1},{3,0},{4,7},{5,6},{6,5},{7,4},{8,11},{9,10},{10,... | collective-permute-start | bytes 393224 | tf_op jit(solution)/shard_map/ppermute | solution.py:514
  82.3 1.5 %collective-permute-done.31.refs_1_ = bf16[128,512]{1,0:T(8,128)(2,1)S(1)} collective-permute-done((bf16[128,512]{1,0:T(8,128)(2,1)S(1)}, bf16[128,512]{1,0:T(8,128)(2,1)S(1)}, u32[]{:S(2)}, u32[]{:S(2)}) %collective-permute-start.31) | collective-permute-done | bytes 131104 | tf_op jit(solution)/shard_map/ppermute | solution.py:514
  83.7 2.6 %collective-permute-start.22 = (bf16[128,768]{1,0:T(8,128)(2,1)S(1)}, bf16[128,768]{1,0:T(8,128)(2,1)S(1)}, u32[]{:S(2)}, u32[]{:S(2)}) collective-permute-start(bf16[128,768]{1,0:T(8,128)(2,1)S(1)} %get-tuple-element.61), channel_id=1, source_target_pairs={{0,16},{4,20},{8,24},{12,28},{16,0},{20,4},{24,8},{28,12},{1,17},{... | collective-permute-start | bytes 589832 | tf_op jit(solution)/shard_map/ppermute | solution.py:517
  86.3 1.3 %collective-permute-start.23 = (bf16[128,768]{1,0:T(8,128)(2,1)S(1)}, bf16[128,768]{1,0:T(8,128)(2,1)S(1)}, u32[]{:S(2)}, u32[]{:S(2)}) collective-permute-start(bf16[128,768]{1,0:T(8,128)(2,1)S(1)} %get-tuple-element.62), channel_id=1, source_target_pairs={{0,24},{4,28},{8,16},{12,20},{16,8},{20,12},{24,0},{28,4},{1,25},{... | collective-permute-start | bytes 589832 | tf_op jit(solution)/shard_map/ppermute | solution.py:517
  87.7 0.6 relay.1
  88.3 3.6 %collective-permute-start.25 = (bf16[64,1408]{1,0:T(8,128)(2,1)S(1)}, bf16[64,1408]{1,0:T(8,128)(2,1)S(1)}, u32[]{:S(2)}, u32[]{:S(2)}) collective-permute-start(bf16[64,1408]{1,0:T(8,128)(2,1)S(1)} %get-tuple-element.65), channel_id=1, source_target_pairs={{0,16},{4,20},{24,8},{28,12},{1,17},{5,21},{25,9},{29,13},{2,18},{... | collective-permute-start | bytes 540680 | tf_op jit(solution)/shard_map/ppermute | solution.py:517
  91.9 0.7 collective-permute-start.26
  92.6 1.2 %collective-permute-start.27 = (bf16[64,1408]{1,0:T(8,128)(2,1)S(1)}, bf16[64,1408]{1,0:T(8,128)(2,1)S(1)}, u32[]{:S(2)}, u32[]{:S(2)}) collective-permute-start(bf16[64,1408]{1,0:T(8,128)(2,1)S(1)} %relay.1), channel_id=1, source_target_pairs={{0,8},{4,12},{24,16},{28,20},{8,24},{12,28},{16,0},{20,4},{1,9},{5... | collective-permute-start | bytes 540680 | tf_op jit(solution)/shard_map/ppermute | solution.py:517
  93.8 1.3 %add_up.1 = bf16[128,512]{1,0:T(8,128)(2,1)} custom-call(s32[9]{0:T(128)S(1)} %stack.36.place_ref, f32[128,512]{1,0:T(8,128)S(1)} %get-tuple-element.69.refs_0_, bf16[128,512]{1,0:T(8,128)(2,1)S(1)} %collective-permute-done.31.refs_1_, bf16[128,512]{1,0:T(8,128)(2,1)S(1)} %collective-permute-done.32.refs_2_, bf16[128,512]{1,0:T(8,128)(2,1)S(1)} %collective-permute-done.33.refs_3_), custom_call_target="tpu_custom_call" | custom-call | flops 524288 | bytes 917504 | tf_op jit(solution)/shard_map/add_up/pallas_call | solution.py:480
  95.1 0.5 slice.3
  95.6 6.1 %collective-permute-done.22.refs_2_ = bf16[128,768]{1,0:T(8,128)(2,1)S(1)} collective-permute-done((bf16[128,768]{1,0:T(8,128)(2,1)S(1)}, bf16[128,768]{1,0:T(8,128)(2,1)S(1)}, u32[]{:S(2)}, u32[]{:S(2)}) %collective-permute-start.22) | collective-permute-done | bytes 196640 | tf_op jit(solution)/shard_map/ppermute | solution.py:517
  101.8 10.8 %collective-permute-done.27.refs_8_ = bf16[64,1408]{1,0:T(8,128)(2,1)S(1)} collective-permute-done((bf16[64,1408]{1,0:T(8,128)(2,1)S(1)}, bf16[64,1408]{1,0:T(8,128)(2,1)S(1)}, u32[]{:S(2)}, u32[]{:S(2)}) %collective-permute-start.27) | collective-permute-done | bytes 180256 | tf_op jit(solution)/shard_map/ppermute | solution.py:517
  112.6 1.7 %finish.1 = f32[64,2048]{1,0:T(8,128)} custom-call(s32[9]{0:T(128)S(1)} %stack.36.place_ref, f32[16,128]{1,0:T(8,128)S(1)} %get-tuple-element.56.own_ref, bf16[128,768]{1,0:T(8,128)(2,1)S(1)} %get-tuple-element.59.refs_0_, bf16[128,768]{1,0:T(8,128)(2,1)S(1)} %collective-permute-done.21.refs_1_, bf16[128,768]{1,0:T(8,128)(2,1)S(1)} %collective-permute-done.22.refs_2_, ...), custom_call_target="tpu_custom_call" | custom-call | flops 1572864 | bytes 2621440 | tf_op jit(solution)/shard_map/finish/pallas_call | solution.py:370
  (37 shorter events, 0.1 us)
Async XLA Ops:
  0.6 10.4 %copy-start.4 = (bf16[1,128,512]{2,1,0:T(8,128)(2,1)S(1)}, bf16[1,128,512]{2,1,0:T(8,128)(2,1)}, u32[]{:S(2)}) copy-start(bf16[1,128,512]{2,1,0:T(8,128)(2,1)} %param.9) | copy-start | bytes 393220
  0.6 10.4 %collective-permute-start.6 = (bf16[128,512]{1,0:T(8,128)(2,1)}, bf16[128,512]{1,0:T(8,128)(2,1)S(1)}, u32[]{:S(2)}, u32[]{:S(2)}) collective-permute-start(bf16[128,512]{1,0:T(8,128)(2,1)} %bitcast.23), channel_id=1, source_target_pairs={{0,1},{1,0},{2,3},{3,2},{4,5},{5,4},{6,7},{7,6},{8,9},{9,8},{10,11... | collective-permute-start | bytes 393224 | tf_op jit(solution)/shard_map/ppermute | solution.py:514
  3.7 8.0 %collective-permute-start.7 = (bf16[128,512]{1,0:T(8,128)(2,1)}, bf16[128,512]{1,0:T(8,128)(2,1)S(1)}, u32[]{:S(2)}, u32[]{:S(2)}) collective-permute-start(bf16[128,512]{1,0:T(8,128)(2,1)} %bitcast.24), channel_id=1, source_target_pairs={{0,2},{1,3},{2,0},{3,1},{4,6},{5,7},{6,4},{7,5},{8,10},{9,11},{10,... | collective-permute-start | bytes 393224 | tf_op jit(solution)/shard_map/ppermute | solution.py:514
  5.2 6.5 %collective-permute-start.8 = (bf16[128,512]{1,0:T(8,128)(2,1)}, bf16[128,512]{1,0:T(8,128)(2,1)S(1)}, u32[]{:S(2)}, u32[]{:S(2)}) collective-permute-start(bf16[128,512]{1,0:T(8,128)(2,1)} %bitcast.25), channel_id=1, source_target_pairs={{0,3},{1,2},{2,1},{3,0},{4,7},{5,6},{6,5},{7,4},{8,11},{9,10},{10,... | collective-permute-start | bytes 393224 | tf_op jit(solution)/shard_map/ppermute | solution.py:514
  6.0 1.6 %copy-start = (bf16[1,128,8192]{2,1,0:T(8,128)(2,1)S(1)}, bf16[1,128,8192]{2,1,0:T(8,128)(2,1)}, u32[]{:S(2)}) copy-start(bf16[1,128,8192]{2,1,0:T(8,128)(2,1)} %param.6) | copy-start | bytes 6291460
  7.6 1.2 %copy-start.2 = (bf16[1,128,4096]{2,1,0:T(8,128)(2,1)S(1)}, bf16[1,128,4096]{2,1,0:T(8,128)(2,1)}, u32[]{:S(2)}) copy-start(bf16[1,128,4096]{2,1,0:T(8,128)(2,1)} %param.10) | copy-start | bytes 3145732
  8.8 1.2 %copy-start.3 = (bf16[1,128,4096]{2,1,0:T(8,128)(2,1)S(1)}, bf16[1,128,4096]{2,1,0:T(8,128)(2,1)}, u32[]{:S(2)}) copy-start(bf16[1,128,4096]{2,1,0:T(8,128)(2,1)} %param.8) | copy-start | bytes 3145732
  17.4 6.5 %collective-permute-start.10 = (bf16[128,512]{1,0:T(8,128)(2,1)S(1)}, bf16[128,512]{1,0:T(8,128)(2,1)S(1)}, u32[]{:S(2)}, u32[]{:S(2)}) collective-permute-start(bf16[128,512]{1,0:T(8,128)(2,1)S(1)} %get-tuple-element.50), channel_id=1, source_target_pairs={{0,2},{1,3},{2,0},{3,1},{4,6},{5,7},{6,4},{7,5},{8,10},{9,11},{10,... | collective-permute-start | bytes 393224 | tf_op jit(solution)/shard_map/ppermute | solution.py:514
  19.0 17.1 %collective-permute-start = (bf16[128,1024]{1,0:T(8,128)(2,1)S(1)}, bf16[128,1024]{1,0:T(8,128)(2,1)S(1)}, u32[]{:S(2)}, u32[]{:S(2)}) collective-permute-start(bf16[128,1024]{1,0:T(8,128)(2,1)S(1)} %get-tuple-element.39), channel_id=1, source_target_pairs={{0,1},{1,0},{2,3},{3,2},{4,5},{5,4},{6,7},{7,6},{8,9},{9,8},{10,11... | collective-permute-start | bytes 786440 | tf_op jit(solution)/shard_map/ppermute | solution.py:514
  20.4 16.2 %collective-permute-start.1 = (bf16[128,1024]{1,0:T(8,128)(2,1)S(1)}, bf16[128,1024]{1,0:T(8,128)(2,1)S(1)}, u32[]{:S(2)}, u32[]{:S(2)}) collective-permute-start(bf16[128,1024]{1,0:T(8,128)(2,1)S(1)} %get-tuple-element.40), channel_id=1, source_target_pairs={{0,2},{1,3},{2,0},{3,1},{4,6},{5,7},{6,4},{7,5},{8,10},{9,11},{10,... | collective-permute-start | bytes 786440 | tf_op jit(solution)/shard_map/ppermute | solution.py:514
  20.9 10.2 %collective-permute-start.11 = (bf16[128,512]{1,0:T(8,128)(2,1)S(1)}, bf16[128,512]{1,0:T(8,128)(2,1)S(1)}, u32[]{:S(2)}, u32[]{:S(2)}) collective-permute-start(bf16[128,512]{1,0:T(8,128)(2,1)S(1)} %get-tuple-element.51), channel_id=1, source_target_pairs={{0,3},{1,2},{2,1},{3,0},{4,7},{5,6},{6,5},{7,4},{8,11},{9,10},{10,... | collective-permute-start | bytes 393224 | tf_op jit(solution)/shard_map/ppermute | solution.py:514
  22.5 11.4 %collective-permute-start.9 = (bf16[128,512]{1,0:T(8,128)(2,1)S(1)}, bf16[128,512]{1,0:T(8,128)(2,1)S(1)}, u32[]{:S(2)}, u32[]{:S(2)}) collective-permute-start(bf16[128,512]{1,0:T(8,128)(2,1)S(1)} %get-tuple-element.49), channel_id=1, source_target_pairs={{0,1},{1,0},{2,3},{3,2},{4,5},{5,4},{6,7},{7,6},{8,9},{9,8},{10,11... | collective-permute-start | bytes 393224 | tf_op jit(solution)/shard_map/ppermute | solution.py:514
  24.0 15.5 %collective-permute-start.2 = (bf16[128,1024]{1,0:T(8,128)(2,1)S(1)}, bf16[128,1024]{1,0:T(8,128)(2,1)S(1)}, u32[]{:S(2)}, u32[]{:S(2)}) collective-permute-start(bf16[128,1024]{1,0:T(8,128)(2,1)S(1)} %get-tuple-element.41), channel_id=1, source_target_pairs={{0,3},{1,2},{2,1},{3,0},{4,7},{5,6},{6,5},{7,4},{8,11},{9,10},{10,... | collective-permute-start | bytes 786440 | tf_op jit(solution)/shard_map/ppermute | solution.py:514
  34.0 8.3 %collective-permute-start.12 = (bf16[512,128]{1,0:T(8,128)(2,1)S(1)}, bf16[512,128]{1,0:T(8,128)(2,1)S(1)}, u32[]{:S(2)}, u32[]{:S(2)}) collective-permute-start(bf16[512,128]{1,0:T(8,128)(2,1)S(1)} %settle.1.refs_4_.refs_8_), channel_id=1, source_target_pairs={{0,1},{1,0},{2,3},{3,2},{4,5},{5,4},{6,7},{7,6},{8,9},{9,8},{10,11... | collective-permute-start | bytes 393224 | tf_op jit(solution)/shard_map/ppermute | solution.py:514
  35.4 19.5 %collective-permute-start.3 = (bf16[128,1024]{1,0:T(8,128)(2,1)S(1)}, bf16[128,1024]{1,0:T(8,128)(2,1)S(1)}, u32[]{:S(2)}, u32[]{:S(2)}) collective-permute-start(bf16[128,1024]{1,0:T(8,128)(2,1)S(1)} %get-tuple-element.43), channel_id=1, source_target_pairs={{0,1},{1,0},{2,3},{3,2},{4,5},{5,4},{6,7},{7,6},{8,9},{9,8},{10,11... | collective-permute-start | bytes 786440 | tf_op jit(solution)/shard_map/ppermute | solution.py:514
  36.1 18.8 %collective-permute-start.4 = (bf16[128,1024]{1,0:T(8,128)(2,1)S(1)}, bf16[128,1024]{1,0:T(8,128)(2,1)S(1)}, u32[]{:S(2)}, u32[]{:S(2)}) collective-permute-start(bf16[128,1024]{1,0:T(8,128)(2,1)S(1)} %get-tuple-element.44), channel_id=1, source_target_pairs={{0,2},{1,3},{2,0},{3,1},{4,6},{5,7},{6,4},{7,5},{8,10},{9,11},{10,... | collective-permute-start | bytes 786440 | tf_op jit(solution)/shard_map/ppermute | solution.py:514
  36.6 25.0 %slice-start = ((s8[8388608]{0:T(1024)(128)(4,1)}), s8[4194304]{0:T(1024)(128)(4,1)S(1)}, s32[]{:S(2)}) async-start(s8[8388608]{0:T(1024)(128)(4,1)} %bitcast.16), calls=%async_computation | async-start | bytes 8388608
  36.6 25.1 %slice-start.1 = ((s8[8388608]{0:T(1024)(128)(4,1)}), s8[4194304]{0:T(1024)(128)(4,1)S(1)}, s32[]{:S(2)}) async-start(s8[8388608]{0:T(1024)(128)(4,1)} %bitcast.16), calls=%async_computation.1 | async-start | bytes 8388608
  36.6 18.3 %collective-permute-start.5 = (bf16[128,1024]{1,0:T(8,128)(2,1)S(1)}, bf16[128,1024]{1,0:T(8,128)(2,1)S(1)}, u32[]{:S(2)}, u32[]{:S(2)}) collective-permute-start(bf16[128,1024]{1,0:T(8,128)(2,1)S(1)} %get-tuple-element.45), channel_id=1, source_target_pairs={{0,3},{1,2},{2,1},{3,0},{4,7},{5,6},{6,5},{7,4},{8,11},{9,10},{10,... | collective-permute-start | bytes 786440 | tf_op jit(solution)/shard_map/ppermute | solution.py:514
  39.4 8.1 %collective-permute-start.13 = (bf16[512,128]{1,0:T(8,128)(2,1)S(1)}, bf16[512,128]{1,0:T(8,128)(2,1)S(1)}, u32[]{:S(2)}, u32[]{:S(2)}) collective-permute-start(bf16[512,128]{1,0:T(8,128)(2,1)S(1)} %settle.1.refs_4_.refs_8_), channel_id=1, source_target_pairs={{0,2},{1,3},{2,0},{3,1},{4,6},{5,7},{6,4},{7,5},{8,10},{9,11},{10,... | collective-permute-start | bytes 393224 | tf_op jit(solution)/shard_map/ppermute | solution.py:514
  42.3 11.5 %collective-permute-start.14 = (bf16[512,128]{1,0:T(8,128)(2,1)S(1)}, bf16[512,128]{1,0:T(8,128)(2,1)S(1)}, u32[]{:S(2)}, u32[]{:S(2)}) collective-permute-start(bf16[512,128]{1,0:T(8,128)(2,1)S(1)} %settle.1.refs_4_.refs_8_), channel_id=1, source_target_pairs={{0,3},{1,2},{2,1},{3,0},{4,7},{5,6},{6,5},{7,4},{8,11},{9,10},{10,... | collective-permute-start | bytes 393224 | tf_op jit(solution)/shard_map/ppermute | solution.py:514
  43.6 18.1 %copy-start.1 = (bf16[1,128,8192]{2,1,0:T(8,128)(2,1)S(1)}, bf16[1,128,8192]{2,1,0:T(8,128)(2,1)}, u32[]{:S(2)}) copy-start(bf16[1,128,8192]{2,1,0:T(8,128)(2,1)} %param.6) | copy-start | bytes 6291460
  56.4 16.3 %collective-permute-start.19 = (bf16[256,1280]{1,0:T(8,128)(2,1)S(1)}, bf16[256,1280]{1,0:T(8,128)(2,1)S(1)}, u32[]{:S(2)}, u32[]{:S(2)}) collective-permute-start(bf16[256,1280]{1,0:T(8,128)(2,1)S(1)} %get-tuple-element.55), channel_id=1, source_target_pairs={{0,4},{4,0},{8,12},{12,8},{16,20},{20,16},{24,28},{28,24},{1,5},{5... | collective-permute-start | bytes 1966088 | tf_op jit(solution)/shard_map/ppermute | solution.py:523
  56.4 2.1 %collective-permute-start.15 = (f32[8,128]{1,0:T(8,128)S(1)}, f32[8,128]{1,0:T(8,128)S(1)}, u32[]{:S(2)}, u32[]{:S(2)}) collective-permute-start(f32[8,128]{1,0:T(8,128)S(1)} %get-tuple-element.53), channel_id=1, source_target_pairs={{0,4},{4,0},{8,12},{12,8},{16,20},{20,16},{24,28},{28,24},{1,5},{5... | collective-permute-start | bytes 12296 | tf_op jit(solution)/shard_map/ppermute | solution.py:523
  56.9 9.6 %collective-permute-start.20 = (bf16[256,768]{1,0:T(8,128)(2,1)S(1)}, bf16[256,768]{1,0:T(8,128)(2,1)S(1)}, u32[]{:S(2)}, u32[]{:S(2)}) collective-permute-start(bf16[256,768]{1,0:T(8,128)(2,1)S(1)} %get-tuple-element.58), channel_id=1, source_target_pairs={{0,4},{4,0},{8,12},{12,8},{16,20},{20,16},{24,28},{28,24},{1,5},{5... | collective-permute-start | bytes 1179656 | tf_op jit(solution)/shard_map/ppermute | solution.py:523
  58.5 5.0 %collective-permute-start.16 = (f32[16,128]{1,0:T(8,128)S(1)}, f32[16,128]{1,0:T(8,128)S(1)}, u32[]{:S(2)}, u32[]{:S(2)}) collective-permute-start(f32[16,128]{1,0:T(8,128)S(1)} %constant_dynamic-update-slice_fusion.refs_0_), channel_id=1, source_target_pairs={{0,1},{1,0},{2,3},{3,2},{4,5},{5,4},{6,7},{7,6},{8,9},{9,8},{10,11... | collective-permute-start | bytes 24584 | tf_op jit(solution)/shard_map/ppermute | solution.py:514
  60.1 3.8 %collective-permute-start.17 = (f32[16,128]{1,0:T(8,128)S(1)}, f32[16,128]{1,0:T(8,128)S(1)}, u32[]{:S(2)}, u32[]{:S(2)}) collective-permute-start(f32[16,128]{1,0:T(8,128)S(1)} %constant_dynamic-update-slice_fusion.refs_0_), channel_id=1, source_target_pairs={{0,2},{1,3},{2,0},{3,1},{4,6},{5,7},{6,4},{7,5},{8,10},{9,11},{10,... | collective-permute-start | bytes 24584 | tf_op jit(solution)/shard_map/ppermute | solution.py:514
  62.9 11.2 %collective-permute-start.28 = (bf16[128,512]{1,0:T(8,128)(2,1)S(1)}, bf16[128,512]{1,0:T(8,128)(2,1)S(1)}, u32[]{:S(2)}, u32[]{:S(2)}) collective-permute-start(bf16[128,512]{1,0:T(8,128)(2,1)S(1)} %project.1.rest_0_), channel_id=1, source_target_pairs={{0,1},{1,0},{2,3},{3,2},{4,5},{5,4},{6,7},{7,6},{8,9},{9,8},{10,11... | collective-permute-start | bytes 393224 | tf_op jit(solution)/shard_map/ppermute | solution.py:514
  63.6 10.6 %collective-permute-start.29 = (bf16[128,512]{1,0:T(8,128)(2,1)S(1)}, bf16[128,512]{1,0:T(8,128)(2,1)S(1)}, u32[]{:S(2)}, u32[]{:S(2)}) collective-permute-start(bf16[128,512]{1,0:T(8,128)(2,1)S(1)} %project.1.rest_0_), channel_id=1, source_target_pairs={{0,2},{1,3},{2,0},{3,1},{4,6},{5,7},{6,4},{7,5},{8,10},{9,11},{10,... | collective-permute-start | bytes 393224 | tf_op jit(solution)/shard_map/ppermute | solution.py:514
  63.9 10.2 %collective-permute-start.30 = (bf16[128,512]{1,0:T(8,128)(2,1)S(1)}, bf16[128,512]{1,0:T(8,128)(2,1)S(1)}, u32[]{:S(2)}, u32[]{:S(2)}) collective-permute-start(bf16[128,512]{1,0:T(8,128)(2,1)S(1)} %project.1.rest_0_), channel_id=1, source_target_pairs={{0,3},{1,2},{2,1},{3,0},{4,7},{5,6},{6,5},{7,4},{8,11},{9,10},{10,... | collective-permute-start | bytes 393224 | tf_op jit(solution)/shard_map/ppermute | solution.py:514
  66.5 4.6 %collective-permute-start.18 = (f32[16,128]{1,0:T(8,128)S(1)}, f32[16,128]{1,0:T(8,128)S(1)}, u32[]{:S(2)}, u32[]{:S(2)}) collective-permute-start(f32[16,128]{1,0:T(8,128)S(1)} %constant_dynamic-update-slice_fusion.refs_0_), channel_id=1, source_target_pairs={{0,3},{1,2},{2,1},{3,0},{4,7},{5,6},{6,5},{7,4},{8,11},{9,10},{10,... | collective-permute-start | bytes 24584 | tf_op jit(solution)/shard_map/ppermute | solution.py:514
  71.1 21.5 %collective-permute-start.21 = (bf16[128,768]{1,0:T(8,128)(2,1)S(1)}, bf16[128,768]{1,0:T(8,128)(2,1)S(1)}, u32[]{:S(2)}, u32[]{:S(2)}) collective-permute-start(bf16[128,768]{1,0:T(8,128)(2,1)S(1)} %get-tuple-element.60), channel_id=1, source_target_pairs={{0,8},{4,12},{8,0},{12,4},{16,24},{20,28},{24,16},{28,20},{1,9},{5... | collective-permute-start | bytes 589832 | tf_op jit(solution)/shard_map/ppermute | solution.py:517
  73.6 12.8 %collective-permute-start.24 = (bf16[64,1408]{1,0:T(8,128)(2,1)S(1)}, bf16[64,1408]{1,0:T(8,128)(2,1)S(1)}, u32[]{:S(2)}, u32[]{:S(2)}) collective-permute-start(bf16[64,1408]{1,0:T(8,128)(2,1)S(1)} %get-tuple-element.64), channel_id=1, source_target_pairs={{0,8},{4,12},{8,0},{12,4},{16,24},{20,28},{24,16},{28,20},{1,9},{5... | collective-permute-start | bytes 540680 | tf_op jit(solution)/shard_map/ppermute | solution.py:517
  78.7 5.0 %collective-permute-start.31 = (bf16[128,512]{1,0:T(8,128)(2,1)S(1)}, bf16[128,512]{1,0:T(8,128)(2,1)S(1)}, u32[]{:S(2)}, u32[]{:S(2)}) collective-permute-start(bf16[128,512]{1,0:T(8,128)(2,1)S(1)} %get-tuple-element.70), channel_id=1, source_target_pairs={{0,1},{1,0},{2,3},{3,2},{4,5},{5,4},{6,7},{7,6},{8,9},{9,8},{10,11... | collective-permute-start | bytes 393224 | tf_op jit(solution)/shard_map/ppermute | solution.py:514
  79.3 9.0 %collective-permute-start.32 = (bf16[128,512]{1,0:T(8,128)(2,1)S(1)}, bf16[128,512]{1,0:T(8,128)(2,1)S(1)}, u32[]{:S(2)}, u32[]{:S(2)}) collective-permute-start(bf16[128,512]{1,0:T(8,128)(2,1)S(1)} %get-tuple-element.71), channel_id=1, source_target_pairs={{0,2},{1,3},{2,0},{3,1},{4,6},{5,7},{6,4},{7,5},{8,10},{9,11},{10,... | collective-permute-start | bytes 393224 | tf_op jit(solution)/shard_map/ppermute | solution.py:514
  80.8 11.1 %collective-permute-start.33 = (bf16[128,512]{1,0:T(8,128)(2,1)S(1)}, bf16[128,512]{1,0:T(8,128)(2,1)S(1)}, u32[]{:S(2)}, u32[]{:S(2)}) collective-permute-start(bf16[128,512]{1,0:T(8,128)(2,1)S(1)} %get-tuple-element.72), channel_id=1, source_target_pairs={{0,3},{1,2},{2,1},{3,0},{4,7},{5,6},{6,5},{7,4},{8,11},{9,10},{10,... | collective-permute-start | bytes 393224 | tf_op jit(solution)/shard_map/ppermute | solution.py:514
  83.7 18.0 %collective-permute-start.22 = (bf16[128,768]{1,0:T(8,128)(2,1)S(1)}, bf16[128,768]{1,0:T(8,128)(2,1)S(1)}, u32[]{:S(2)}, u32[]{:S(2)}) collective-permute-start(bf16[128,768]{1,0:T(8,128)(2,1)S(1)} %get-tuple-element.61), channel_id=1, source_target_pairs={{0,16},{4,20},{8,24},{12,28},{16,0},{20,4},{24,8},{28,12},{1,17},{... | collective-permute-start | bytes 589832 | tf_op jit(solution)/shard_map/ppermute | solution.py:517
  86.3 15.4 %collective-permute-start.23 = (bf16[128,768]{1,0:T(8,128)(2,1)S(1)}, bf16[128,768]{1,0:T(8,128)(2,1)S(1)}, u32[]{:S(2)}, u32[]{:S(2)}) collective-permute-start(bf16[128,768]{1,0:T(8,128)(2,1)S(1)} %get-tuple-element.62), channel_id=1, source_target_pairs={{0,24},{4,28},{8,16},{12,20},{16,8},{20,12},{24,0},{28,4},{1,25},{... | collective-permute-start | bytes 589832 | tf_op jit(solution)/shard_map/ppermute | solution.py:517
  88.3 13.5 %collective-permute-start.25 = (bf16[64,1408]{1,0:T(8,128)(2,1)S(1)}, bf16[64,1408]{1,0:T(8,128)(2,1)S(1)}, u32[]{:S(2)}, u32[]{:S(2)}) collective-permute-start(bf16[64,1408]{1,0:T(8,128)(2,1)S(1)} %get-tuple-element.65), channel_id=1, source_target_pairs={{0,16},{4,20},{24,8},{28,12},{1,17},{5,21},{25,9},{29,13},{2,18},{... | collective-permute-start | bytes 540680 | tf_op jit(solution)/shard_map/ppermute | solution.py:517
  91.9 9.8 %collective-permute-start.26 = (bf16[64,1408]{1,0:T(8,128)(2,1)S(1)}, bf16[64,1408]{1,0:T(8,128)(2,1)S(1)}, u32[]{:S(2)}, u32[]{:S(2)}) collective-permute-start(bf16[64,1408]{1,0:T(8,128)(2,1)S(1)} %get-tuple-element.65), channel_id=1, source_target_pairs={{8,16},{12,20},{16,8},{20,12},{9,17},{13,21},{17,9},{21,13},{10,18... | collective-permute-start | bytes 540680 | tf_op jit(solution)/shard_map/ppermute | solution.py:517
  92.6 20.0 %collective-permute-start.27 = (bf16[64,1408]{1,0:T(8,128)(2,1)S(1)}, bf16[64,1408]{1,0:T(8,128)(2,1)S(1)}, u32[]{:S(2)}, u32[]{:S(2)}) collective-permute-start(bf16[64,1408]{1,0:T(8,128)(2,1)S(1)} %relay.1), channel_id=1, source_target_pairs={{0,8},{4,12},{24,16},{28,20},{8,24},{12,28},{16,0},{20,4},{1,9},{5... | collective-permute-start | bytes 540680 | tf_op jit(solution)/shard_map/ppermute | solution.py:517

commit v3 on v2

--- a/solution.py
+++ b/solution.py
@@ -333,38 +333,54 @@
     chunk = plain[0].shape[1]
     rest = mine.shape[1] - LANES
 
+    def pieces(size):
+        step = 3 * LANES
+        return [(at, min(step, size - at)) for at in range(0, size, step)]
+
+    count = len(pieces(rest)) + len(pieces(chunk))
+
     def kernel(place_ref, own_ref, *refs):
         plain_refs, (mine_ref, *got_refs, out_ref, held, sems) = refs[:planes], refs[planes:]
+        copies = []
+
+        def put(start, size, value):
+            held[:, start : start + size] = value
+            span = pl.ds(start, size)
+            copy = pltpu.make_async_copy(held.at[:, span], out_ref.at[:, span], sems.at[len(copies)])
+            copy.start()
+            copies.append(copy)
+
         factors = [[own_ref[:1, :1], own_ref[8:9, :1]]]
-        sums = mine_ref[:, :rest].astype(F32)
         if flag is None:
+            inner, added = None, got_refs
             for r in got_refs:
                 factors.append(gather_terms(r[:TERMS, rest:]))
-                sums = sums + r[:, :rest].astype(F32)
         else:
             first_ref, far_ref, near_ref, last_ref = got_refs
-            inner = place_ref[flag] == 1
+            inner, added = place_ref[flag] == 1, got_refs[1:]
             factors.append(gather_terms(first_ref[:TERMS, rest:]))
             last = last_ref[: 2 * TERMS, rest:]
             for ref, start in ((far_ref, 0), (near_ref, TERMS)):
                 direct = gather_terms(ref[:TERMS, rest:])
                 passed = gather_terms(last[start : start + TERMS])
                 factors.append([jnp.where(inner, d, p) for d, p in zip(direct, passed)])
-            for r in got_refs[1:]:
-                sums = sums + r[:, :rest].astype(F32)
-            got = first_ref[:, :rest].astype(F32)
-            sums = sums + jnp.where(inner, jnp.zeros_like(got), got)
-        held[:, chunk:] = sums
-        back = pltpu.make_async_copy(held.at[:, pl.ds(chunk, rest)], out_ref.at[:, pl.ds(chunk, rest)], sems.at[0])
-        back.start()
-        total = 0.0
-        for (even, odd), r in zip(factors, plain_refs):
-            total = total + r[:width, :].astype(F32) * even + r[width:, :].astype(F32) * odd
-        held[:, :chunk] = total
-        front = pltpu.make_async_copy(held.at[:, pl.ds(0, chunk)], out_ref.at[:, pl.ds(0, chunk)], sems.at[1])
-        front.start()
-        back.wait()
-        front.wait()
+        for at, size in pieces(rest):
+            span = slice(at, at + size)
+            sums = mine_ref[:, span].astype(F32)
+            for r in added:
+                sums = sums + r[:, span].astype(F32)
+            if flag is not None:
+                got = got_refs[0][:, span].astype(F32)
+                sums = sums + jnp.where(inner, jnp.zeros_like(got), got)
+            put(chunk + at, size, sums)
+        for at, size in pieces(chunk):
+            span = slice(at, at + size)
+            total = 0.0
+            for (even, odd), r in zip(factors, plain_refs):
+                total = total + r[:width, span].astype(F32) * even + r[width:, span].astype(F32) * odd
+            put(at, size, total)
+        for copy in copies:
+            copy.wait()
 
     args = [own, *plain, mine, first, *others]
     return pl.pallas_call(
@@ -372,7 +388,7 @@
         out_shape=jax.ShapeDtypeStruct((width, chunk + rest), F32),
         in_specs=[SMEM] + [VMEM] * len(args),
         out_specs=pl.BlockSpec(memory_space=pl.ANY),
-        scratch_shapes=[pltpu.VMEM((width, chunk + rest), F32), pltpu.SemaphoreType.DMA((2,))],
+        scratch_shapes=[pltpu.VMEM((width, chunk + rest), F32), pltpu.SemaphoreType.DMA((count,))],
         compiler_params=grant(8),
         cost_estimate=estimate(12 * width * (chunk + rest), 20 * width * (chunk + rest)),
         name="finish",

time: 115 us -> 114 us (level)
  no operation moved by 1% of the time
where the time goes in v3:
time: 114 us
  starting transfers between devices  44 us (39%)
  waiting for transfers between devices  43.7 us (38%)
  Pallas kernels  20.2 us (18%)
  local copies, waits for them, and re-layouts  4.66 us (4%)
  between operations  1.51 us (1%)
    ppermute x24, starting transfers between devices, over_context(): return lax.ppermute(x, 'context', [(i, i ^ k) for i in range(parts)])  31.8 us
    ppermute x24, waiting for transfers between devices, over_context(): return lax.ppermute(x, 'context', [(i, i ^ k) for i in range(parts)])  25.2 us
    ppermute x7, waiting for transfers between devices, over_planes(): lax.ppermute(x, 'dp', [(2 * a + c, 2 * b + c) for a, b in hops for c in r...  17 us
    ppermute x7, starting transfers between devices, over_planes(): lax.ppermute(x, 'dp', [(2 * a + c, 2 * b + c) for a, b in hops for c in r...  11.5 us
    pallas_call x1, Pallas kernels, weigh(): pl.pallas_call(kernel, out_shape=[jax.ShapeDtypeStruct((groups, total, he...  5.78 us
    pallas_call x1, Pallas kernels, key_side(): pl.pallas_call(kernel, out_shape=[jax.ShapeDtypeStruct((rows, kv_width),...  4.57 us
    unnamed x15, local copies, waits for them, and re-layouts  4.06 us
    pallas_call x2, Pallas kernels, doc_grad(): pl.pallas_call(kernel, out_shape=[jax.ShapeDtypeStruct((half * width, chu...  2.55 us
  transfers between devices with their start and end apart: 34, of which 13 were waited for; matrix products, arithmetic and copies ran while one was open for 1% of the time, Pallas kernels for 10%

profile of v3, /device:TPU:0, one launch (start us, length us, event | category | flops | bytes accessed | tf_op | source)
XLA Modules:
  0.0 114.1 jit_solution(8392992213884236362)
XLA Ops:
  0.6 3.0 %collective-permute-start.6 = (bf16[128,512]{1,0:T(8,128)(2,1)}, bf16[128,512]{1,0:T(8,128)(2,1)S(1)}, u32[]{:S(2)}, u32[]{:S(2)}) collective-permute-start(bf16[128,512]{1,0:T(8,128)(2,1)} %bitcast.23), channel_id=1, source_target_pairs={{0,1},{1,0},{2,3},{3,2},{4,5},{5,4},{6,7},{7,6},{8,9},{9,8},{10,11... | collective-permute-start | bytes 393224 | tf_op jit(solution)/shard_map/ppermute | solution.py:530
  3.7 1.5 %collective-permute-start.7 = (bf16[128,512]{1,0:T(8,128)(2,1)}, bf16[128,512]{1,0:T(8,128)(2,1)S(1)}, u32[]{:S(2)}, u32[]{:S(2)}) collective-permute-start(bf16[128,512]{1,0:T(8,128)(2,1)} %bitcast.24), channel_id=1, source_target_pairs={{0,2},{1,3},{2,0},{3,1},{4,6},{5,7},{6,4},{7,5},{8,10},{9,11},{10,... | collective-permute-start | bytes 393224 | tf_op jit(solution)/shard_map/ppermute | solution.py:530
  5.2 0.0 collective-permute-start.8
  5.9 0.1 stack.36.place_ref
  6.0 1.6 %copy-done = bf16[1,128,8192]{2,1,0:T(8,128)(2,1)S(1)} copy-done((bf16[1,128,8192]{2,1,0:T(8,128)(2,1)S(1)}, bf16[1,128,8192]{2,1,0:T(8,128)(2,1)}, u32[]{:S(2)}) %copy-start) | copy-done | bytes 2097176
  7.6 1.2 %copy-done.2 = bf16[1,128,4096]{2,1,0:T(8,128)(2,1)S(1)} copy-done((bf16[1,128,4096]{2,1,0:T(8,128)(2,1)S(1)}, bf16[1,128,4096]{2,1,0:T(8,128)(2,1)}, u32[]{:S(2)}) %copy-start.2) | copy-done | bytes 1048600
  8.8 1.2 %copy-done.3 = bf16[1,128,4096]{2,1,0:T(8,128)(2,1)S(1)} copy-done((bf16[1,128,4096]{2,1,0:T(8,128)(2,1)S(1)}, bf16[1,128,4096]{2,1,0:T(8,128)(2,1)}, u32[]{:S(2)}) %copy-start.3) | copy-done | bytes 1048600
  10.0 1.0 cut.1
  11.1 0.6 collective-permute-done.7.rest_2_
  11.7 5.8 %weigh.1 = (bf16[4,512,1024]{2,1,0:T(8,128)(2,1)S(1)}, f32[128,512]{1,0:T(8,128)S(1)}, bf16[128,512]{1,0:T(8,128)(2,1)S(1)}, bf16[128,512]{1,0:T(8,128)(2,1)S(1)}, bf16[128,512]{1,0:T(8,128)(2,1)S(1)}) custom-call(s32[9]{0:T(128)S(1)} %stack.36.place_ref, bf16[128,4096]{1,0:T(8,128)(2,1)S(1)} %get-tuple-element.46.q_ref, ...), custom_call_target="tpu_custom_call" | custom-call | flops 10737418240 | bytes 3145728 | tf_op jit(solution)/shard_map/weigh/pallas_call | solution.py:167
  17.4 1.6 %collective-permute-start.10 = (bf16[128,512]{1,0:T(8,128)(2,1)S(1)}, bf16[128,512]{1,0:T(8,128)(2,1)S(1)}, u32[]{:S(2)}, u32[]{:S(2)}) collective-permute-start(bf16[128,512]{1,0:T(8,128)(2,1)S(1)} %get-tuple-element.50), channel_id=1, source_target_pairs={{0,2},{1,3},{2,0},{3,1},{4,6},{5,7},{6,4},{7,5},{8,10},{9,11},{10,... | collective-permute-start | bytes 393224 | tf_op jit(solution)/shard_map/ppermute | solution.py:530
  19.0 1.4 %collective-permute-start = (bf16[128,1024]{1,0:T(8,128)(2,1)S(1)}, bf16[128,1024]{1,0:T(8,128)(2,1)S(1)}, u32[]{:S(2)}, u32[]{:S(2)}) collective-permute-start(bf16[128,1024]{1,0:T(8,128)(2,1)S(1)} %get-tuple-element.39), channel_id=1, source_target_pairs={{0,1},{1,0},{2,3},{3,2},{4,5},{5,4},{6,7},{7,6},{8,9},{9,8},{10,11... | collective-permute-start | bytes 786440 | tf_op jit(solution)/shard_map/ppermute | solution.py:530
  20.4 0.5 collective-permute-start.1
  20.9 1.6 %collective-permute-start.11 = (bf16[128,512]{1,0:T(8,128)(2,1)S(1)}, bf16[128,512]{1,0:T(8,128)(2,1)S(1)}, u32[]{:S(2)}, u32[]{:S(2)}) collective-permute-start(bf16[128,512]{1,0:T(8,128)(2,1)S(1)} %get-tuple-element.51), channel_id=1, source_target_pairs={{0,3},{1,2},{2,1},{3,0},{4,7},{5,6},{6,5},{7,4},{8,11},{9,10},{10,... | collective-permute-start | bytes 393224 | tf_op jit(solution)/shard_map/ppermute | solution.py:530
  22.5 1.4 %collective-permute-start.9 = (bf16[128,512]{1,0:T(8,128)(2,1)S(1)}, bf16[128,512]{1,0:T(8,128)(2,1)S(1)}, u32[]{:S(2)}, u32[]{:S(2)}) collective-permute-start(bf16[128,512]{1,0:T(8,128)(2,1)S(1)} %get-tuple-element.49), channel_id=1, source_target_pairs={{0,1},{1,0},{2,3},{3,2},{4,5},{5,4},{6,7},{7,6},{8,9},{9,8},{10,11... | collective-permute-start | bytes 393224 | tf_op jit(solution)/shard_map/ppermute | solution.py:530
  23.9 0.1 collective-permute-done.10.refs_2_
  24.0 2.5 %collective-permute-start.2 = (bf16[128,1024]{1,0:T(8,128)(2,1)S(1)}, bf16[128,1024]{1,0:T(8,128)(2,1)S(1)}, u32[]{:S(2)}, u32[]{:S(2)}) collective-permute-start(bf16[128,1024]{1,0:T(8,128)(2,1)S(1)} %get-tuple-element.41), channel_id=1, source_target_pairs={{0,3},{1,2},{2,1},{3,0},{4,7},{5,6},{6,5},{7,4},{8,11},{9,10},{10,... | collective-permute-start | bytes 786440 | tf_op jit(solution)/shard_map/ppermute | solution.py:530
  26.4 4.6 %collective-permute-done.11.refs_3_ = bf16[128,512]{1,0:T(8,128)(2,1)S(1)} collective-permute-done((bf16[128,512]{1,0:T(8,128)(2,1)S(1)}, bf16[128,512]{1,0:T(8,128)(2,1)S(1)}, u32[]{:S(2)}, u32[]{:S(2)}) %collective-permute-start.11) | collective-permute-done | bytes 131104 | tf_op jit(solution)/shard_map/ppermute | solution.py:530
  31.1 2.8 %collective-permute-done.9.refs_1_ = bf16[128,512]{1,0:T(8,128)(2,1)S(1)} collective-permute-done((bf16[128,512]{1,0:T(8,128)(2,1)S(1)}, bf16[128,512]{1,0:T(8,128)(2,1)S(1)}, u32[]{:S(2)}, u32[]{:S(2)}) %collective-permute-start.9) | collective-permute-done | bytes 131104 | tf_op jit(solution)/shard_map/ppermute | solution.py:530
  33.9 0.1 settle.1.refs_4_.refs_8_
  34.0 1.4 %collective-permute-start.12 = (bf16[512,128]{1,0:T(8,128)(2,1)S(1)}, bf16[512,128]{1,0:T(8,128)(2,1)S(1)}, u32[]{:S(2)}, u32[]{:S(2)}) collective-permute-start(bf16[512,128]{1,0:T(8,128)(2,1)S(1)} %settle.1.refs_4_.refs_8_), channel_id=1, source_target_pairs={{0,1},{1,0},{2,3},{3,2},{4,5},{5,4},{6,7},{7,6},{8,9},{9,8},{10,11... | collective-permute-start | bytes 393224 | tf_op jit(solution)/shard_map/ppermute | solution.py:530
  35.4 0.7 collective-permute-start.3
  36.1 0.5 collective-permute-start.4
  36.6 2.3 %collective-permute-start.5 = (bf16[128,1024]{1,0:T(8,128)(2,1)S(1)}, bf16[128,1024]{1,0:T(8,128)(2,1)S(1)}, u32[]{:S(2)}, u32[]{:S(2)}) collective-permute-start(bf16[128,1024]{1,0:T(8,128)(2,1)S(1)} %get-tuple-element.45), channel_id=1, source_target_pairs={{0,3},{1,2},{2,1},{3,0},{4,7},{5,6},{6,5},{7,4},{8,11},{9,10},{10,... | collective-permute-start | bytes 786440 | tf_op jit(solution)/shard_map/ppermute | solution.py:530
  38.9 0.5 collective-permute-done.2.refs_3_
  39.4 1.5 %collective-permute-start.13 = (bf16[512,128]{1,0:T(8,128)(2,1)S(1)}, bf16[512,128]{1,0:T(8,128)(2,1)S(1)}, u32[]{:S(2)}, u32[]{:S(2)}) collective-permute-start(bf16[512,128]{1,0:T(8,128)(2,1)S(1)} %settle.1.refs_4_.refs_8_), channel_id=1, source_target_pairs={{0,2},{1,3},{2,0},{3,1},{4,6},{5,7},{6,4},{7,5},{8,10},{9,11},{10,... | collective-permute-start | bytes 393224 | tf_op jit(solution)/shard_map/ppermute | solution.py:530
  40.9 1.3 %collective-permute-done.12.refs_5_.refs_9_ = bf16[512,128]{1,0:T(8,128)(2,1)S(1)} collective-permute-done((bf16[512,128]{1,0:T(8,128)(2,1)S(1)}, bf16[512,128]{1,0:T(8,128)(2,1)S(1)}, u32[]{:S(2)}, u32[]{:S(2)}) %collective-permute-start.12) | collective-permute-done | bytes 131104 | tf_op jit(solution)/shard_map/ppermute | solution.py:530
  42.3 1.3 %collective-permute-start.14 = (bf16[512,128]{1,0:T(8,128)(2,1)S(1)}, bf16[512,128]{1,0:T(8,128)(2,1)S(1)}, u32[]{:S(2)}, u32[]{:S(2)}) collective-permute-start(bf16[512,128]{1,0:T(8,128)(2,1)S(1)} %settle.1.refs_4_.refs_8_), channel_id=1, source_target_pairs={{0,3},{1,2},{2,1},{3,0},{4,7},{5,6},{6,5},{7,4},{8,11},{9,10},{10,... | collective-permute-start | bytes 393224 | tf_op jit(solution)/shard_map/ppermute | solution.py:530
  43.6 3.9 %collective-permute-done.13.refs_6_.refs_10_ = bf16[512,128]{1,0:T(8,128)(2,1)S(1)} collective-permute-done((bf16[512,128]{1,0:T(8,128)(2,1)S(1)}, bf16[512,128]{1,0:T(8,128)(2,1)S(1)}, u32[]{:S(2)}, u32[]{:S(2)}) %collective-permute-start.13) | collective-permute-done | bytes 131104 | tf_op jit(solution)/shard_map/ppermute | solution.py:530
  47.5 6.3 %collective-permute-done.14.refs_7_.refs_11_ = bf16[512,128]{1,0:T(8,128)(2,1)S(1)} collective-permute-done((bf16[512,128]{1,0:T(8,128)(2,1)S(1)}, bf16[512,128]{1,0:T(8,128)(2,1)S(1)}, u32[]{:S(2)}, u32[]{:S(2)}) %collective-permute-start.14) | collective-permute-done | bytes 131104 | tf_op jit(solution)/shard_map/ppermute | solution.py:530
  53.8 1.1 doc_grad.2
  54.9 1.4 %doc_grad.3 = (f32[256,1280]{1,0:T(8,128)S(1)}, bf16[256,1280]{1,0:T(8,128)(2,1)S(1)}, f32[8,128]{1,0:T(8,128)S(1)}) custom-call(s32[9]{0:T(128)S(1)} %stack.36.place_ref, bf16[128,1024]{1,0:T(8,128)(2,1)S(1)} %get-tuple-element.38.refs_0_, bf16[128,1024]{1,0:T(8,128)(2,1)S(1)} %collective-permute-done.refs_1_, ...), custom_call_target="tpu_custom_call" | custom-call | flops 671088640 | bytes 3801088 | tf_op jit(solution)/shard_map/doc_grad/pallas_call | solution.py:293
  56.4 0.1 collective-permute-start.19
  56.4 0.5 collective-permute-start.15
  56.9 0.1 collective-permute-start.20
  57.0 1.5 %collective-permute-done.15 = f32[8,128]{1,0:T(8,128)S(1)} collective-permute-done((f32[8,128]{1,0:T(8,128)S(1)}, f32[8,128]{1,0:T(8,128)S(1)}, u32[]{:S(2)}, u32[]{:S(2)}) %collective-permute-start.15) | collective-permute-done | bytes 4128 | tf_op jit(solution)/shard_map/ppermute | solution.py:539
  58.5 1.6 %collective-permute-start.16 = (f32[16,128]{1,0:T(8,128)S(1)}, f32[16,128]{1,0:T(8,128)S(1)}, u32[]{:S(2)}, u32[]{:S(2)}) collective-permute-start(f32[16,128]{1,0:T(8,128)S(1)} %constant_dynamic-update-slice_fusion.refs_0_), channel_id=1, source_target_pairs={{0,1},{1,0},{2,3},{3,2},{4,5},{5,4},{6,7},{7,6},{8,9},{9,8},{10,11... | collective-permute-start | bytes 24584 | tf_op jit(solution)/shard_map/ppermute | solution.py:530
  60.1 1.5 %collective-permute-start.17 = (f32[16,128]{1,0:T(8,128)S(1)}, f32[16,128]{1,0:T(8,128)S(1)}, u32[]{:S(2)}, u32[]{:S(2)}) collective-permute-start(f32[16,128]{1,0:T(8,128)S(1)} %constant_dynamic-update-slice_fusion.refs_0_), channel_id=1, source_target_pairs={{0,2},{1,3},{2,0},{3,1},{4,6},{5,7},{6,4},{7,5},{8,10},{9,11},{10,... | collective-permute-start | bytes 24584 | tf_op jit(solution)/shard_map/ppermute | solution.py:530
  61.7 1.3 %project.1.rest_0_ = bf16[128,512]{1,0:T(8,128)(2,1)S(1)} custom-call(bf16[128,8192]{1,0:T(8,128)(2,1)S(1)} %bitcast.19, bf16[8192,512]{1,0:T(8,128)(2,1)S(1)} %bitcast.17), custom_call_target="tpu_custom_call" | custom-call | flops 1073741824 | bytes 10485760 | tf_op jit(solution)/shard_map/project/pallas_call | solution.py:99
  62.9 0.6 collective-permute-start.28
  63.6 0.4 collective-permute-start.29
  63.9 2.6 %collective-permute-start.30 = (bf16[128,512]{1,0:T(8,128)(2,1)S(1)}, bf16[128,512]{1,0:T(8,128)(2,1)S(1)}, u32[]{:S(2)}, u32[]{:S(2)}) collective-permute-start(bf16[128,512]{1,0:T(8,128)(2,1)S(1)} %project.1.rest_0_), channel_id=1, source_target_pairs={{0,3},{1,2},{2,1},{3,0},{4,7},{5,6},{6,5},{7,4},{8,11},{9,10},{10,... | collective-permute-start | bytes 393224 | tf_op jit(solution)/shard_map/ppermute | solution.py:530
  66.5 0.3 collective-permute-start.18
  66.9 0.6 pack.1
  67.5 3.6 %collective-permute-done.18.refs_3_ = f32[16,128]{1,0:T(8,128)S(1)} collective-permute-done((f32[16,128]{1,0:T(8,128)S(1)}, f32[16,128]{1,0:T(8,128)S(1)}, u32[]{:S(2)}, u32[]{:S(2)}) %collective-permute-start.18) | collective-permute-done | bytes 8224 | tf_op jit(solution)/shard_map/ppermute | solution.py:530
  71.1 1.6 %collective-permute-start.21 = (bf16[128,768]{1,0:T(8,128)(2,1)S(1)}, bf16[128,768]{1,0:T(8,128)(2,1)S(1)}, u32[]{:S(2)}, u32[]{:S(2)}) collective-permute-start(bf16[128,768]{1,0:T(8,128)(2,1)S(1)} %get-tuple-element.60), channel_id=1, source_target_pairs={{0,8},{4,12},{8,0},{12,4},{16,24},{20,28},{24,16},{28,20},{1,9},{5... | collective-permute-start | bytes 589832 | tf_op jit(solution)/shard_map/ppermute | solution.py:533
  72.6 1.0 combine.1
  73.6 0.5 collective-permute-start.24
  74.1 4.6 %key_side.1 = (f32[128,512]{1,0:T(8,128)S(1)}, bf16[128,512]{1,0:T(8,128)(2,1)S(1)}, bf16[128,512]{1,0:T(8,128)(2,1)S(1)}, bf16[128,512]{1,0:T(8,128)(2,1)S(1)}) custom-call(bf16[4,512,1024]{2,1,0:T(8,128)(2,1)S(1)} %get-tuple-element.68.p_ref, bf16[128,4096]{1,0:T(8,128)(2,1)S(1)} %get-tuple-element.46.q_ref, ...), custom_call_target="tpu_custom_call" | custom-call | flops 1073741824 | bytes 3145728 | tf_op jit(solution)/shard_map/key_side/pallas_call | solution.py:221
  78.7 0.6 collective-permute-start.31
  79.3 1.5 %collective-permute-start.32 = (bf16[128,512]{1,0:T(8,128)(2,1)S(1)}, bf16[128,512]{1,0:T(8,128)(2,1)S(1)}, u32[]{:S(2)}, u32[]{:S(2)}) collective-permute-start(bf16[128,512]{1,0:T(8,128)(2,1)S(1)} %get-tuple-element.71), channel_id=1, source_target_pairs={{0,2},{1,3},{2,0},{3,1},{4,6},{5,7},{6,4},{7,5},{8,10},{9,11},{10,... | collective-permute-start | bytes 393224 | tf_op jit(solution)/shard_map/ppermute | solution.py:530
  80.8 1.5 %collective-permute-start.33 = (bf16[128,512]{1,0:T(8,128)(2,1)S(1)}, bf16[128,512]{1,0:T(8,128)(2,1)S(1)}, u32[]{:S(2)}, u32[]{:S(2)}) collective-permute-start(bf16[128,512]{1,0:T(8,128)(2,1)S(1)} %get-tuple-element.72), channel_id=1, source_target_pairs={{0,3},{1,2},{2,1},{3,0},{4,7},{5,6},{6,5},{7,4},{8,11},{9,10},{10,... | collective-permute-start | bytes 393224 | tf_op jit(solution)/shard_map/ppermute | solution.py:530
  82.3 1.5 %collective-permute-done.31.refs_1_ = bf16[128,512]{1,0:T(8,128)(2,1)S(1)} collective-permute-done((bf16[128,512]{1,0:T(8,128)(2,1)S(1)}, bf16[128,512]{1,0:T(8,128)(2,1)S(1)}, u32[]{:S(2)}, u32[]{:S(2)}) %collective-permute-start.31) | collective-permute-done | bytes 131104 | tf_op jit(solution)/shard_map/ppermute | solution.py:530
  83.7 2.6 %collective-permute-start.22 = (bf16[128,768]{1,0:T(8,128)(2,1)S(1)}, bf16[128,768]{1,0:T(8,128)(2,1)S(1)}, u32[]{:S(2)}, u32[]{:S(2)}) collective-permute-start(bf16[128,768]{1,0:T(8,128)(2,1)S(1)} %get-tuple-element.61), channel_id=1, source_target_pairs={{0,16},{4,20},{8,24},{12,28},{16,0},{20,4},{24,8},{28,12},{1,17},{... | collective-permute-start | bytes 589832 | tf_op jit(solution)/shard_map/ppermute | solution.py:533
  86.3 1.3 %collective-permute-start.23 = (bf16[128,768]{1,0:T(8,128)(2,1)S(1)}, bf16[128,768]{1,0:T(8,128)(2,1)S(1)}, u32[]{:S(2)}, u32[]{:S(2)}) collective-permute-start(bf16[128,768]{1,0:T(8,128)(2,1)S(1)} %get-tuple-element.62), channel_id=1, source_target_pairs={{0,24},{4,28},{8,16},{12,20},{16,8},{20,12},{24,0},{28,4},{1,25},{... | collective-permute-start | bytes 589832 | tf_op jit(solution)/shard_map/ppermute | solution.py:533
  87.7 0.6 relay.1
  88.3 3.6 %collective-permute-start.25 = (bf16[64,1408]{1,0:T(8,128)(2,1)S(1)}, bf16[64,1408]{1,0:T(8,128)(2,1)S(1)}, u32[]{:S(2)}, u32[]{:S(2)}) collective-permute-start(bf16[64,1408]{1,0:T(8,128)(2,1)S(1)} %get-tuple-element.65), channel_id=1, source_target_pairs={{0,16},{4,20},{24,8},{28,12},{1,17},{5,21},{25,9},{29,13},{2,18},{... | collective-permute-start | bytes 540680 | tf_op jit(solution)/shard_map/ppermute | solution.py:533
  91.9 0.7 collective-permute-start.26
  92.6 1.2 %collective-permute-start.27 = (bf16[64,1408]{1,0:T(8,128)(2,1)S(1)}, bf16[64,1408]{1,0:T(8,128)(2,1)S(1)}, u32[]{:S(2)}, u32[]{:S(2)}) collective-permute-start(bf16[64,1408]{1,0:T(8,128)(2,1)S(1)} %relay.1), channel_id=1, source_target_pairs={{0,8},{4,12},{24,16},{28,20},{8,24},{12,28},{16,0},{20,4},{1,9},{5... | collective-permute-start | bytes 540680 | tf_op jit(solution)/shard_map/ppermute | solution.py:533
  93.8 1.3 %add_up.1 = bf16[128,512]{1,0:T(8,128)(2,1)} custom-call(s32[9]{0:T(128)S(1)} %stack.36.place_ref, f32[128,512]{1,0:T(8,128)S(1)} %get-tuple-element.69.refs_0_, bf16[128,512]{1,0:T(8,128)(2,1)S(1)} %collective-permute-done.31.refs_1_, bf16[128,512]{1,0:T(8,128)(2,1)S(1)} %collective-permute-done.32.refs_2_, bf16[128,512]{1,0:T(8,128)(2,1)S(1)} %collective-permute-done.33.refs_3_), custom_call_target="tpu_custom_call" | custom-call | flops 524288 | bytes 917504 | tf_op jit(solution)/shard_map/add_up/pallas_call | solution.py:496
  95.1 0.5 slice.3
  95.6 6.1 %collective-permute-done.22.refs_2_ = bf16[128,768]{1,0:T(8,128)(2,1)S(1)} collective-permute-done((bf16[128,768]{1,0:T(8,128)(2,1)S(1)}, bf16[128,768]{1,0:T(8,128)(2,1)S(1)}, u32[]{:S(2)}, u32[]{:S(2)}) %collective-permute-start.22) | collective-permute-done | bytes 196640 | tf_op jit(solution)/shard_map/ppermute | solution.py:533
  101.8 10.8 %collective-permute-done.27.refs_8_ = bf16[64,1408]{1,0:T(8,128)(2,1)S(1)} collective-permute-done((bf16[64,1408]{1,0:T(8,128)(2,1)S(1)}, bf16[64,1408]{1,0:T(8,128)(2,1)S(1)}, u32[]{:S(2)}, u32[]{:S(2)}) %collective-permute-start.27) | collective-permute-done | bytes 180256 | tf_op jit(solution)/shard_map/ppermute | solution.py:533
  112.6 1.5 %finish.1 = f32[64,2048]{1,0:T(8,128)} custom-call(s32[9]{0:T(128)S(1)} %stack.36.place_ref, f32[16,128]{1,0:T(8,128)S(1)} %get-tuple-element.56.own_ref, bf16[128,768]{1,0:T(8,128)(2,1)S(1)} %get-tuple-element.59.refs_0_, bf16[128,768]{1,0:T(8,128)(2,1)S(1)} %collective-permute-done.21.refs_1_, bf16[128,768]{1,0:T(8,128)(2,1)S(1)} %collective-permute-done.22.refs_2_, ...), custom_call_target="tpu_custom_call" | custom-call | flops 1572864 | bytes 2621440 | tf_op jit(solution)/shard_map/finish/pallas_call | solution.py:386
  (37 shorter events, 0.1 us)
Async XLA Ops:
  0.6 10.4 %copy-start.4 = (bf16[1,128,512]{2,1,0:T(8,128)(2,1)S(1)}, bf16[1,128,512]{2,1,0:T(8,128)(2,1)}, u32[]{:S(2)}) copy-start(bf16[1,128,512]{2,1,0:T(8,128)(2,1)} %param.9) | copy-start | bytes 393220
  0.6 10.4 %collective-permute-start.6 = (bf16[128,512]{1,0:T(8,128)(2,1)}, bf16[128,512]{1,0:T(8,128)(2,1)S(1)}, u32[]{:S(2)}, u32[]{:S(2)}) collective-permute-start(bf16[128,512]{1,0:T(8,128)(2,1)} %bitcast.23), channel_id=1, source_target_pairs={{0,1},{1,0},{2,3},{3,2},{4,5},{5,4},{6,7},{7,6},{8,9},{9,8},{10,11... | collective-permute-start | bytes 393224 | tf_op jit(solution)/shard_map/ppermute | solution.py:530
  3.7 8.0 %collective-permute-start.7 = (bf16[128,512]{1,0:T(8,128)(2,1)}, bf16[128,512]{1,0:T(8,128)(2,1)S(1)}, u32[]{:S(2)}, u32[]{:S(2)}) collective-permute-start(bf16[128,512]{1,0:T(8,128)(2,1)} %bitcast.24), channel_id=1, source_target_pairs={{0,2},{1,3},{2,0},{3,1},{4,6},{5,7},{6,4},{7,5},{8,10},{9,11},{10,... | collective-permute-start | bytes 393224 | tf_op jit(solution)/shard_map/ppermute | solution.py:530
  5.2 6.5 %collective-permute-start.8 = (bf16[128,512]{1,0:T(8,128)(2,1)}, bf16[128,512]{1,0:T(8,128)(2,1)S(1)}, u32[]{:S(2)}, u32[]{:S(2)}) collective-permute-start(bf16[128,512]{1,0:T(8,128)(2,1)} %bitcast.25), channel_id=1, source_target_pairs={{0,3},{1,2},{2,1},{3,0},{4,7},{5,6},{6,5},{7,4},{8,11},{9,10},{10,... | collective-permute-start | bytes 393224 | tf_op jit(solution)/shard_map/ppermute | solution.py:530
  6.0 1.6 %copy-start = (bf16[1,128,8192]{2,1,0:T(8,128)(2,1)S(1)}, bf16[1,128,8192]{2,1,0:T(8,128)(2,1)}, u32[]{:S(2)}) copy-start(bf16[1,128,8192]{2,1,0:T(8,128)(2,1)} %param.6) | copy-start | bytes 6291460
  7.6 1.2 %copy-start.2 = (bf16[1,128,4096]{2,1,0:T(8,128)(2,1)S(1)}, bf16[1,128,4096]{2,1,0:T(8,128)(2,1)}, u32[]{:S(2)}) copy-start(bf16[1,128,4096]{2,1,0:T(8,128)(2,1)} %param.10) | copy-start | bytes 3145732
  8.8 1.2 %copy-start.3 = (bf16[1,128,4096]{2,1,0:T(8,128)(2,1)S(1)}, bf16[1,128,4096]{2,1,0:T(8,128)(2,1)}, u32[]{:S(2)}) copy-start(bf16[1,128,4096]{2,1,0:T(8,128)(2,1)} %param.8) | copy-start | bytes 3145732
  17.4 6.5 %collective-permute-start.10 = (bf16[128,512]{1,0:T(8,128)(2,1)S(1)}, bf16[128,512]{1,0:T(8,128)(2,1)S(1)}, u32[]{:S(2)}, u32[]{:S(2)}) collective-permute-start(bf16[128,512]{1,0:T(8,128)(2,1)S(1)} %get-tuple-element.50), channel_id=1, source_target_pairs={{0,2},{1,3},{2,0},{3,1},{4,6},{5,7},{6,4},{7,5},{8,10},{9,11},{10,... | collective-permute-start | bytes 393224 | tf_op jit(solution)/shard_map/ppermute | solution.py:530
  19.0 17.1 %collective-permute-start = (bf16[128,1024]{1,0:T(8,128)(2,1)S(1)}, bf16[128,1024]{1,0:T(8,128)(2,1)S(1)}, u32[]{:S(2)}, u32[]{:S(2)}) collective-permute-start(bf16[128,1024]{1,0:T(8,128)(2,1)S(1)} %get-tuple-element.39), channel_id=1, source_target_pairs={{0,1},{1,0},{2,3},{3,2},{4,5},{5,4},{6,7},{7,6},{8,9},{9,8},{10,11... | collective-permute-start | bytes 786440 | tf_op jit(solution)/shard_map/ppermute | solution.py:530
  20.4 16.2 %collective-permute-start.1 = (bf16[128,1024]{1,0:T(8,128)(2,1)S(1)}, bf16[128,1024]{1,0:T(8,128)(2,1)S(1)}, u32[]{:S(2)}, u32[]{:S(2)}) collective-permute-start(bf16[128,1024]{1,0:T(8,128)(2,1)S(1)} %get-tuple-element.40), channel_id=1, source_target_pairs={{0,2},{1,3},{2,0},{3,1},{4,6},{5,7},{6,4},{7,5},{8,10},{9,11},{10,... | collective-permute-start | bytes 786440 | tf_op jit(solution)/shard_map/ppermute | solution.py:530
  20.9 10.2 %collective-permute-start.11 = (bf16[128,512]{1,0:T(8,128)(2,1)S(1)}, bf16[128,512]{1,0:T(8,128)(2,1)S(1)}, u32[]{:S(2)}, u32[]{:S(2)}) collective-permute-start(bf16[128,512]{1,0:T(8,128)(2,1)S(1)} %get-tuple-element.51), channel_id=1, source_target_pairs={{0,3},{1,2},{2,1},{3,0},{4,7},{5,6},{6,5},{7,4},{8,11},{9,10},{10,... | collective-permute-start | bytes 393224 | tf_op jit(solution)/shard_map/ppermute | solution.py:530
  22.5 11.4 %collective-permute-start.9 = (bf16[128,512]{1,0:T(8,128)(2,1)S(1)}, bf16[128,512]{1,0:T(8,128)(2,1)S(1)}, u32[]{:S(2)}, u32[]{:S(2)}) collective-permute-start(bf16[128,512]{1,0:T(8,128)(2,1)S(1)} %get-tuple-element.49), channel_id=1, source_target_pairs={{0,1},{1,0},{2,3},{3,2},{4,5},{5,4},{6,7},{7,6},{8,9},{9,8},{10,11... | collective-permute-start | bytes 393224 | tf_op jit(solution)/shard_map/ppermute | solution.py:530
  24.0 15.5 %collective-permute-start.2 = (bf16[128,1024]{1,0:T(8,128)(2,1)S(1)}, bf16[128,1024]{1,0:T(8,128)(2,1)S(1)}, u32[]{:S(2)}, u32[]{:S(2)}) collective-permute-start(bf16[128,1024]{1,0:T(8,128)(2,1)S(1)} %get-tuple-element.41), channel_id=1, source_target_pairs={{0,3},{1,2},{2,1},{3,0},{4,7},{5,6},{6,5},{7,4},{8,11},{9,10},{10,... | collective-permute-start | bytes 786440 | tf_op jit(solution)/shard_map/ppermute | solution.py:530
  34.0 8.3 %collective-permute-start.12 = (bf16[512,128]{1,0:T(8,128)(2,1)S(1)}, bf16[512,128]{1,0:T(8,128)(2,1)S(1)}, u32[]{:S(2)}, u32[]{:S(2)}) collective-permute-start(bf16[512,128]{1,0:T(8,128)(2,1)S(1)} %settle.1.refs_4_.refs_8_), channel_id=1, source_target_pairs={{0,1},{1,0},{2,3},{3,2},{4,5},{5,4},{6,7},{7,6},{8,9},{9,8},{10,11... | collective-permute-start | bytes 393224 | tf_op jit(solution)/shard_map/ppermute | solution.py:530
  35.4 19.5 %collective-permute-start.3 = (bf16[128,1024]{1,0:T(8,128)(2,1)S(1)}, bf16[128,1024]{1,0:T(8,128)(2,1)S(1)}, u32[]{:S(2)}, u32[]{:S(2)}) collective-permute-start(bf16[128,1024]{1,0:T(8,128)(2,1)S(1)} %get-tuple-element.43), channel_id=1, source_target_pairs={{0,1},{1,0},{2,3},{3,2},{4,5},{5,4},{6,7},{7,6},{8,9},{9,8},{10,11... | collective-permute-start | bytes 786440 | tf_op jit(solution)/shard_map/ppermute | solution.py:530
  36.1 18.8 %collective-permute-start.4 = (bf16[128,1024]{1,0:T(8,128)(2,1)S(1)}, bf16[128,1024]{1,0:T(8,128)(2,1)S(1)}, u32[]{:S(2)}, u32[]{:S(2)}) collective-permute-start(bf16[128,1024]{1,0:T(8,128)(2,1)S(1)} %get-tuple-element.44), channel_id=1, source_target_pairs={{0,2},{1,3},{2,0},{3,1},{4,6},{5,7},{6,4},{7,5},{8,10},{9,11},{10,... | collective-permute-start | bytes 786440 | tf_op jit(solution)/shard_map/ppermute | solution.py:530
  36.6 25.0 %slice-start = ((s8[8388608]{0:T(1024)(128)(4,1)}), s8[4194304]{0:T(1024)(128)(4,1)S(1)}, s32[]{:S(2)}) async-start(s8[8388608]{0:T(1024)(128)(4,1)} %bitcast.16), calls=%async_computation | async-start | bytes 8388608
  36.6 25.1 %slice-start.1 = ((s8[8388608]{0:T(1024)(128)(4,1)}), s8[4194304]{0:T(1024)(128)(4,1)S(1)}, s32[]{:S(2)}) async-start(s8[8388608]{0:T(1024)(128)(4,1)} %bitcast.16), calls=%async_computation.1 | async-start | bytes 8388608
  36.6 18.3 %collective-permute-start.5 = (bf16[128,1024]{1,0:T(8,128)(2,1)S(1)}, bf16[128,1024]{1,0:T(8,128)(2,1)S(1)}, u32[]{:S(2)}, u32[]{:S(2)}) collective-permute-start(bf16[128,1024]{1,0:T(8,128)(2,1)S(1)} %get-tuple-element.45), channel_id=1, source_target_pairs={{0,3},{1,2},{2,1},{3,0},{4,7},{5,6},{6,5},{7,4},{8,11},{9,10},{10,... | collective-permute-start | bytes 786440 | tf_op jit(solution)/shard_map/ppermute | solution.py:530
  39.4 8.1 %collective-permute-start.13 = (bf16[512,128]{1,0:T(8,128)(2,1)S(1)}, bf16[512,128]{1,0:T(8,128)(2,1)S(1)}, u32[]{:S(2)}, u32[]{:S(2)}) collective-permute-start(bf16[512,128]{1,0:T(8,128)(2,1)S(1)} %settle.1.refs_4_.refs_8_), channel_id=1, source_target_pairs={{0,2},{1,3},{2,0},{3,1},{4,6},{5,7},{6,4},{7,5},{8,10},{9,11},{10,... | collective-permute-start | bytes 393224 | tf_op jit(solution)/shard_map/ppermute | solution.py:530
  42.3 11.5 %collective-permute-start.14 = (bf16[512,128]{1,0:T(8,128)(2,1)S(1)}, bf16[512,128]{1,0:T(8,128)(2,1)S(1)}, u32[]{:S(2)}, u32[]{:S(2)}) collective-permute-start(bf16[512,128]{1,0:T(8,128)(2,1)S(1)} %settle.1.refs_4_.refs_8_), channel_id=1, source_target_pairs={{0,3},{1,2},{2,1},{3,0},{4,7},{5,6},{6,5},{7,4},{8,11},{9,10},{10,... | collective-permute-start | bytes 393224 | tf_op jit(solution)/shard_map/ppermute | solution.py:530
  43.6 18.1 %copy-start.1 = (bf16[1,128,8192]{2,1,0:T(8,128)(2,1)S(1)}, bf16[1,128,8192]{2,1,0:T(8,128)(2,1)}, u32[]{:S(2)}) copy-start(bf16[1,128,8192]{2,1,0:T(8,128)(2,1)} %param.6) | copy-start | bytes 6291460
  56.4 16.3 %collective-permute-start.19 = (bf16[256,1280]{1,0:T(8,128)(2,1)S(1)}, bf16[256,1280]{1,0:T(8,128)(2,1)S(1)}, u32[]{:S(2)}, u32[]{:S(2)}) collective-permute-start(bf16[256,1280]{1,0:T(8,128)(2,1)S(1)} %get-tuple-element.55), channel_id=1, source_target_pairs={{0,4},{4,0},{8,12},{12,8},{16,20},{20,16},{24,28},{28,24},{1,5},{5... | collective-permute-start | bytes 1966088 | tf_op jit(solution)/shard_map/ppermute | solution.py:539
  56.4 2.1 %collective-permute-start.15 = (f32[8,128]{1,0:T(8,128)S(1)}, f32[8,128]{1,0:T(8,128)S(1)}, u32[]{:S(2)}, u32[]{:S(2)}) collective-permute-start(f32[8,128]{1,0:T(8,128)S(1)} %get-tuple-element.53), channel_id=1, source_target_pairs={{0,4},{4,0},{8,12},{12,8},{16,20},{20,16},{24,28},{28,24},{1,5},{5... | collective-permute-start | bytes 12296 | tf_op jit(solution)/shard_map/ppermute | solution.py:539
  56.9 9.6 %collective-permute-start.20 = (bf16[256,768]{1,0:T(8,128)(2,1)S(1)}, bf16[256,768]{1,0:T(8,128)(2,1)S(1)}, u32[]{:S(2)}, u32[]{:S(2)}) collective-permute-start(bf16[256,768]{1,0:T(8,128)(2,1)S(1)} %get-tuple-element.58), channel_id=1, source_target_pairs={{0,4},{4,0},{8,12},{12,8},{16,20},{20,16},{24,28},{28,24},{1,5},{5... | collective-permute-start | bytes 1179656 | tf_op jit(solution)/shard_map/ppermute | solution.py:539
  58.5 5.0 %collective-permute-start.16 = (f32[16,128]{1,0:T(8,128)S(1)}, f32[16,128]{1,0:T(8,128)S(1)}, u32[]{:S(2)}, u32[]{:S(2)}) collective-permute-start(f32[16,128]{1,0:T(8,128)S(1)} %constant_dynamic-update-slice_fusion.refs_0_), channel_id=1, source_target_pairs={{0,1},{1,0},{2,3},{3,2},{4,5},{5,4},{6,7},{7,6},{8,9},{9,8},{10,11... | collective-permute-start | bytes 24584 | tf_op jit(solution)/shard_map/ppermute | solution.py:530
  60.1 3.8 %collective-permute-start.17 = (f32[16,128]{1,0:T(8,128)S(1)}, f32[16,128]{1,0:T(8,128)S(1)}, u32[]{:S(2)}, u32[]{:S(2)}) collective-permute-start(f32[16,128]{1,0:T(8,128)S(1)} %constant_dynamic-update-slice_fusion.refs_0_), channel_id=1, source_target_pairs={{0,2},{1,3},{2,0},{3,1},{4,6},{5,7},{6,4},{7,5},{8,10},{9,11},{10,... | collective-permute-start | bytes 24584 | tf_op jit(solution)/shard_map/ppermute | solution.py:530
  62.9 11.2 %collective-permute-start.28 = (bf16[128,512]{1,0:T(8,128)(2,1)S(1)}, bf16[128,512]{1,0:T(8,128)(2,1)S(1)}, u32[]{:S(2)}, u32[]{:S(2)}) collective-permute-start(bf16[128,512]{1,0:T(8,128)(2,1)S(1)} %project.1.rest_0_), channel_id=1, source_target_pairs={{0,1},{1,0},{2,3},{3,2},{4,5},{5,4},{6,7},{7,6},{8,9},{9,8},{10,11... | collective-permute-start | bytes 393224 | tf_op jit(solution)/shard_map/ppermute | solution.py:530
  63.6 10.6 %collective-permute-start.29 = (bf16[128,512]{1,0:T(8,128)(2,1)S(1)}, bf16[128,512]{1,0:T(8,128)(2,1)S(1)}, u32[]{:S(2)}, u32[]{:S(2)}) collective-permute-start(bf16[128,512]{1,0:T(8,128)(2,1)S(1)} %project.1.rest_0_), channel_id=1, source_target_pairs={{0,2},{1,3},{2,0},{3,1},{4,6},{5,7},{6,4},{7,5},{8,10},{9,11},{10,... | collective-permute-start | bytes 393224 | tf_op jit(solution)/shard_map/ppermute | solution.py:530
  63.9 10.2 %collective-permute-start.30 = (bf16[128,512]{1,0:T(8,128)(2,1)S(1)}, bf16[128,512]{1,0:T(8,128)(2,1)S(1)}, u32[]{:S(2)}, u32[]{:S(2)}) collective-permute-start(bf16[128,512]{1,0:T(8,128)(2,1)S(1)} %project.1.rest_0_), channel_id=1, source_target_pairs={{0,3},{1,2},{2,1},{3,0},{4,7},{5,6},{6,5},{7,4},{8,11},{9,10},{10,... | collective-permute-start | bytes 393224 | tf_op jit(solution)/shard_map/ppermute | solution.py:530
  66.5 4.6 %collective-permute-start.18 = (f32[16,128]{1,0:T(8,128)S(1)}, f32[16,128]{1,0:T(8,128)S(1)}, u32[]{:S(2)}, u32[]{:S(2)}) collective-permute-start(f32[16,128]{1,0:T(8,128)S(1)} %constant_dynamic-update-slice_fusion.refs_0_), channel_id=1, source_target_pairs={{0,3},{1,2},{2,1},{3,0},{4,7},{5,6},{6,5},{7,4},{8,11},{9,10},{10,... | collective-permute-start | bytes 24584 | tf_op jit(solution)/shard_map/ppermute | solution.py:530
  71.1 21.5 %collective-permute-start.21 = (bf16[128,768]{1,0:T(8,128)(2,1)S(1)}, bf16[128,768]{1,0:T(8,128)(2,1)S(1)}, u32[]{:S(2)}, u32[]{:S(2)}) collective-permute-start(bf16[128,768]{1,0:T(8,128)(2,1)S(1)} %get-tuple-element.60), channel_id=1, source_target_pairs={{0,8},{4,12},{8,0},{12,4},{16,24},{20,28},{24,16},{28,20},{1,9},{5... | collective-permute-start | bytes 589832 | tf_op jit(solution)/shard_map/ppermute | solution.py:533
  73.6 12.8 %collective-permute-start.24 = (bf16[64,1408]{1,0:T(8,128)(2,1)S(1)}, bf16[64,1408]{1,0:T(8,128)(2,1)S(1)}, u32[]{:S(2)}, u32[]{:S(2)}) collective-permute-start(bf16[64,1408]{1,0:T(8,128)(2,1)S(1)} %get-tuple-element.64), channel_id=1, source_target_pairs={{0,8},{4,12},{8,0},{12,4},{16,24},{20,28},{24,16},{28,20},{1,9},{5... | collective-permute-start | bytes 540680 | tf_op jit(solution)/shard_map/ppermute | solution.py:533
  78.7 5.0 %collective-permute-start.31 = (bf16[128,512]{1,0:T(8,128)(2,1)S(1)}, bf16[128,512]{1,0:T(8,128)(2,1)S(1)}, u32[]{:S(2)}, u32[]{:S(2)}) collective-permute-start(bf16[128,512]{1,0:T(8,128)(2,1)S(1)} %get-tuple-element.70), channel_id=1, source_target_pairs={{0,1},{1,0},{2,3},{3,2},{4,5},{5,4},{6,7},{7,6},{8,9},{9,8},{10,11... | collective-permute-start | bytes 393224 | tf_op jit(solution)/shard_map/ppermute | solution.py:530
  79.3 9.0 %collective-permute-start.32 = (bf16[128,512]{1,0:T(8,128)(2,1)S(1)}, bf16[128,512]{1,0:T(8,128)(2,1)S(1)}, u32[]{:S(2)}, u32[]{:S(2)}) collective-permute-start(bf16[128,512]{1,0:T(8,128)(2,1)S(1)} %get-tuple-element.71), channel_id=1, source_target_pairs={{0,2},{1,3},{2,0},{3,1},{4,6},{5,7},{6,4},{7,5},{8,10},{9,11},{10,... | collective-permute-start | bytes 393224 | tf_op jit(solution)/shard_map/ppermute | solution.py:530
  80.8 11.1 %collective-permute-start.33 = (bf16[128,512]{1,0:T(8,128)(2,1)S(1)}, bf16[128,512]{1,0:T(8,128)(2,1)S(1)}, u32[]{:S(2)}, u32[]{:S(2)}) collective-permute-start(bf16[128,512]{1,0:T(8,128)(2,1)S(1)} %get-tuple-element.72), channel_id=1, source_target_pairs={{0,3},{1,2},{2,1},{3,0},{4,7},{5,6},{6,5},{7,4},{8,11},{9,10},{10,... | collective-permute-start | bytes 393224 | tf_op jit(solution)/shard_map/ppermute | solution.py:530
  83.7 18.0 %collective-permute-start.22 = (bf16[128,768]{1,0:T(8,128)(2,1)S(1)}, bf16[128,768]{1,0:T(8,128)(2,1)S(1)}, u32[]{:S(2)}, u32[]{:S(2)}) collective-permute-start(bf16[128,768]{1,0:T(8,128)(2,1)S(1)} %get-tuple-element.61), channel_id=1, source_target_pairs={{0,16},{4,20},{8,24},{12,28},{16,0},{20,4},{24,8},{28,12},{1,17},{... | collective-permute-start | bytes 589832 | tf_op jit(solution)/shard_map/ppermute | solution.py:533
  86.3 15.4 %collective-permute-start.23 = (bf16[128,768]{1,0:T(8,128)(2,1)S(1)}, bf16[128,768]{1,0:T(8,128)(2,1)S(1)}, u32[]{:S(2)}, u32[]{:S(2)}) collective-permute-start(bf16[128,768]{1,0:T(8,128)(2,1)S(1)} %get-tuple-element.62), channel_id=1, source_target_pairs={{0,24},{4,28},{8,16},{12,20},{16,8},{20,12},{24,0},{28,4},{1,25},{... | collective-permute-start | bytes 589832 | tf_op jit(solution)/shard_map/ppermute | solution.py:533
  88.3 13.5 %collective-permute-start.25 = (bf16[64,1408]{1,0:T(8,128)(2,1)S(1)}, bf16[64,1408]{1,0:T(8,128)(2,1)S(1)}, u32[]{:S(2)}, u32[]{:S(2)}) collective-permute-start(bf16[64,1408]{1,0:T(8,128)(2,1)S(1)} %get-tuple-element.65), channel_id=1, source_target_pairs={{0,16},{4,20},{24,8},{28,12},{1,17},{5,21},{25,9},{29,13},{2,18},{... | collective-permute-start | bytes 540680 | tf_op jit(solution)/shard_map/ppermute | solution.py:533
  91.9 9.8 %collective-permute-start.26 = (bf16[64,1408]{1,0:T(8,128)(2,1)S(1)}, bf16[64,1408]{1,0:T(8,128)(2,1)S(1)}, u32[]{:S(2)}, u32[]{:S(2)}) collective-permute-start(bf16[64,1408]{1,0:T(8,128)(2,1)S(1)} %get-tuple-element.65), channel_id=1, source_target_pairs={{8,16},{12,20},{16,8},{20,12},{9,17},{13,21},{17,9},{21,13},{10,18... | collective-permute-start | bytes 540680 | tf_op jit(solution)/shard_map/ppermute | solution.py:533
  92.6 20.0 %collective-permute-start.27 = (bf16[64,1408]{1,0:T(8,128)(2,1)S(1)}, bf16[64,1408]{1,0:T(8,128)(2,1)S(1)}, u32[]{:S(2)}, u32[]{:S(2)}) collective-permute-start(bf16[64,1408]{1,0:T(8,128)(2,1)S(1)} %relay.1), channel_id=1, source_target_pairs={{0,8},{4,12},{24,16},{28,20},{8,24},{12,28},{16,0},{20,4},{1,9},{5... | collective-permute-start | bytes 540680 | tf_op jit(solution)/shard_map/ppermute | solution.py:533
